TPU v7x, 32 devices: a whole 2x2x4 slice. The times are simulated.
32 devices in a mesh: fsdp: 4 (over y, core), ctx: 2 (over x), tp: 4 (over z).
Axes of the slice: x: 2, y: 2, z: 4, core: 2. Of those that a mesh axis runs over, the one named last changes fastest.
Arguments:
- inputs: bfloat16 [32, 320, 1024], P('fsdp', 'ctx'), may hold values from -6 to 6
- cotangent: bfloat16 [32, 320, 1024], P('fsdp', 'ctx'), may hold values from -6 to 6
- visible: int32 [32, 320], P('fsdp'), may hold values from 0 to 1, as said below
- w_qkv: float32 [1024, 3, 1024], P('fsdp', None, 'tp'), may hold values from -0.1875 to 0.1875
- b_qv: float32 [2, 1024], P(None, 'tp'), may hold values from -3 to 3
- w_out: float32 [1024, 1024], P('tp', 'fsdp'), may hold values from -0.75 to 0.75
- b_out: float32 [1024], replicated, may hold values from -3 to 3
- w_up: float32 [1024, 4096], P('fsdp', 'tp'), may hold values from -0.1875 to 0.1875
- b_up: float32 [4096], P('tp'), may hold values from -3 to 3
- w_down: float32 [4096, 1024], P('tp', 'fsdp'), may hold values from -0.09375 to 0.09375
- b_down: float32 [1024], replicated, may hold values from -3 to 3
- gain_one: float32 [1024], replicated, may hold values from 0.1 to 1.9
- shift_one: float32 [1024], replicated, may hold values from -3 to 3
- gain_two: float32 [1024], replicated, may hold values from 0.1 to 1.9
- shift_two: float32 [1024], replicated, may hold values from -3 to 3
Outputs:
- output: float32 [32, 320, 1024], P('fsdp', 'ctx')
- grad_inputs: float32 [32, 320, 1024], P('fsdp', 'ctx')
- grad_w_qkv: float32 [1024, 3, 1024], P('fsdp', None, 'tp')
- grad_b_qv: float32 [2, 1024], P(None, 'tp')
- grad_w_out: float32 [1024, 1024], P('tp', 'fsdp')
- grad_b_out: float32 [1024], replicated
- grad_w_up: float32 [1024, 4096], P('fsdp', 'tp')
- grad_b_up: float32 [4096], P('tp')
- grad_w_down: float32 [4096, 1024], P('tp', 'fsdp')
- grad_b_down: float32 [1024], replicated
- grad_gain_one: float32 [1024], replicated
- grad_shift_one: float32 [1024], replicated
- grad_gain_two: float32 [1024], replicated
- grad_shift_two: float32 [1024], replicated
Inputs may be any that keep to these rules, and one draw needn't show every extreme that they name: `visible`: the first 64 tokens of every image are 1; of the 256 image tokens of each image between a tenth and two fifths are 0.
All inputs are finite; a program needn't handle non-finite values.
Results may differ from a plain program's by a relative error of at most 0.012.
Values may be sent and summed in bfloat16 or wider, within the bound.
No kernel may reach another device: no remote copies, remote signals or barrier semaphores. Data moves between devices by JAX's collectives and lax.ppermute only.
A program may use at most 192 MiB of HBM per device.

v0:
```python
import jax
import jax.numpy as jnp
from jax import lax
from jax.sharding import PartitionSpec as P

HEAD = 64


EPSILON = 1e-06


def layer_norm(values, gain, shift):
    center = values - jnp.mean(values, axis=-1, keepdims=True)
    spread = jnp.mean(center * center, axis=-1, keepdims=True)
    return center * lax.rsqrt(spread + EPSILON) * gain + shift


def gelu_exact(values):
    return jax.nn.gelu(values, approximate=False)


def head_total(partial_sum):
    return lax.psum(partial_sum, "tp")


def attend(queries, keys_all, values_all, key_keep, scale_factor):
    scores = (
        jnp.einsum("iqhe,ikhe->ihqk", queries, keys_all, preferred_element_type=jnp.float32)
        * scale_factor
    )
    scores = jnp.where(key_keep, scores, -1e30)
    row_max = jnp.max(scores, axis=-1, keepdims=True)
    exponent = jnp.exp(scores - row_max)
    row_total = jnp.sum(exponent, axis=-1, keepdims=True)
    log_total = row_max + jnp.log(row_total)
    probability = exponent / row_total
    mixed = jnp.einsum(
        "ihqk,ikhe->iqhe",
        probability.astype(jnp.bfloat16),
        values_all,
        preferred_element_type=jnp.float32,
    )
    return (mixed, log_total)


def attend_back(queries, keys_all, values_all, key_keep, log_total, grad_mixed, scale_factor):
    again = (
        jnp.einsum("iqhe,ikhe->ihqk", queries, keys_all, preferred_element_type=jnp.float32)
        * scale_factor
    )
    again = jnp.where(key_keep, again, -1e30)
    prob_again = jnp.exp(again - log_total)
    grad_probs = jnp.einsum(
        "iqhe,ikhe->ihqk", grad_mixed, values_all, preferred_element_type=jnp.float32
    )
    grad_values = jnp.einsum(
        "ihqk,iqhe->ikhe",
        prob_again.astype(jnp.bfloat16),
        grad_mixed,
        preferred_element_type=jnp.float32,
    )
    grad_scores = prob_again * (
        grad_probs - jnp.sum(grad_probs * prob_again, axis=-1, keepdims=True)
    )
    grad_scores_low = grad_scores.astype(jnp.bfloat16)
    grad_queries = (
        jnp.einsum("ihqk,ikhe->iqhe", grad_scores_low, keys_all, preferred_element_type=jnp.float32)
        * scale_factor
    )
    grad_keys = (
        jnp.einsum("ihqk,iqhe->ikhe", grad_scores_low, queries, preferred_element_type=jnp.float32)
        * scale_factor
    )
    return (grad_queries, grad_keys, grad_values)


def on_device(
    inputs,
    cotangent,
    visible,
    w_qkv,
    b_qv,
    w_out,
    b_out,
    w_up,
    b_up,
    w_down,
    b_down,
    gain_one,
    shift_one,
    gain_two,
    shift_two,
):
    images, row_count, model_width = inputs.shape
    seq_total = visible.shape[1]
    tokens = images * row_count
    scale_factor = HEAD ** (-0.5)
    first_row = lax.axis_index("ctx") * row_count
    row_keep = (
        lax.dynamic_slice_in_dim(visible, first_row, row_count, 1)
        .astype(jnp.float32)
        .reshape(tokens, 1)
    )
    key_keep = (visible > 0)[:, None, None, :]
    qkv_w, out_w, up_w, down_w = (
        lax.all_gather(w_qkv.astype(jnp.bfloat16), "fsdp", axis=0, tiled=True),
        lax.all_gather(w_out.astype(jnp.bfloat16), "fsdp", axis=1, tiled=True),
        lax.all_gather(w_up.astype(jnp.bfloat16), "fsdp", axis=0, tiled=True),
        lax.all_gather(w_down.astype(jnp.bfloat16), "fsdp", axis=1, tiled=True),
    )
    local_width = qkv_w.shape[2]
    local_heads = local_width // HEAD
    flat_in = inputs.astype(jnp.float32).reshape(tokens, model_width)
    normed, norm_one_back = jax.vjp(layer_norm, flat_in, gain_one, shift_one)
    normed_low = normed.astype(jnp.bfloat16)
    bias_all = jnp.stack([b_qv[0], jnp.zeros_like(b_qv[0]), b_qv[1]])
    projected = (
        jnp.einsum("td,dcf->tcf", normed_low, qkv_w, preferred_element_type=jnp.float32) + bias_all
    )
    projected_low = projected.astype(jnp.bfloat16)
    queries = projected_low[:, 0].reshape(images, row_count, local_heads, HEAD)
    keys_here = projected_low[:, 1].reshape(images, row_count, local_width)
    values_here = projected_low[:, 2].reshape(images, row_count, local_width)
    keys_all, values_all = (
        lax.all_gather(keys_here, "ctx", axis=1, tiled=True),
        lax.all_gather(values_here, "ctx", axis=1, tiled=True),
    )
    keys_all = keys_all.reshape(images, seq_total, local_heads, HEAD)
    values_all = values_all.reshape(images, seq_total, local_heads, HEAD)
    mixed_heads, log_total = attend(queries, keys_all, values_all, key_keep, scale_factor)
    mixed_low = mixed_heads.astype(jnp.bfloat16).reshape(tokens, local_width)
    attended = head_total(jnp.dot(mixed_low, out_w, preferred_element_type=jnp.float32)) + b_out
    residual = flat_in + attended
    normed_two, norm_two_back = jax.vjp(layer_norm, residual, gain_two, shift_two)
    normed_two_low = normed_two.astype(jnp.bfloat16)
    hidden = jnp.dot(normed_two_low, up_w, preferred_element_type=jnp.float32) + b_up
    active, gelu_back = jax.vjp(gelu_exact, hidden)
    active_low = active.astype(jnp.bfloat16)
    branch = head_total(jnp.dot(active_low, down_w, preferred_element_type=jnp.float32)) + b_down
    result = row_keep * (residual + branch)
    grad_out = cotangent.astype(jnp.float32).reshape(tokens, model_width) * row_keep
    grad_branch = grad_out.astype(jnp.bfloat16)
    down_grad = jnp.dot(active_low.T, grad_branch, preferred_element_type=jnp.float32)
    down_bias_grad = jnp.sum(grad_branch.astype(jnp.float32), axis=0)
    grad_active = jnp.dot(grad_branch, down_w.T, preferred_element_type=jnp.float32)
    (grad_hidden,) = gelu_back(grad_active)
    grad_hidden_low = grad_hidden.astype(jnp.bfloat16)
    up_bias_grad = jnp.sum(grad_hidden_low.astype(jnp.float32), axis=0)
    up_grad = jnp.dot(normed_two_low.T, grad_hidden_low, preferred_element_type=jnp.float32)
    grad_normed_two = head_total(
        jnp.dot(grad_hidden_low, up_w.T, preferred_element_type=jnp.float32)
    )
    grad_resid_norm, gain_two_grad, shift_two_grad = norm_two_back(grad_normed_two)
    grad_resid = grad_out + grad_resid_norm
    grad_attended = grad_resid.astype(jnp.bfloat16)
    out_bias_grad = jnp.sum(grad_attended.astype(jnp.float32), axis=0)
    out_grad = jnp.dot(mixed_low.T, grad_attended, preferred_element_type=jnp.float32)
    grad_mixed_low = jnp.dot(grad_attended, out_w.T, preferred_element_type=jnp.float32).astype(
        jnp.bfloat16
    )
    grad_mixed = grad_mixed_low.reshape(images, row_count, local_heads, HEAD)
    grad_queries, grad_keys, grad_values = attend_back(
        queries, keys_all, values_all, key_keep, log_total, grad_mixed, scale_factor
    )
    grad_keys_here, grad_values_here = (
        lax.psum_scatter(
            grad_keys.reshape(images, seq_total, local_width),
            "ctx",
            scatter_dimension=1,
            tiled=True,
        ),
        lax.psum_scatter(
            grad_values.reshape(images, seq_total, local_width),
            "ctx",
            scatter_dimension=1,
            tiled=True,
        ),
    )
    grad_projected = jnp.stack(
        [
            grad_queries.reshape(tokens, local_width),
            grad_keys_here.reshape(tokens, local_width),
            grad_values_here.reshape(tokens, local_width),
        ],
        axis=1,
    ).astype(jnp.bfloat16)
    qv_bias_grad = jnp.sum(grad_projected.astype(jnp.float32)[:, 0::2], axis=0)
    qkv_grad = jnp.einsum(
        "td,tcf->dcf", normed_low, grad_projected, preferred_element_type=jnp.float32
    )
    grad_normed = head_total(
        jnp.einsum("tcf,dcf->td", grad_projected, qkv_w, preferred_element_type=jnp.float32)
    )
    grad_input_norm, gain_one_grad, shift_one_grad = norm_one_back(grad_normed)
    grad_input = (grad_resid + grad_input_norm).reshape(images, row_count, model_width)
    spread = (
        lax.psum_scatter(qkv_grad, "fsdp", scatter_dimension=0, tiled=True),
        lax.psum_scatter(out_grad, "fsdp", scatter_dimension=1, tiled=True),
        lax.psum_scatter(up_grad, "fsdp", scatter_dimension=0, tiled=True),
        lax.psum_scatter(down_grad, "fsdp", scatter_dimension=1, tiled=True),
    )
    qkv_total, out_total, up_total, down_total = lax.psum(
        (spread[0], spread[1], spread[2], spread[3]), "ctx"
    )
    small = lax.psum(
        (
            qv_bias_grad,
            out_bias_grad,
            up_bias_grad,
            down_bias_grad,
            gain_one_grad,
            shift_one_grad,
            gain_two_grad,
            shift_two_grad,
        ),
        ("fsdp", "ctx"),
    )
    return (
        result.reshape(images, row_count, model_width),
        grad_input,
        qkv_total,
        small[0],
        out_total,
        small[1],
        up_total,
        small[2],
        down_total,
        small[3],
        small[4],
        small[5],
        small[6],
        small[7],
    )


def solution(mesh):
    placed = (
        P("fsdp", "ctx", None),
        P("fsdp", "ctx", None),
        P("fsdp", None),
        P("fsdp", None, "tp"),
        P(None, "tp"),
        P("tp", "fsdp"),
        P(),
        P("fsdp", "tp"),
        P("tp"),
        P("tp", "fsdp"),
        P(),
        P(),
        P(),
        P(),
        P(),
    )
    return jax.shard_map(
        on_device,
        mesh=mesh,
        in_specs=placed,
        out_specs=(
            P("fsdp", "ctx", None),
            P("fsdp", "ctx", None),
            P("fsdp", None, "tp"),
            P(None, "tp"),
            P("tp", "fsdp"),
            P(),
            P("fsdp", "tp"),
            P("tp"),
            P("tp", "fsdp"),
            P(),
            P(),
            P(),
            P(),
            P(),
        ),
        check_vma=False,
    )
```

profile of v0, /device:TPU:0, one launch (start us, length us, event | category | flops | bytes accessed | tf_op | source)
XLA Modules:
  0.0 1293.8 jit_solution(9456932758075033936)
XLA Ops:
  15.6 17.0 %all-gather.6.cloned.1.call-done = bf16[1024,3,256]{2,0,1:T(8,128)(2,1)} async-done(((bf16[256,3,256]{2,0,1:T(8,128)(2,1)}), bf16[1024,3,256]{2,0,1:T(8,128)(2,1)}) %all-gather.6.cloned.1.call-update) | async-done | bytes 1572880 | tf_op jit(solution)/shard_map/all_gather | solution.py:106
  38.3 7.6 all_gather.21
  51.2 11.4 all-gather.10.cloned.1.call-done
  74.6 14.4 %all-gather.8.cloned.1.call-done = bf16[8,320,256]{2,1,0:T(8,128)(2,1)} async-done(((bf16[8,160,256]{2,1,0:T(8,128)(2,1)}), bf16[8,320,256]{2,1,0:T(8,128)(2,1)}) %all-gather.8.cloned.1.call-update) | async-done | bytes 1310736 | tf_op jit(solution)/shard_map/all_gather | solution.py:126
  91.6 5.1 fusion.30
  109.5 4.5 fusion.19
  114.0 179.8 %all-reduce.8.cloned.1.call-done = f32[1280,1024]{1,0:T(8,128)} async-done(((f32[1280,1024]{1,0:T(8,128)}), f32[1280,1024]{1,0:T(8,128)}) %all-reduce.8.cloned.1.call-update) | async-done | bytes 5242896 | tf_op jit(solution)/shard_map/psum | solution.py:23
  300.1 17.3 %all-gather.12.cloned.1.call-done = bf16[1024,1024]{1,0:T(8,128)(2,1)} async-done(((bf16[256,1024]{1,0:T(8,128)(2,1)}), bf16[1024,1024]{1,0:T(8,128)(2,1)}) %all-gather.12.cloned.1.call-update) | async-done | bytes 2097168 | tf_op jit(solution)/shard_map/all_gather | solution.py:108
  317.4 8.5 fusion.39
  325.9 16.3 %all-gather.14.cloned.1.call-done = bf16[1024,1024]{1,0:T(8,128)(2,1)} async-done(((bf16[1024,256]{1,0:T(8,128)(2,1)}), bf16[1024,1024]{1,0:T(8,128)(2,1)}) %all-gather.14.cloned.1.call-update) | async-done | bytes 2097168 | tf_op jit(solution)/shard_map/all_gather | solution.py:109
  342.3 18.4 %convert_reduce_fusion.2 = (f32[1024]{0:T(1024)S(1)}, bf16[1280,1024]{1,0:T(8,128)(2,1)S(1)}, f32[1280,1024]{1,0:T(8,128)}) fusion(f32[1280,1024]{1,0:T(8,128)} %fusion.39, f32[1024]{0:T(1024)S(1)} %copy-done.29, bf16[1280,1024]{1,0:T(8,128)(2,1)} %fusion.19, bf16[1024,1024]{1,0:T(8,128)(2,1)} %all-gather.14.cloned.1.call-done), kind=kOutput, calls=%fused_computation.31 | convolution fusion | flops 2782657536 | bytes 17833984 | tf_op jit(solution)/shard_map/dot_general | solution.py:145
  362.1 4.7 fusion.49
  367.3 188.6 %all-reduce.10.cloned.1.call-done = f32[1280,1024]{1,0:T(8,128)} async-done(((f32[1280,1024]{1,0:T(8,128)}), f32[1280,1024]{1,0:T(8,128)}) %all-reduce.10.cloned.1.call-update) | async-done | bytes 5242896 | tf_op jit(solution)/shard_map/psum | solution.py:23
  555.9 5.2 multiply_reduce_fusion.1
  577.5 7.2 fusion.20
  588.4 7.3 multiply_reduce_fusion
  595.8 5.4 multiply_convert_fusion
  611.4 5.6 multiply_convert_fusion.2
  618.5 4.5 fusion.51
  623.1 8.6 fusion.38
  632.0 6.2 fusion.31
  646.2 18.7 %reduce-scatter.7.cloned.1.call-done = f32[8,160,256]{2,0,1:T(8,128)} async-done(((f32[8,320,256]{2,0,1:T(8,128)}), f32[8,160,256]{2,0,1:T(8,128)}) %reduce-scatter.7.cloned.1.call-update) | async-done | bytes 1310736 | tf_op jit(solution)/shard_map/reduce_scatter | solution.py:166
  667.3 5.8 fusion.26
  673.2 8.0 fusion.48
  681.2 4.6 convolution_bitcast_fusion
  692.8 47.2 %reduce-scatter.17.cloned.1.call-done = f32[1024,256]{1,0:T(8,128)} async-done(((f32[1024,1024]{1,0:T(8,128)}), f32[1024,256]{1,0:T(8,128)}) %reduce-scatter.17.cloned.1.call-update) | async-done | bytes 1048592 | tf_op jit(solution)/shard_map/reduce_scatter | solution.py:200
  740.0 46.9 %reduce-scatter.15.cloned.1.call-done = f32[256,1024]{1,0:T(8,128)} async-done(((f32[1024,1024]{1,0:T(8,128)}), f32[256,1024]{1,0:T(8,128)}) %reduce-scatter.15.cloned.1.call-update) | async-done | bytes 1048592 | tf_op jit(solution)/shard_map/reduce_scatter | solution.py:199
  787.0 40.7 %reduce-scatter.11.cloned.1.call-done = f32[256,3,256]{2,0,1:T(8,128)} async-done(((f32[1024,3,256]{2,0,1:T(8,128)}), f32[256,3,256]{2,0,1:T(8,128)}) %reduce-scatter.11.cloned.1.call-update) | async-done | bytes 786448 | tf_op jit(solution)/shard_map/reduce_scatter | solution.py:197
  827.7 362.2 %all-reduce.12.cloned.1.call-done = (f32[1280,1024]{1,0:T(8,128)}, f32[1280,1024]{1,0:T(8,128)}) async-done(((f32[1280,1024]{1,0:T(8,128)}, f32[1280,1024]{1,0:T(8,128)}), (f32[1280,1024]{1,0:T(8,128)}, f32[1280,1024]{1,0:T(8,128)})) %all-reduce.12.cloned.1.call-update) | async-done | bytes 10485776 | tf_op jit(solution)/shard_map/psum | solution.py:23
  1196.9 25.6 %all-reduce = (f32[2,256]{1,0:T(2,128)}, f32[1024]{0:T(1024)}, f32[1024]{0:T(1024)}, f32[1024]{0:T(1024)}, f32[1024]{0:T(1024)}, /*index=5*/f32[1024]{0:T(1024)}, f32[1024]{0:T(1024)}, f32[1024]{0:T(1024)}) all-reduce(f32[2,256]{1,0:T(2,128)S(1)} %convert_reduce_fusion.4, ...), channel_id=1, replica_groups=mesh['fsdp'=4,'ctx'=2,'tp'=4] {'fsdp','ctx'}, use_global_device_ids=true, to_apply=%region_20.21 | all-reduce | flops 7680 | bytes 61440 | tf_op jit(solution)/shard_map/psum | solution.py:205
  1222.5 13.8 %add_add_fusion.2 = (f32[1280,1024]{1,0:T(8,128)}, f32[1280,1024]{1,0:T(8,128)}) fusion(f32[1280,1024]{1,0:T(8,128)} %copy-done.4, bf16[8,160,1024]{2,1,0:T(8,128)(2,1)} %param.16, f32[1280]{0:T(1024)S(1)} %negate_multiply_fusion.1, f32[1280]{0:T(1024)S(1)} %negate_multiply_fusion.2, f32[1280]{0:T(1024)S(1)} %mul.190, f32[1280]{0:T(1024)S(1)} %multiply_multiply_fusion.5, ...), kind=kLoop, calls=%fused_computation.33 | loop fusion | flops 20971520 | bytes 36739072 | tf_op jit(solution)/shard_map/add | solution.py:195
  1236.3 42.5 %all-reduce.14.cloned.1.call-done = (f32[256,3,256]{2,0,1:T(8,128)}, f32[256,256]{1,0:T(8,128)}, f32[256,1024]{1,0:T(8,128)}, f32[1024,256]{1,0:T(8,128)}) async-done(((f32[256,3,256]{2,0,1:T(8,128)}, f32[256,256]{1,0:T(8,128)}, f32[256,1024]{1,0:T(8,128)}, f32[1024,256]{1,0:T(8,128)}), (f32[256,3,256]{2,0,1:T(8,128)}, f32[256,256]{1,0:T(8,128)}, f32[256,1024]{1,0:T(8,128)}, ...) | async-done | bytes 3145744 | tf_op jit(solution)/shard_map/psum | solution.py:202
  (166 shorter events, 119.3 us)
Async XLA Ops:
  7.2 25.4 %all-gather.6.cloned.1.call-start = ((), (), s32[]{:S(2)}) async-start(), calls=%async_computation.6 | async-start | bytes 1966080 | tf_op jit(solution)/shard_map/all_gather | solution.py:106
  9.4 53.3 %all-gather.10.cloned.1.call-start = ((), (), s32[]{:S(2)}) async-start(), calls=%async_computation.8 | async-start | bytes 1966080 | tf_op jit(solution)/shard_map/all_gather | solution.py:125
  11.7 20.9 %copy-start.17 = (f32[1280]{0:T(1024)}, f32[1280]{0:T(1024)S(1)}, u32[]{:S(2)}) copy-start(f32[1280]{0:T(1024)S(1)} %div.47) | copy-start | bytes 15364
  12.6 20.0 %copy-start.21 = (f32[1280]{0:T(1024)}, f32[1280]{0:T(1024)S(1)}, u32[]{:S(2)}) copy-start(f32[1280]{0:T(1024)S(1)} %add.140) | copy-start | bytes 15364
  15.6 22.7 %copy-start.16 = (f32[256,256]{1,0:T(8,128)S(1)}, f32[256,256]{1,0:T(8,128)}, u32[]{:S(2)}) copy-start(f32[256,256]{1,0:T(8,128)} %param.20) | copy-start | bytes 786436
  37.0 9.2 copy-start.25
  38.2 50.8 %all-gather.8.cloned.1.call-start = ((), (), s32[]{:S(2)}) async-start(), calls=%async_computation.7 | async-start | bytes 1966080 | tf_op jit(solution)/shard_map/all_gather | solution.py:126
  46.0 247.8 %all-reduce.8.cloned.1.call-start = ((), (), s32[]{:S(2)}) async-start(), calls=%async_computation.9 | async-start | bytes 10485760 | tf_op jit(solution)/shard_map/psum | solution.py:23
  104.7 189.1 %copy-start.28 = (f32[1024]{0:T(1024)S(1)}, f32[1024]{0:T(1024)}, u32[]{:S(2)}) copy-start(f32[1024]{0:T(1024)} %param.21) | copy-start | bytes 12292
  104.8 212.6 %all-gather.12.cloned.1.call-start = ((), (), s32[]{:S(2)}) async-start(), calls=%async_computation.10 | async-start | bytes 2621440 | tf_op jit(solution)/shard_map/all_gather | solution.py:108
  106.9 235.3 %all-gather.14.cloned.1.call-start = ((), (), s32[]{:S(2)}) async-start(), calls=%async_computation.11 | async-start | bytes 2621440 | tf_op jit(solution)/shard_map/all_gather | solution.py:109
  109.1 446.8 %all-reduce.10.cloned.1.call-start = ((), (), s32[]{:S(2)}) async-start(), calls=%async_computation.12 | async-start | bytes 10485760 | tf_op jit(solution)/shard_map/psum | solution.py:23
  297.1 20.3 %copy-start.26 = (f32[1024]{0:T(1024)S(1)}, f32[1024]{0:T(1024)}, u32[]{:S(2)}) copy-start(f32[1024]{0:T(1024)} %param.28) | copy-start | bytes 12292
  297.1 20.3 %copy-start.34 = (f32[1024]{0:T(1024)S(1)}, f32[1024]{0:T(1024)}, u32[]{:S(2)}) copy-start(f32[1024]{0:T(1024)} %param.29) | copy-start | bytes 12292
  300.1 42.2 %copy-start.29 = (f32[1024]{0:T(1024)S(1)}, f32[1024]{0:T(1024)}, u32[]{:S(2)}) copy-start(f32[1024]{0:T(1024)} %param.23) | copy-start | bytes 12292
  342.3 19.8 %copy-start.32 = (bf16[1024,1024]{1,0:T(8,128)(2,1)S(1)}, bf16[1024,1024]{1,0:T(8,128)(2,1)}, u32[]{:S(2)}) copy-start(bf16[1024,1024]{1,0:T(8,128)(2,1)} %all-gather.12.cloned.1.call-done) | copy-start | bytes 6291460
  366.8 277.9 %reduce-scatter.9.cloned.1.call-start = ((), (), s32[]{:S(2)}) async-start(), calls=%async_computation.14 | async-start | bytes 3932160 | tf_op jit(solution)/shard_map/reduce_scatter | solution.py:172
  588.2 76.7 %reduce-scatter.7.cloned.1.call-start = ((), (), s32[]{:S(2)}) async-start(), calls=%async_computation.13 | async-start | bytes 3932160 | tf_op jit(solution)/shard_map/reduce_scatter | solution.py:166
  607.7 85.1 %reduce-scatter.13.cloned.1.call-start = ((), (), s32[]{:S(2)}) async-start(), calls=%async_computation.16 | async-start | bytes 1310720 | tf_op jit(solution)/shard_map/reduce_scatter | solution.py:198
  611.3 128.7 %reduce-scatter.17.cloned.1.call-start = ((), (), s32[]{:S(2)}) async-start(), calls=%async_computation.18 | async-start | bytes 5242880 | tf_op jit(solution)/shard_map/reduce_scatter | solution.py:200
  623.1 163.9 %reduce-scatter.15.cloned.1.call-start = ((), (), s32[]{:S(2)}) async-start(), calls=%async_computation.17 | async-start | bytes 5242880 | tf_op jit(solution)/shard_map/reduce_scatter | solution.py:199
  631.8 195.9 %reduce-scatter.11.cloned.1.call-start = ((), (), s32[]{:S(2)}) async-start(), calls=%async_computation.15 | async-start | bytes 3932160 | tf_op jit(solution)/shard_map/reduce_scatter | solution.py:197
  673.1 516.7 %all-reduce.12.cloned.1.call-start = ((), (), s32[]{:S(2)}) async-start(), calls=%async_computation.19 | async-start | bytes 20971520 | tf_op jit(solution)/shard_map/psum | solution.py:23
  673.2 8.0 copy-start.13
  673.2 8.0 copy-start.14
  673.2 8.0 copy-start.33
  685.8 504.1 %copy-start.18 = (f32[1280]{0:T(1024)S(1)}, f32[1280]{0:T(1024)}, u32[]{:S(2)}) copy-start(f32[1280]{0:T(1024)} %copy-done.17) | copy-start | bytes 15364
  685.8 504.1 %copy-start.24 = (f32[1024]{0:T(1024)S(1)}, f32[1024]{0:T(1024)}, u32[]{:S(2)}) copy-start(f32[1024]{0:T(1024)} %param.26) | copy-start | bytes 12292
  685.8 592.9 %all-reduce.14.cloned.1.call-start = ((), (), s32[]{:S(2)}) async-start(), calls=%async_computation.20 | async-start | bytes 6291456 | tf_op jit(solution)/shard_map/psum | solution.py:202
  827.6 366.1 %copy-start.22 = (f32[1280]{0:T(1024)S(1)}, f32[1280]{0:T(1024)}, u32[]{:S(2)}) copy-start(f32[1280]{0:T(1024)} %copy-done.21) | copy-start | bytes 15364
  827.6 366.1 %copy-start.20 = (f32[1280]{0:T(1024)S(1)}, f32[1280]{0:T(1024)}, u32[]{:S(2)}) copy-start(f32[1280]{0:T(1024)} %copy-done.19) | copy-start | bytes 15364
  1193.7 28.8 %copy-start.30 = (f32[1024]{0:T(1024)S(1)}, f32[1024]{0:T(1024)}, u32[]{:S(2)}) copy-start(f32[1024]{0:T(1024)} %param.25) | copy-start | bytes 12292
  (19 other events, 69.1 us)
Sparse Core Ops, SparseCore 0:
  10.2 22.3 all-gather.5
  38.3 24.2 all-gather.9
  64.7 24.2 all-gather.7
  104.9 188.8 all-reduce.7
  295.8 21.5 all-gather.11
  319.4 22.8 all-gather.13
  366.9 188.9 all-reduce.9
  588.3 36.5 reduce-scatter.8
  627.3 37.5 reduce-scatter.6
  667.8 24.8 reduce-scatter.12
  695.5 44.5 reduce-scatter.16
  742.4 44.5 reduce-scatter.14
  789.7 37.9 reduce-scatter.10
  830.7 359.1 all-reduce.11
  1192.2 86.5 all-reduce.13
where the time goes:
time: 1300 us; the launch traced here: 1290 us
  waiting for transfers between devices  1010 us (78%)
  matrix products  110 us (8%)
  other arithmetic  71.5 us (6%)
  local copies, waits for them, and re-layouts  56.8 us (4%)
  blocking collectives  33.2 us (3%)
  between operations  14.7 us (1%)
    psum x3, waiting for transfers between devices, head_total(): return lax.psum(partial_sum, 'tp')  731 us
    reduce_scatter x1, waiting for transfers between devices, on_device(): lax.psum_scatter(down_grad, 'fsdp', scatter_dimension=1, tiled=True)  47.2 us
    reduce_scatter x1, waiting for transfers between devices, on_device(): lax.psum_scatter(up_grad, 'fsdp', scatter_dimension=0, tiled=True)  46.9 us
    psum x1, waiting for transfers between devices, on_device(): lax.psum((spread[0], spread[1], spread[2], spread[3]), 'ctx')  42.5 us
    reduce_scatter x1, waiting for transfers between devices, on_device(): lax.psum_scatter(qkv_grad, 'fsdp', scatter_dimension=0, tiled=True)  40.7 us
  transfers between devices with their start and end apart: 15, of which 14 were waited for; matrix products, arithmetic and copies ran while one was open for 11% of the time, Pallas kernels for 0%

commit v1 on v0

v1 whole, which is shorter than its diff:
```python
import functools

import jax
import jax.numpy as jnp
from jax import lax
from jax.experimental import pallas as pl
from jax.experimental.pallas import tpu as pltpu
from jax.sharding import PartitionSpec as P

HEAD = 64
EPSILON = 1e-06
F32 = jnp.float32
LOW = jnp.bfloat16

NN = (((1,), (0,)), ((), ()))
NT = (((1,), (1,)), ((), ()))
TN = (((0,), (0,)), ((), ()))


def mm(left, right, dims=NN):
    return lax.dot_general(left, right, dims, preferred_element_type=F32)


def whole(shape):
    return pl.BlockSpec(shape, lambda t: (0,) * len(shape))


def part(shape):
    return pl.BlockSpec((1,) + shape, lambda t: (t,) + (0,) * len(shape))


def call(body, parts, ins, outs, args, flops, moved, exps=0):
    return pl.pallas_call(
        body,
        grid=(parts,),
        in_specs=ins,
        out_specs=[spec for spec, _ in outs],
        out_shape=[shape for _, shape in outs],
        compiler_params=pltpu.CompilerParams(
            dimension_semantics=("arbitrary",), vmem_limit_bytes=48 << 20
        ),
        cost_estimate=pl.CostEstimate(flops=flops, bytes_accessed=moved, transcendentals=exps),
    )(*args)


def attention_body(n_ref, w_ref, b_ref, keep_ref, p_ref, o_ref, l_ref):
    width = o_ref.shape[2]
    low = (mm(n_ref[...], w_ref[0]) + b_ref[0]).astype(LOW)
    p_ref[0] = low
    keep = keep_ref[...] > 0
    for head in range(width // HEAD):
        at = head * HEAD
        query = low[:, at : at + HEAD]
        key = low[:, width + at : width + at + HEAD]
        value = low[:, 2 * width + at : 2 * width + at + HEAD]
        scores = jnp.where(keep, mm(key, query, NT) * HEAD**-0.5, -1e30)
        top = jnp.max(scores, axis=0, keepdims=True)
        exponent = jnp.exp(scores - top)
        total = jnp.sum(exponent, axis=0, keepdims=True)
        probability = (exponent * (1.0 / total)).astype(LOW)
        o_ref[0, :, at : at + HEAD] = mm(probability, value, TN).astype(LOW)
        l_ref[0, head : head + 1, :] = top + jnp.log(total)


def attention(normed, weights, bias, keep):
    parts, width_in, width3 = weights.shape
    rows = normed.shape[0]
    width = width3 // 3
    heads = width // HEAD
    return call(
        attention_body,
        parts,
        [whole((rows, width_in)), part((width_in, width3)), part((1, width3)), whole((rows, 1))],
        [
            (part((rows, width3)), jax.ShapeDtypeStruct((parts, rows, width3), LOW)),
            (part((rows, width)), jax.ShapeDtypeStruct((parts, rows, width), LOW)),
            (part((heads, rows)), jax.ShapeDtypeStruct((parts, heads, rows), F32)),
        ],
        (normed, weights, bias, keep),
        2 * parts * rows * width_in * width3 + 4 * parts * rows * rows * width,
        2 * weights.size + 16 * parts * rows * width,
        parts * heads * rows * rows,
    )


def attention_back_body(d_ref, wo_ref, p_ref, l_ref, keep_ref, w_ref, dp_ref, dn_ref, db_ref):
    width = wo_ref.shape[2]
    grad_mixed = mm(d_ref[...], wo_ref[0]).astype(LOW)
    keep = keep_ref[...] > 0
    for head in range(width // HEAD):
        at = head * HEAD
        query = p_ref[0, :, at : at + HEAD]
        key = p_ref[0, :, width + at : width + at + HEAD]
        value = p_ref[0, :, 2 * width + at : 2 * width + at + HEAD]
        grad = grad_mixed[:, at : at + HEAD]
        scores = jnp.where(keep, mm(key, query, NT) * HEAD**-0.5, -1e30)
        probability = jnp.exp(scores - l_ref[0, head : head + 1, :])
        grad_probability = mm(value, grad, NT)
        grad_value = mm(probability.astype(LOW), grad)
        inner = jnp.sum(grad_probability * probability, axis=0, keepdims=True)
        grad_scores = (probability * (grad_probability - inner)).astype(LOW)
        grad_query = mm(grad_scores, key, TN) * HEAD**-0.5
        grad_key = mm(grad_scores, query) * HEAD**-0.5
        dp_ref[0, :, at : at + HEAD] = grad_query.astype(LOW)
        dp_ref[0, :, width + at : width + at + HEAD] = grad_key.astype(LOW)
        dp_ref[0, :, 2 * width + at : 2 * width + at + HEAD] = grad_value.astype(LOW)
    low = dp_ref[0]
    db_ref[0] = jnp.sum(low.astype(F32), axis=0, keepdims=True)
    grad_normed = mm(low, w_ref[0], NT)

    @pl.when(pl.program_id(0) == 0)
    def _():
        dn_ref[...] = grad_normed

    @pl.when(pl.program_id(0) > 0)
    def _():
        dn_ref[...] += grad_normed


def attention_back(grad, out_w, projected, log_total, keep, weights):
    parts, width_in, width3 = weights.shape
    rows = grad.shape[0]
    width = width3 // 3
    heads = width // HEAD
    return call(
        attention_back_body,
        parts,
        [
            whole((rows, width_in)),
            part((width_in, width)),
            part((rows, width3)),
            part((heads, rows)),
            whole((rows, 1)),
            part((width_in, width3)),
        ],
        [
            (part((rows, width3)), jax.ShapeDtypeStruct((parts, rows, width3), LOW)),
            (whole((rows, width_in)), jax.ShapeDtypeStruct((rows, width_in), F32)),
            (part((1, width3)), jax.ShapeDtypeStruct((parts, 1, width3), F32)),
        ],
        (grad, out_w, projected, log_total, keep, weights),
        2 * parts * rows * width_in * (width3 + width) + 10 * parts * rows * rows * width,
        2 * weights.size + 2 * out_w.size + 16 * parts * rows * width,
        parts * heads * rows * rows,
    )


def output_body(o_ref, w_ref, x_ref, b_ref, gain_ref, shift_ref, y_ref, n_ref):
    product = mm(o_ref[0], w_ref[0], NT)

    @pl.when(pl.program_id(0) == 0)
    def _():
        y_ref[...] = x_ref[...].astype(F32) + b_ref[...] + product

    @pl.when(pl.program_id(0) > 0)
    def _():
        y_ref[...] += product

    @pl.when(pl.program_id(0) == pl.num_programs(0) - 1)
    def _():
        n_ref[...] = layer_norm(y_ref[...], gain_ref[...], shift_ref[...]).astype(LOW)


def output_product(mixed, out_w, tokens, bias, gain, shift):
    parts, rows, width = mixed.shape
    wide = out_w.shape[1]
    return call(
        output_body,
        parts,
        [part((rows, width)), part((wide, width)), whole((rows, wide))] + [whole((1, wide))] * 3,
        [
            (whole((rows, wide)), jax.ShapeDtypeStruct((rows, wide), F32)),
            (whole((rows, wide)), jax.ShapeDtypeStruct((rows, wide), LOW)),
        ],
        (mixed, out_w, tokens, bias[None], gain[None], shift[None]),
        2 * parts * rows * width * wide,
        2 * out_w.size + 8 * rows * wide,
    )


def up_body(n_ref, w_ref, b_ref, a_ref, s_ref):
    hidden = mm(n_ref[...], w_ref[0]) + b_ref[0]
    bell = 0.5 * (1.0 + lax.erf(hidden * 0.5**0.5))
    a_ref[0] = (hidden * bell).astype(LOW)
    slope = bell + hidden * jnp.exp(hidden * hidden * -0.5) * 0.3989422804014327
    s_ref[0] = slope.astype(LOW)


def up_product(normed, weights, bias):
    parts, width_in, width = weights.shape
    rows = normed.shape[0]
    shape = jax.ShapeDtypeStruct((parts, rows, width), LOW)
    return call(
        up_body,
        parts,
        [whole((rows, width_in)), part((width_in, width)), part((1, width))],
        [(part((rows, width)), shape), (part((rows, width)), shape)],
        (normed, weights, bias),
        2 * parts * rows * width_in * width,
        2 * weights.size + 4 * parts * rows * width,
        2 * parts * rows * width,
    )


def down_body(a_ref, w_ref, g_ref, s_ref, wu_ref, r_ref, du_ref, dn_ref, db_ref):
    branch = mm(a_ref[0], w_ref[0], NT)
    low = (mm(g_ref[...], w_ref[0]) * s_ref[0].astype(F32)).astype(LOW)
    du_ref[0] = low
    db_ref[0] = jnp.sum(low.astype(F32), axis=0, keepdims=True)
    grad_normed = mm(low, wu_ref[0], NT)

    @pl.when(pl.program_id(0) == 0)
    def _():
        r_ref[...] = branch
        dn_ref[...] = grad_normed

    @pl.when(pl.program_id(0) > 0)
    def _():
        r_ref[...] += branch
        dn_ref[...] += grad_normed


def down_product(active, down_w, grad, slope, up_w):
    parts, rows, width = active.shape
    wide = down_w.shape[1]
    return call(
        down_body,
        parts,
        [
            part((rows, width)),
            part((wide, width)),
            whole((rows, wide)),
            part((rows, width)),
            part((wide, width)),
        ],
        [
            (whole((rows, wide)), jax.ShapeDtypeStruct((rows, wide), F32)),
            (part((rows, width)), jax.ShapeDtypeStruct((parts, rows, width), LOW)),
            (whole((rows, wide)), jax.ShapeDtypeStruct((rows, wide), F32)),
            (part((1, width)), jax.ShapeDtypeStruct((parts, 1, width), F32)),
        ],
        (active, down_w, grad, slope, up_w),
        6 * parts * rows * width * wide,
        4 * down_w.size + 6 * parts * rows * width + 8 * rows * wide,
    )


def weight_body(l_ref, r_ref, w_ref):
    w_ref[0] = mm(l_ref[...], r_ref[0]).astype(LOW)


def weight_product(turned, right):
    parts, rows, width = right.shape
    wide = turned.shape[0]
    return call(
        weight_body,
        parts,
        [whole((wide, rows)), part((rows, width))],
        [(part((wide, width)), jax.ShapeDtypeStruct((parts, wide, width), LOW))],
        (turned, right),
        2 * parts * rows * width * wide,
        2 * parts * width * (rows + wide),
    )[0]


def layer_norm(values, gain, shift):
    center = values - jnp.mean(values, axis=-1, keepdims=True)
    spread = jnp.mean(center * center, axis=-1, keepdims=True)
    return center * lax.rsqrt(spread + EPSILON) * gain + shift


def layer_norm_back(values, gain, grad):
    center = values - jnp.mean(values, axis=-1, keepdims=True)
    scale = lax.rsqrt(jnp.mean(center * center, axis=-1, keepdims=True) + EPSILON)
    unit = center * scale
    scaled = grad * gain
    back = scale * (
        scaled
        - jnp.mean(scaled, axis=-1, keepdims=True)
        - unit * jnp.mean(scaled * unit, axis=-1, keepdims=True)
    )
    return back, jnp.sum(grad * unit, axis=0), jnp.sum(grad, axis=0)


def on_device(
    inputs,
    cotangent,
    visible,
    w_qkv,
    b_qv,
    w_out,
    b_out,
    w_up,
    b_up,
    w_down,
    b_down,
    gain_one,
    shift_one,
    gain_two,
    shift_two,
):
    images, half, wide = inputs.shape
    ctx_at, tp_at = lax.axis_index("ctx"), lax.axis_index("tp")
    blocks, parts = lax.axis_size("ctx"), lax.axis_size("tp")
    assert blocks == 2 and images == blocks * parts
    first = blocks * tp_at
    mine, other = first + ctx_at, first + 1 - ctx_at
    spread_axes = ("tp", "fsdp")

    def swap(values):
        return lax.ppermute(values, "ctx", [(0, 1), (1, 0)])

    def pick(values, index):
        return lax.dynamic_index_in_dim(values, index, 0, keepdims=False)

    def in_order(own, received):
        first_half = jnp.where(ctx_at == 0, own, received)
        second_half = jnp.where(ctx_at == 0, received, own)
        return first_half, second_half

    def gather(shard):
        full = lax.all_gather(shard, spread_axes, axis=0, tiled=True)
        return full.reshape(parts, wide, shard.shape[1])

    heads_width = w_qkv.shape[2]
    hidden_half = w_up.shape[1] // 2
    qkv_w = gather(w_qkv.astype(LOW).reshape(-1, 3 * heads_width))
    out_w = gather(w_out.T.astype(LOW))
    up_w = gather(lax.dynamic_slice_in_dim(w_up, ctx_at * hidden_half, hidden_half, 1).astype(LOW))
    down_w = gather(
        lax.dynamic_slice_in_dim(w_down, ctx_at * hidden_half, hidden_half, 0).T.astype(LOW)
    )
    biases = lax.all_gather(jnp.concatenate([b_qv.reshape(-1), b_up]), "tp", axis=0)
    bias_q, bias_v = biases[:, :heads_width], biases[:, heads_width : 2 * heads_width]
    qkv_bias = jnp.concatenate([bias_q, jnp.zeros_like(bias_q), bias_v], axis=1)[:, None]
    up_bias = lax.dynamic_slice_in_dim(
        biases, 2 * heads_width + ctx_at * hidden_half, hidden_half, 1
    )[:, None]

    tokens = jnp.concatenate([pick(inputs, mine), swap(pick(inputs, other))], axis=0)
    cot_pair = jnp.stack([pick(cotangent, mine), pick(cotangent, other)])
    cot_swapped = swap(cot_pair)
    mine_seen = pick(visible, mine).reshape(blocks, half)
    other_seen = pick(visible, other).reshape(blocks, half)
    keep = jnp.concatenate([pick(mine_seen, ctx_at), pick(mine_seen, 1 - ctx_at)])
    keep_other = jnp.concatenate([pick(other_seen, 1 - ctx_at), pick(other_seen, ctx_at)])
    keep, keep_other = keep[:, None], keep_other[:, None]
    keep_all = jnp.concatenate([keep, keep_other]).astype(LOW)
    grad_low = (
        jnp.concatenate([cot_pair[0], cot_swapped[1], cot_swapped[0], cot_pair[1]]) * keep_all
    )
    rows = 2 * half

    flat_in = tokens.astype(F32)
    normed_low = layer_norm(flat_in, gain_one, shift_one).astype(LOW)
    projected, mixed, log_total = attention(normed_low, qkv_w, qkv_bias, keep)
    residual, normed_two = output_product(mixed, out_w, tokens, b_out, gain_two, shift_two)
    both = jnp.concatenate([normed_two, swap(normed_two)])
    active, slope = up_product(both, up_w, up_bias)
    down_grad = weight_product(grad_low.T, active)
    branch, grad_hidden, grad_both, up_bias_grad = down_product(
        active, down_w, grad_low, slope, up_w
    )
    up_grad = weight_product(both.T, grad_hidden)

    sent = jnp.concatenate([residual[half:] + branch[half:rows], branch[rows : rows + half]])
    came = swap(sent.astype(LOW)).astype(F32)
    out_mine = residual[:half] + branch[:half] + came[half:] + b_down
    out_other = branch[rows + half :] + came[:half] + b_down
    out_mine = (out_mine * keep[:half].astype(F32)).astype(LOW)
    out_other = (out_other * keep_other[half:].astype(F32)).astype(LOW)
    out_pair = jnp.stack(in_order(out_mine, out_other))
    result = lax.all_gather(out_pair, "tp", axis=0, tiled=True).astype(F32)

    grad_normed_two = grad_both[:rows] + swap(grad_both[rows:].astype(LOW)).astype(F32)
    back_two, gain_two_grad, shift_two_grad = layer_norm_back(residual, gain_two, grad_normed_two)
    grad_out = grad_low[:rows].astype(F32)
    grad_residual = grad_out + back_two
    grad_attended = grad_residual.astype(LOW)
    out_grad = weight_product(grad_attended.T, mixed)
    grad_projected, grad_normed, qkv_bias_grad = attention_back(
        grad_attended, out_w, projected, log_total, keep, qkv_w
    )
    qkv_grad = weight_product(normed_low.T, grad_projected)
    back_one, gain_one_grad, shift_one_grad = layer_norm_back(flat_in, gain_one, grad_normed)
    grad_in = (grad_residual + back_one).astype(LOW)
    grad_in_pair = jnp.stack(in_order(grad_in[:half], swap(grad_in[half:])))
    grad_inputs = lax.all_gather(grad_in_pair, "tp", axis=0, tiled=True).astype(F32)

    def scatter(grad):
        flat = grad.reshape(-1, grad.shape[2])
        return lax.psum_scatter(flat, spread_axes, scatter_dimension=0, tiled=True)

    down_own, up_own, out_own, qkv_own = (
        scatter(down_grad),
        scatter(up_grad),
        scatter(out_grad),
        scatter(qkv_grad),
    )
    out_total = out_own.astype(F32) + swap(out_own).astype(F32)
    qkv_total = qkv_own.astype(F32) + swap(qkv_own).astype(F32)
    up_total = jnp.concatenate(in_order(up_own, swap(up_own)), axis=1).astype(F32)
    down_total = jnp.concatenate(in_order(down_own, swap(down_own)), axis=1).astype(F32)

    up_bias_slot = jnp.zeros((parts, 2, hidden_half), F32)
    up_bias_slot = lax.dynamic_update_slice(up_bias_slot, up_bias_grad, (0, ctx_at, 0))
    qkv_bias_grad = qkv_bias_grad.reshape(parts, 3, heads_width)
    small = lax.psum(
        (
            qkv_bias_grad[:, 0::2],
            up_bias_slot,
            jnp.sum(grad_attended.astype(F32), axis=0),
            jnp.sum(grad_out, axis=0),
            gain_one_grad,
            shift_one_grad,
            gain_two_grad,
            shift_two_grad,
        ),
        ("fsdp", "ctx", "tp"),
    )
    return (
        result,
        grad_inputs,
        qkv_total.reshape(-1, 3, heads_width),
        pick(small[0], tp_at),
        out_total.T,
        small[2],
        up_total,
        pick(small[1], tp_at).reshape(-1),
        down_total.T,
        small[3],
        small[4],
        small[5],
        small[6],
        small[7],
    )


def solution(mesh):
    placed = (
        P("fsdp", "ctx", None),
        P("fsdp", "ctx", None),
        P("fsdp", None),
        P("fsdp", None, "tp"),
        P(None, "tp"),
        P("tp", "fsdp"),
        P(),
        P("fsdp", "tp"),
        P("tp"),
        P("tp", "fsdp"),
        P(),
        P(),
        P(),
        P(),
        P(),
    )
    return jax.shard_map(
        on_device,
        mesh=mesh,
        in_specs=placed,
        out_specs=(
            P("fsdp", "ctx", None),
            P("fsdp", "ctx", None),
            P("fsdp", None, "tp"),
            P(None, "tp"),
            P("tp", "fsdp"),
            P(),
            P("fsdp", "tp"),
            P("tp"),
            P("tp", "fsdp"),
            P(),
            P(),
            P(),
            P(),
            P(),
        ),
        check_vma=False,
    )
```

time: 1300 us -> 717 us (0.55)
  waiting for transfers between devices: 1010 us -> 416 us
  matrix products: 110 us -> 0 us
  Pallas kernels: 0 us -> 68.6 us
  local copies, waits for them, and re-layouts: 56.8 us -> 106 us
  other arithmetic: 71.5 us -> 40.1 us
  blocking collectives: 33.2 us -> 54.4 us
    psum x4 -> x0, waiting for transfers between devices: 773 us -> none  [the longest x3 731 us: head_total(): return lax.psum(partial_sum, 'tp')]
    all_gather x5 -> x6, waiting for transfers between devices: 76.5 us -> 218 us  [the longest x4 134 us: gather(): full = lax.all_gather(shard, spread_axes, axis=0, tiled=True)]
    dot_general x18 -> x0, matrix products: 110 us -> none  [the longest x1 18.4 us: on_device(): jnp.dot(grad_branch, down_w.T, preferred_element_type=jnp.float32)]
    pallas_call x0 -> x9, Pallas kernels: none -> 68.6 us  [call(): pl.pallas_call(body, grid=(parts,), in_specs=ins, out_specs=[spec for spe...]
    ppermute x0 -> x10, waiting for transfers between devices: none -> 41.3 us  [swap(): return lax.ppermute(values, 'ctx', [(0, 1), (1, 0)])]
    psum x1, blocking collectives: 25.6 us -> 40.6 us  [on_device(): lax.psum((qkv_bias_grad[:, 0::2], up_bias_slot, jnp.sum(grad_attended.ast...]
    ppermute x0 -> x10, starting transfers between devices: none -> 14.2 us  [swap(): return lax.ppermute(values, 'ctx', [(0, 1), (1, 0)])]
    add x3 -> x1, other arithmetic: 13.8 us -> 0.08 us  [on_device(): qkv_total = qkv_own.astype(F32) + swap(qkv_own).astype(F32)]
  transfers between devices with their start and end apart: 15 -> 20, of which waited for: 14 -> 13; matrix products, arithmetic and copies ran while one was open for 11% -> 16% of each run, Pallas kernels for 0% -> 6%
where the time goes in v1:
time: 717 us; the launch traced here: 715 us
  waiting for transfers between devices  416 us (58%)
  local copies, waits for them, and re-layouts  106 us (15%)
  Pallas kernels  68.6 us (10%)
  blocking collectives  54.4 us (8%)
  other arithmetic  40.1 us (6%)
  between operations  14.9 us (2%)
  starting transfers between devices  14.6 us (2%)
    reduce_scatter x4, waiting for transfers between devices, scatter(): return lax.psum_scatter(flat, spread_axes, scatter_dimension=0, tiled=True)  157 us
    all_gather x4, waiting for transfers between devices, gather(): full = lax.all_gather(shard, spread_axes, axis=0, tiled=True)  134 us
    pallas_call x9, Pallas kernels, call(): pl.pallas_call(body, grid=(parts,), in_specs=ins, out_specs=[spec for spe...  68.6 us
    all_gather x1, waiting for transfers between devices, on_device(): lax.all_gather(grad_in_pair, 'tp', axis=0, tiled=True).astype(F32)  51 us
    ppermute x10, waiting for transfers between devices, swap(): return lax.ppermute(values, 'ctx', [(0, 1), (1, 0)])  41.3 us
    psum x1, blocking collectives, on_device(): lax.psum((qkv_bias_grad[:, 0::2], up_bias_slot, jnp.sum(grad_attended.ast...  40.6 us
    all_gather x1, waiting for transfers between devices, on_device(): result = lax.all_gather(out_pair, 'tp', axis=0, tiled=True).astype(F32)  32.3 us
    reshape x4, local copies, waits for them, and re-layouts, scatter(): flat = grad.reshape(-1, grad.shape[2])  24.5 us
  transfers between devices with their start and end apart: 20, of which 13 were waited for; matrix products, arithmetic and copies ran while one was open for 16% of the time, Pallas kernels for 6%

profile of v1, /device:TPU:0, one launch (start us, length us, event | category | flops | bytes accessed | tf_op | source)
XLA Modules:
  0.0 714.7 jit_solution(12044864387465751447)
XLA Ops:
  20.5 13.9 %all-gather.1 = f32[4,1,1536]{2,1,0:T(1,128)S(1)} all-gather(f32[1,1,1536]{2,1,0:T(1,128)S(1)} %reshape.166), channel_id=2, replica_groups=mesh['fsdp'=4,'ctx'=2,'tp'=4] {'tp'}, dimensions={0}, use_global_device_ids=true | all-gather | bytes 30720 | tf_op jit(solution)/shard_map/all_gather | solution.py:333
  37.3 16.9 %all-gather.11.cloned.1.call-done = bf16[4096,256]{0,1:T(8,128)(2,1)} async-done(((bf16[256,256]{0,1:T(8,128)(2,1)}), bf16[4096,256]{0,1:T(8,128)(2,1)}) %all-gather.11.cloned.1.call-update) | async-done | bytes 2097168 | tf_op jit(solution)/shard_map/all_gather | solution.py:322
  54.2 3.3 copy.104
  57.5 64.1 %all-gather.9.cloned.1.call-done = bf16[4096,768]{0,1:T(8,128)(2,1)} async-done(((bf16[256,768]{0,1:T(8,128)(2,1)}), bf16[4096,768]{0,1:T(8,128)(2,1)}) %all-gather.9.cloned.1.call-update) | async-done | bytes 6291472 | tf_op jit(solution)/shard_map/all_gather | solution.py:322
  121.6 8.7 %copy.101 = bf16[4096,768]{1,0:T(8,128)(2,1)} copy(bf16[4096,768]{0,1:T(8,128)(2,1)} %all-gather.9.cloned.1.call-done) | data formatting | bytes 12582912 | tf_op jit(solution)/shard_map/all_gather | solution.py:322
  130.3 11.3 %shard_map.254 = (bf16[4,320,768]{2,1,0:T(8,128)(2,1)S(1)}, bf16[4,320,256]{2,1,0:T(8,128)(2,1)S(1)}, f32[4,4,320]{2,1,0:T(4,128)S(1)}) custom-call(bf16[320,1024]{1,0:T(8,128)(2,1)S(1)} %copy.102.n_ref, bf16[4,1024,768]{2,1,0:T(8,128)(2,1)} %bitcast.65, f32[4,1,768]{2,1,0:T(1,128)S(1)} %broadcast_in_dim.17.b_ref, s32[320,1]{1,0:T(8,128)S(1)} %broadcast_in_dim.24.keep_ref), custom_call_target="tpu_custom_call" | custom-call | flops 2432696320 | bytes 11534336 | tf_op jit(solution)/shard_map/pallas_call | solution.py:33
  141.7 3.3 shard_map.255
  156.9 18.3 %all-gather.15.cloned.1.call-done = bf16[4096,512]{0,1:T(8,128)(2,1)} async-done(((bf16[256,512]{0,1:T(8,128)(2,1)}), bf16[4096,512]{0,1:T(8,128)(2,1)}) %all-gather.15.cloned.1.call-update) | async-done | bytes 4194320 | tf_op jit(solution)/shard_map/all_gather | solution.py:322
  175.2 6.4 copy.110
  191.4 35.1 %all-gather.13.cloned.1.call-done = bf16[4096,512]{1,0:T(8,128)(2,1)} async-done(((bf16[256,512]{1,0:T(8,128)(2,1)}), bf16[4096,512]{1,0:T(8,128)(2,1)}) %all-gather.13.cloned.1.call-update) | async-done | bytes 4194320 | tf_op jit(solution)/shard_map/all_gather | solution.py:322
  227.8 7.5 %shard_map.256 = (bf16[4,640,512]{2,1,0:T(8,128)(2,1)S(1)}, bf16[4,640,512]{2,1,0:T(8,128)(2,1)}) custom-call(bf16[640,1024]{1,0:T(8,128)(2,1)S(1)} %copy-done.14, bf16[4,1024,512]{2,1,0:T(8,128)(2,1)} %bitcast.89, f32[4,1,512]{2,1,0:T(1,128)S(1)} %constant_dynamic-slice_fusion.6.b_ref), custom_call_target="tpu_custom_call" | custom-call | flops 2684354560 | bytes 9437184 | tf_op jit(solution)/shard_map/pallas_call | solution.py:33
  236.9 14.6 %shard_map.257 = (f32[640,1024]{1,0:T(8,128)S(1)}, bf16[4,640,512]{2,1,0:T(8,128)(2,1)}, f32[640,1024]{1,0:T(8,128)}, f32[4,1,512]{2,1,0:T(1,128)S(1)}) custom-call(bf16[4,640,512]{2,1,0:T(8,128)(2,1)} %copy-done.20, bf16[4,1024,512]{2,1,0:T(8,128)(2,1)} %bitcast.67, bf16[640,1024]{1,0:T(8,128)(2,1)S(1)} %copy-done.13, ...), custom_call_target="tpu_custom_call" | custom-call | flops 8053063680 | bytes 21495808 | tf_op jit(solution)/shard_map/pallas_call | solution.py:33
  260.3 3.3 copy.121
  263.6 8.9 %collective-permute-done.4 = bf16[320,1024]{1,0:T(8,128)(2,1)} collective-permute-done((bf16[320,1024]{1,0:T(8,128)(2,1)}, bf16[320,1024]{1,0:T(8,128)(2,1)}, u32[]{:S(2)}, u32[]{:S(2)}) %collective-permute-start.4) | collective-permute-done | bytes 655392 | tf_op jit(solution)/shard_map/ppermute | solution.py:311
  287.3 4.9 shard_map.261
  292.2 6.4 copy.130
  306.9 11.7 %collective-permute-done.3 = bf16[320,1024]{1,0:T(8,128)(2,1)} collective-permute-done((bf16[320,1024]{1,0:T(8,128)(2,1)}, bf16[320,1024]{1,0:T(8,128)(2,1)}, u32[]{:S(2)}, u32[]{:S(2)}) %collective-permute-start.3) | collective-permute-done | bytes 655392 | tf_op jit(solution)/shard_map/ppermute | solution.py:311
  328.0 14.9 %shard_map.258 = (bf16[4,320,768]{2,1,0:T(8,128)(2,1)S(1)}, f32[320,1024]{1,0:T(8,128)S(1)}, f32[4,1,768]{2,1,0:T(1,128)S(1)}) custom-call(bf16[320,1024]{1,0:T(8,128)(2,1)S(1)} %copy.123.d_ref, bf16[4,1024,256]{2,1,0:T(8,128)(2,1)} %bitcast.59, bf16[4,320,768]{2,1,0:T(8,128)(2,1)S(1)} %copy-done.24, f32[4,4,320]{2,1,0:T(4,128)S(1)} %get-tuple-element.36.l_ref, ...), custom_call_target="tpu_custom_call" | custom-call | flops 3732930560 | bytes 13631488 | tf_op jit(solution)/shard_map/pallas_call | solution.py:33
  351.7 11.0 %collective-permute-done.5 = bf16[160,1024]{0,1:T(8,128)(2,1)S(1)} collective-permute-done((bf16[160,1024]{0,1:T(8,128)(2,1)S(1)}, bf16[160,1024]{0,1:T(8,128)(2,1)S(1)}, u32[]{:S(2)}, u32[]{:S(2)}) %collective-permute-start.5) | collective-permute-done | bytes 327712 | tf_op jit(solution)/shard_map/ppermute | solution.py:311
  368.1 4.9 shard_map.262
  373.0 6.6 copy.131
  381.6 5.4 shard_map.259
  386.9 8.5 %copy.127 = bf16[4096,768]{0,1:T(8,128)(2,1)} copy(bf16[4096,768]{1,0:T(8,128)(2,1)} %bitcast.64) | data formatting | bytes 12582912 | tf_op jit(solution)/shard_map/reshape | solution.py:391
  395.7 40.6 %all-reduce = (f32[4,2,256]{2,0,1:T(4,128)S(1)}, f32[1024]{0:T(1024)}, f32[4,2,512]{2,1,0:T(2,128)S(1)}, f32[1024]{0:T(1024)}, f32[1024]{0:T(1024)}, /*index=5*/f32[1024]{0:T(1024)}, f32[1024]{0:T(1024)}, f32[1024]{0:T(1024)}) all-reduce(f32[4,2,256]{2,0,1:T(4,128)S(1)} %slice.77, ...), channel_id=1, replica_groups=mesh['fsdp'=4,'ctx'=2,'tp'=4] {'fsdp','ctx','tp'}, use_global_device_ids=true, to_apply=%region_9.10 | all-reduce | flops 12288 | bytes 98304 | tf_op jit(solution)/shard_map/psum | solution.py:408
  439.7 3.3 collective-permute-done.7
  444.6 32.3 %all-gather.17.cloned.1.call-done = bf16[8,160,1024]{2,1,0:T(8,128)(2,1)} async-done(((bf16[2,160,1024]{2,1,0:T(8,128)(2,1)}), bf16[8,160,1024]{2,1,0:T(8,128)(2,1)}) %all-gather.17.cloned.1.call-update) | async-done | bytes 2621456 | tf_op jit(solution)/shard_map/all_gather | solution.py:373
  476.9 4.7 convert_element_type.99
  481.6 51.0 %all-gather.19.cloned.1.call-done = bf16[8,160,1024]{2,1,0:T(8,128)(2,1)} async-done(((bf16[2,160,1024]{2,1,0:T(8,128)(2,1)}), bf16[8,160,1024]{2,1,0:T(8,128)(2,1)}) %all-gather.19.cloned.1.call-update) | async-done | bytes 2621456 | tf_op jit(solution)/shard_map/all_gather | solution.py:388
  532.6 4.7 convert_element_type.104
  537.4 70.3 %reduce-scatter.11.cloned.1.call-done = bf16[256,512]{0,1:T(8,128)(2,1)} async-done(((bf16[4096,512]{0,1:T(8,128)(2,1)}), bf16[256,512]{0,1:T(8,128)(2,1)}) %reduce-scatter.11.cloned.1.call-update) | async-done | bytes 262160 | tf_op jit(solution)/shard_map/reduce_scatter | solution.py:392
  609.2 87.1 %reduce-scatter.5.cloned.1.call-done = bf16[256,768]{0,1:T(8,128)(2,1)} async-done(((bf16[4096,768]{0,1:T(8,128)(2,1)}), bf16[256,768]{0,1:T(8,128)(2,1)}) %reduce-scatter.5.cloned.1.call-update) | async-done | bytes 393232 | tf_op jit(solution)/shard_map/reduce_scatter | solution.py:392
  700.2 6.4 collective-permute-done.6
  (224 shorter events, 109.5 us)
Async XLA Ops:
  7.2 47.0 %all-gather.11.cloned.1.call-start = ((), (), s32[]{:S(2)}) async-start(), calls=%async_computation.5 | async-start | bytes 2228224 | tf_op jit(solution)/shard_map/all_gather | solution.py:322
  9.0 112.6 %all-gather.9.cloned.1.call-start = ((), (), s32[]{:S(2)}) async-start(), calls=%async_computation.4 | async-start | bytes 6684672 | tf_op jit(solution)/shard_map/all_gather | solution.py:322
  11.1 164.1 %all-gather.15.cloned.1.call-start = ((), (), s32[]{:S(2)}) async-start(), calls=%async_computation.7 | async-start | bytes 4456448 | tf_op jit(solution)/shard_map/all_gather | solution.py:322
  11.9 214.6 %all-gather.13.cloned.1.call-start = ((), (), s32[]{:S(2)}) async-start(), calls=%async_computation.6 | async-start | bytes 4456448 | tf_op jit(solution)/shard_map/all_gather | solution.py:322
  13.8 422.5 %reduce-scatter.7.cloned.1.call-start = ((), (), s32[]{:S(2)}) async-start(), calls=%async_computation.11 | async-start | bytes 2228224 | tf_op jit(solution)/shard_map/reduce_scatter | solution.py:392
  15.2 19.2 %copy-start.34 = (bf16[1,160,1024]{2,1,0:T(8,128)(2,1)}, bf16[1,160,1024]{2,1,0:T(8,128)(2,1)S(1)}, u32[]{:S(2)}) copy-start(bf16[1,160,1024]{2,1,0:T(8,128)(2,1)S(1)} %get-tuple-element.111) | copy-start | bytes 983044
  15.2 19.2 %copy-start.35 = (bf16[1,160,1024]{2,1,0:T(8,128)(2,1)}, bf16[1,160,1024]{2,1,0:T(8,128)(2,1)S(1)}, u32[]{:S(2)}) copy-start(bf16[1,160,1024]{2,1,0:T(8,128)(2,1)S(1)} %get-tuple-element.112) | copy-start | bytes 983044
  15.5 19.4 %collective-permute-start = (bf16[160,1024]{0,1:T(8,128)(2,1)S(1)}, bf16[160,1024]{0,1:T(8,128)(2,1)S(1)}, u32[]{:S(2)}, u32[]{:S(2)}) collective-permute-start(bf16[160,1024]{0,1:T(8,128)(2,1)S(1)} %bitcast.77), channel_id=1, source_target_pairs={{0,4},{4,0},{1,5},{5,1},{2,6},{6,2},{3,7},{7,3},{8,12},{12,8},{9,1... | collective-permute-start | bytes 983048 | tf_op jit(solution)/shard_map/ppermute | solution.py:311
  19.4 130.4 %collective-permute-start.2 = (bf16[2,160,1024]{2,1,0:T(8,128)(2,1)}, bf16[2,160,1024]{2,1,0:T(8,128)(2,1)}, u32[]{:S(2)}, u32[]{:S(2)}) collective-permute-start(bf16[2,160,1024]{2,1,0:T(8,128)(2,1)} %pad_maximum_fusion.4), channel_id=1, source_target_pairs={{0,4},{4,0},{1,5},{5,1},{2,6},{6,2},{3,7},{7,3},{8,12},{12,8},{9,1... | collective-permute-start | bytes 1966088 | tf_op jit(solution)/shard_map/ppermute | solution.py:311
  34.7 95.5 %copy-start.15 = (s32[320,1]{1,0:T(8,128)}, s32[320,1]{1,0:T(8,128)S(1)}, u32[]{:S(2)}) copy-start(s32[320,1]{1,0:T(8,128)S(1)} %broadcast_in_dim.24.keep_ref) | copy-start | bytes 3844
  57.5 84.1 %copy-start.2 = (bf16[4096,256]{1,0:T(8,128)(2,1)}, bf16[4096,256]{1,0:T(8,128)(2,1)S(1)}, u32[]{:S(2)}) copy-start(bf16[4096,256]{1,0:T(8,128)(2,1)S(1)} %copy.104) | copy-start | bytes 6291460
  130.3 11.4 %copy-start.17 = (f32[1024]{0:T(1024)S(1)}, f32[1024]{0:T(1024)}, u32[]{:S(2)}) copy-start(f32[1024]{0:T(1024)} %param.28) | copy-start | bytes 12292
  130.3 11.4 %copy-start.18 = (f32[1024]{0:T(1024)S(1)}, f32[1024]{0:T(1024)}, u32[]{:S(2)}) copy-start(f32[1024]{0:T(1024)} %param.21) | copy-start | bytes 12292
  130.3 11.4 %copy-start.19 = (f32[1024]{0:T(1024)S(1)}, f32[1024]{0:T(1024)}, u32[]{:S(2)}) copy-start(f32[1024]{0:T(1024)} %param.29) | copy-start | bytes 12292
  145.0 113.4 %copy-start.3 = (f32[320,1024]{1,0:T(8,128)}, f32[320,1024]{1,0:T(8,128)S(1)}, u32[]{:S(2)}) copy-start(f32[320,1024]{1,0:T(8,128)S(1)} %get-tuple-element.29) | copy-start | bytes 3932164
  145.0 38.8 %collective-permute-start.1 = (bf16[320,1024]{1,0:T(8,128)(2,1)}, bf16[320,1024]{1,0:T(8,128)(2,1)}, u32[]{:S(2)}, u32[]{:S(2)}) collective-permute-start(bf16[320,1024]{1,0:T(8,128)(2,1)} %get-tuple-element.30), channel_id=1, source_target_pairs={{0,4},{4,0},{1,5},{5,1},{2,6},{6,2},{3,7},{7,3},{8,12},{12,8},{9,1... | collective-permute-start | bytes 1966088 | tf_op jit(solution)/shard_map/ppermute | solution.py:311
  255.3 17.2 %collective-permute-start.4 = (bf16[320,1024]{1,0:T(8,128)(2,1)}, bf16[320,1024]{1,0:T(8,128)(2,1)}, u32[]{:S(2)}, u32[]{:S(2)}) collective-permute-start(bf16[320,1024]{1,0:T(8,128)(2,1)} %slice.131), channel_id=1, source_target_pairs={{0,4},{4,0},{1,5},{5,1},{2,6},{6,2},{3,7},{7,3},{8,12},{12,8},{9,1... | collective-permute-start | bytes 1966088 | tf_op jit(solution)/shard_map/ppermute | solution.py:311
  260.3 14.5 %copy-start.27 = (f32[320,1024]{0,1:T(8,128)S(1)}, f32[320,1024]{0,1:T(8,128)}, u32[]{:S(2)}) copy-start(f32[320,1024]{0,1:T(8,128)} %copy.106) | copy-start | bytes 3932164
  284.2 154.2 %reduce-scatter.9.cloned.1.call-start = ((), (), s32[]{:S(2)}) async-start(), calls=%async_computation.12 | async-start | bytes 4456448 | tf_op jit(solution)/shard_map/reduce_scatter | solution.py:392
  298.6 178.3 %all-gather.17.cloned.1.call-start = ((), (), s32[]{:S(2)}) async-start(), calls=%async_computation.8 | async-start | bytes 3276800 | tf_op jit(solution)/shard_map/all_gather | solution.py:373
  302.2 16.4 %collective-permute-start.3 = (bf16[320,1024]{1,0:T(8,128)(2,1)}, bf16[320,1024]{1,0:T(8,128)(2,1)}, u32[]{:S(2)}, u32[]{:S(2)}) collective-permute-start(bf16[320,1024]{1,0:T(8,128)(2,1)} %pad_maximum_fusion.5), channel_id=1, source_target_pairs={{0,4},{4,0},{1,5},{5,1},{2,6},{6,2},{3,7},{7,3},{8,12},{12,8},{9,1... | collective-permute-start | bytes 1966088 | tf_op jit(solution)/shard_map/ppermute | solution.py:311
  306.9 15.2 %copy-start.28 = (f32[320,1024]{0,1:T(8,128)S(1)}, f32[320,1024]{0,1:T(8,128)}, u32[]{:S(2)}) copy-start(f32[320,1024]{0,1:T(8,128)} %copy.106) | copy-start | bytes 3932164
  306.9 15.2 %copy-start.42 = (f32[1024]{0:T(1024)S(1)}, f32[1024]{0:T(1024)}, u32[]{:S(2)}) copy-start(f32[1024]{0:T(1024)} %param.25) | copy-start | bytes 12292
  326.1 206.6 %all-gather.19.cloned.1.call-start = ((), (), s32[]{:S(2)}) async-start(), calls=%async_computation.9 | async-start | bytes 3276800 | tf_op jit(solution)/shard_map/all_gather | solution.py:388
  350.2 12.5 %collective-permute-start.5 = (bf16[160,1024]{0,1:T(8,128)(2,1)S(1)}, bf16[160,1024]{0,1:T(8,128)(2,1)S(1)}, u32[]{:S(2)}, u32[]{:S(2)}) collective-permute-start(bf16[160,1024]{0,1:T(8,128)(2,1)S(1)} %slice.92), channel_id=1, source_target_pairs={{0,4},{4,0},{1,5},{5,1},{2,6},{6,2},{3,7},{7,3},{8,12},{12,8},{9,1... | collective-permute-start | bytes 983048 | tf_op jit(solution)/shard_map/ppermute | solution.py:311
  366.1 241.5 %reduce-scatter.11.cloned.1.call-start = ((), (), s32[]{:S(2)}) async-start(), calls=%async_computation.13 | async-start | bytes 4456448 | tf_op jit(solution)/shard_map/reduce_scatter | solution.py:392
  379.6 316.6 %reduce-scatter.5.cloned.1.call-start = ((), (), s32[]{:S(2)}) async-start(), calls=%async_computation.10 | async-start | bytes 6684672 | tf_op jit(solution)/shard_map/reduce_scatter | solution.py:392
  436.3 6.7 collective-permute-start.7
  438.4 170.7 %collective-permute-start.8 = (bf16[256,512]{0,1:T(8,128)(2,1)}, bf16[256,512]{0,1:T(8,128)(2,1)S(1)}, u32[]{:S(2)}, u32[]{:S(2)}) collective-permute-start(bf16[256,512]{0,1:T(8,128)(2,1)} %reduce-scatter.9.cloned.1.call-done), channel_id=1, source_target_pairs={{0,4},{4,0},{1,5},{5,1},{2,6},{6,2},{3,7},{7,3},{8,12},{12,8},{9,1... | collective-permute-start | bytes 786440 | tf_op jit(solution)/shard_map/ppermute | solution.py:311
  481.6 127.5 %copy-start.37 = (bf16[256,512]{0,1:T(8,128)(2,1)S(1)}, bf16[256,512]{0,1:T(8,128)(2,1)}, u32[]{:S(2)}) copy-start(bf16[256,512]{0,1:T(8,128)(2,1)} %reduce-scatter.9.cloned.1.call-done) | copy-start | bytes 786436
  607.6 91.5 %collective-permute-start.9 = (bf16[256,512]{0,1:T(8,128)(2,1)}, bf16[256,512]{0,1:T(8,128)(2,1)S(1)}, u32[]{:S(2)}, u32[]{:S(2)}) collective-permute-start(bf16[256,512]{0,1:T(8,128)(2,1)} %reduce-scatter.11.cloned.1.call-done), channel_id=1, source_target_pairs={{0,4},{4,0},{1,5},{5,1},{2,6},{6,2},{3,7},{7,3},{8,12},{12,8},{9,1... | collective-permute-start | bytes 786440 | tf_op jit(solution)/shard_map/ppermute | solution.py:311
  696.3 10.4 %collective-permute-start.6 = (bf16[256,768]{0,1:T(8,128)(2,1)}, bf16[256,768]{0,1:T(8,128)(2,1)S(1)}, u32[]{:S(2)}, u32[]{:S(2)}) collective-permute-start(bf16[256,768]{0,1:T(8,128)(2,1)} %reduce-scatter.5.cloned.1.call-done), channel_id=1, source_target_pairs={{0,4},{4,0},{1,5},{5,1},{2,6},{6,2},{3,7},{7,3},{8,12},{12,8},{9,1... | collective-permute-start | bytes 1179656 | tf_op jit(solution)/shard_map/ppermute | solution.py:311
  (32 other events, 96.2 us)
Sparse Core Ops, SparseCore 0:
  10.2 44.0 all-gather.10
  57.0 64.5 all-gather.8
  123.7 51.3 all-gather.14
  177.8 48.7 all-gather.12
  284.3 60.0 reduce-scatter.6
  349.2 71.9 reduce-scatter.8
  423.3 53.4 all-gather.16
  479.0 53.5 all-gather.18
  536.5 71.0 reduce-scatter.10
  611.9 84.2 reduce-scatter.4

commit v2 on v1

v2 whole, which is shorter than its diff:
```python
import jax
import jax.numpy as jnp
from jax import lax
from jax.experimental import pallas as pl
from jax.experimental.pallas import tpu as pltpu
from jax.sharding import PartitionSpec as P

HEAD = 64
EPSILON = 1e-06
F32 = jnp.float32
LOW = jnp.bfloat16

NN = (((1,), (0,)), ((), ()))
NT = (((1,), (1,)), ((), ()))
TN = (((0,), (0,)), ((), ()))


def mm(left, right, dims=NN):
    return lax.dot_general(left, right, dims, preferred_element_type=F32)


def whole(*shape):
    return pl.BlockSpec(shape, lambda t, _: (0,) * len(shape))


def part(*shape):
    return pl.BlockSpec((1,) + shape, lambda t, _: (t,) + (0,) * len(shape))


def columns(rows, width, at):
    return pl.BlockSpec((1, rows, width), lambda t, _: (t, 0, at))


def call(body, grid, where, ins, outs, args, scratch=(), flops=0, moved=0, exps=0):
    return pl.pallas_call(
        body,
        grid_spec=pltpu.PrefetchScalarGridSpec(
            num_scalar_prefetch=1,
            grid=(grid,),
            in_specs=ins,
            out_specs=[spec for spec, _, _ in outs],
            scratch_shapes=list(scratch),
        ),
        out_shape=[jax.ShapeDtypeStruct(shape, kind) for _, shape, kind in outs],
        compiler_params=pltpu.CompilerParams(
            dimension_semantics=("arbitrary",), vmem_limit_bytes=48 << 20
        ),
        cost_estimate=pl.CostEstimate(flops=flops, bytes_accessed=moved, transcendentals=exps),
    )(where, *args)


def layer_norm(values, gain, shift):
    center = values - jnp.mean(values, axis=-1, keepdims=True)
    spread = jnp.mean(center * center, axis=-1, keepdims=True)
    return center * lax.rsqrt(spread + EPSILON) * gain + shift


def layer_norm_back(values, gain, grad):
    center = values - jnp.mean(values, axis=-1, keepdims=True)
    scale = lax.rsqrt(jnp.mean(center * center, axis=-1, keepdims=True) + EPSILON)
    unit = center * scale
    scaled = grad * gain
    back = scale * (
        scaled
        - jnp.mean(scaled, axis=-1, keepdims=True)
        - unit * jnp.mean(scaled * unit, axis=-1, keepdims=True)
    )
    return back, row_sum(grad * unit), row_sum(grad)


def row_sum(values):
    return jnp.sum(values, axis=0, keepdims=True)


def shards_body(where_ref, qkv_ref, out_ref, up_ref, down_ref, a_ref, f_ref):
    width = qkv_ref.shape[2]
    hidden = up_ref.shape[1]
    for piece in range(3):
        a_ref[:, piece * width : (piece + 1) * width] = qkv_ref[:, piece, :].astype(LOW)
    a_ref[:, 3 * width :] = out_ref[...].T.astype(LOW)
    f_ref[:, :hidden] = up_ref[...].astype(LOW)
    f_ref[:, hidden:] = down_ref[...].T.astype(LOW)


def shards(where, w_qkv, w_out, w_up, w_down):
    rows, _, width = w_qkv.shape
    hidden = w_up.shape[1] // 2
    return call(
        shards_body,
        1,
        where,
        [
            whole(rows, 3, width),
            whole(width, rows),
            pl.BlockSpec((rows, hidden), lambda t, at: (0, at[0])),
            pl.BlockSpec((hidden, rows), lambda t, at: (at[0], 0)),
        ],
        [
            (whole(rows, 4 * width), (rows, 4 * width), LOW),
            (whole(rows, 2 * hidden), (rows, 2 * hidden), LOW),
        ],
        (w_qkv, w_out, w_up, w_down),
        moved=6 * rows * (4 * width + 2 * hidden),
    )


def attention_body(
    where_ref,
    own_ref,
    far_ref,
    w_ref,
    wo_ref,
    b_ref,
    keep_ref,
    bo_ref,
    g1_ref,
    s1_ref,
    g2_ref,
    s2_ref,
    n1_ref,
    p_ref,
    o_ref,
    l_ref,
    y_ref,
    n2_ref,
):
    width = o_ref.shape[2]
    half = own_ref.shape[0]
    step = pl.program_id(0)

    @pl.when(step == 0)
    def _():
        for at, ref in ((0, own_ref), (half, far_ref)):
            tokens = ref[...].astype(F32)
            n1_ref[at : at + half] = layer_norm(tokens, g1_ref[...], s1_ref[...]).astype(LOW)
            y_ref[at : at + half] = tokens + bo_ref[...]

    low = (mm(n1_ref[...], w_ref[0]) + b_ref[0]).astype(LOW)
    p_ref[0] = low
    keep = keep_ref[...] > 0
    for head in range(width // HEAD):
        at = head * HEAD
        query = low[:, at : at + HEAD]
        key = low[:, width + at : width + at + HEAD]
        value = low[:, 2 * width + at : 2 * width + at + HEAD]
        scores = jnp.where(keep, mm(key, query, NT) * HEAD**-0.5, -1e30)
        top = jnp.max(scores, axis=0, keepdims=True)
        exponent = jnp.exp(scores - top)
        total = jnp.sum(exponent, axis=0, keepdims=True)
        probability = (exponent * (1.0 / total)).astype(LOW)
        o_ref[0, :, at : at + HEAD] = mm(probability, value, TN).astype(LOW)
        l_ref[0, head : head + 1, :] = top + jnp.log(total)
    y_ref[...] += mm(o_ref[0], wo_ref[0], NT)

    @pl.when(step == pl.num_programs(0) - 1)
    def _():
        n2_ref[...] = layer_norm(y_ref[...], g2_ref[...], s2_ref[...]).astype(LOW)


def attention(where, own, far, weights, bias, keep, b_out, norms):
    parts, wide, width4 = weights.shape
    width = width4 // 4
    half = own.shape[0]
    rows = 2 * half
    heads = width // HEAD
    return call(
        attention_body,
        parts,
        where,
        [
            whole(half, wide),
            whole(half, wide),
            columns(wide, 3 * width, 0),
            columns(wide, width, 3),
            part(1, 3 * width),
            whole(rows, 1),
        ]
        + [whole(1, wide)] * 5,
        [
            (whole(rows, wide), (rows, wide), LOW),
            (part(rows, 3 * width), (parts, rows, 3 * width), LOW),
            (part(rows, width), (parts, rows, width), LOW),
            (part(heads, rows), (parts, heads, rows), F32),
            (whole(rows, wide), (rows, wide), F32),
            (whole(rows, wide), (rows, wide), LOW),
        ],
        (own, far, weights, weights, bias, keep, b_out, *norms),
        flops=2 * parts * rows * wide * width4 + 4 * parts * rows * rows * width,
        moved=2 * weights.size + 12 * rows * wide,
        exps=parts * heads * rows * rows,
    )


def up_body(where_ref, own_ref, far_ref, w_ref, b_ref, a_ref, s_ref, both_ref):
    half = own_ref.shape[0]

    @pl.when(pl.program_id(0) == 0)
    def _():
        both_ref[:half] = own_ref[...]
        both_ref[half:] = far_ref[...]

    hidden = mm(both_ref[...], w_ref[0]) + b_ref[0]
    bell = 0.5 * (1.0 + lax.erf(hidden * 0.5**0.5))
    a_ref[0] = (hidden * bell).astype(LOW)
    slope = bell + hidden * jnp.exp(hidden * hidden * -0.5) * 0.3989422804014327
    s_ref[0] = slope.astype(LOW)


def up_product(where, own, far, weights, bias):
    parts, wide, width2 = weights.shape
    width = width2 // 2
    rows = 2 * own.shape[0]
    shape = (parts, rows, width)
    return call(
        up_body,
        parts,
        where,
        [
            whole(rows // 2, wide),
            whole(rows // 2, wide),
            columns(wide, width, 0),
            part(1, width),
        ],
        [(part(rows, width), shape, LOW), (part(rows, width), shape, LOW)],
        (own, far, weights, bias),
        [pltpu.VMEM((rows, wide), LOW)],
        flops=2 * parts * rows * wide * width,
        moved=weights.size + 4 * parts * rows * width,
        exps=2 * parts * rows * width,
    )


def down_body(
    where_ref,
    a_ref,
    wd_ref,
    g_ref,
    s_ref,
    wu_ref,
    y_ref,
    du_ref,
    db_ref,
    keep_ref,
    send_ref,
    dn_keep_ref,
    dn_send_ref,
    r_ref,
    dn_ref,
):
    step = pl.program_id(0)
    rows = y_ref.shape[0]
    half = rows // 2
    low = (mm(g_ref[...], wd_ref[0]) * s_ref[0].astype(F32)).astype(LOW)
    du_ref[0] = low
    db_ref[0] = row_sum(low.astype(F32))
    branch = mm(a_ref[0], wd_ref[0], NT)
    grad_normed = mm(low, wu_ref[0], NT)

    @pl.when(step == 0)
    def _():
        r_ref[...] = branch
        dn_ref[...] = grad_normed

    @pl.when(step > 0)
    def _():
        r_ref[...] += branch
        dn_ref[...] += grad_normed

    @pl.when(step == pl.num_programs(0) - 1)
    def _():
        keep_ref[:half] = y_ref[:half] + r_ref[:half]
        keep_ref[half:] = r_ref[rows + half :]
        send_ref[:half] = (y_ref[half:] + r_ref[half:rows]).astype(LOW)
        send_ref[half:] = r_ref[rows : rows + half].astype(LOW)
        dn_keep_ref[...] = dn_ref[:rows]
        dn_send_ref[...] = dn_ref[rows:].astype(LOW)


def down_product(where, active, weights, grad, slope, residual):
    parts, rows, width = active.shape
    wide = weights.shape[1]
    mine = rows // 2
    return call(
        down_body,
        parts,
        where,
        [
            part(rows, width),
            columns(wide, width, 1),
            whole(rows, wide),
            part(rows, width),
            columns(wide, width, 0),
            whole(mine, wide),
        ],
        [
            (part(rows, width), (parts, rows, width), LOW),
            (part(1, width), (parts, 1, width), F32),
            (whole(mine, wide), (mine, wide), F32),
            (whole(mine, wide), (mine, wide), LOW),
            (whole(mine, wide), (mine, wide), F32),
            (whole(mine, wide), (mine, wide), LOW),
        ],
        (active, weights, grad, slope, weights, residual),
        [pltpu.VMEM((rows, wide), F32), pltpu.VMEM((rows, wide), F32)],
        flops=6 * parts * rows * width * wide,
        moved=2 * weights.size + 6 * parts * rows * width + 8 * rows * wide,
    )


def weight_body(where_ref, xa_ref, xb_ref, z_ref, ya_ref, yb_ref, *rest):
    *outs, turned_ref, second_ref = rest
    near = xa_ref.shape[0]

    @pl.when(pl.program_id(0) == 0)
    def _():
        turned_ref[:, :near] = xa_ref[...].T
        if xb_ref.shape[0] == near:
            turned_ref[:, near:] = xb_ref[...].T
        second_ref[...] = z_ref[...].T

    at = ya_ref.shape[2]
    if len(outs) == 1:
        used = ya_ref.shape[1]
        outs[0][0, :, :at] = mm(turned_ref[:, :used], ya_ref[0]).astype(LOW)
        outs[0][0, :, at:] = mm(second_ref[...], yb_ref[0]).astype(LOW)
        return
    core, row = where_ref[1], where_ref[2]
    rows = outs[0].shape[2]
    used = ya_ref.shape[1]
    for which, out_ref in enumerate(outs):
        for far in range(2):
            owner = 2 * (row + far - 2 * row * far) + (core + which - 2 * core * which)
            span = pl.ds(pl.multiple_of(owner * rows, rows), rows)
            out_ref[far, 0, :, :at] = mm(turned_ref[span, :used], ya_ref[0]).astype(LOW)
            out_ref[far, 0, :, at:] = mm(second_ref[span, :], yb_ref[0]).astype(LOW)


def weight_product(where, first, second, left, right, owners):
    parts, rows, width = left.shape
    other = right.shape[2]
    wide = second.shape[1]
    xa, xb = first if len(first) == 2 else (first[0], jnp.zeros((8, wide), LOW))
    total = width + other
    if owners == 4:
        block = pl.BlockSpec(
            (2, 1, wide // 4, total), lambda t, at: (0, lax.rem(t - at[3] + parts, parts), 0, 0)
        )
        outs = [(block, (2, parts, wide // 4, total), LOW)] * 2
    else:
        outs = [(part(wide, total), (parts, wide, total), LOW)]
    return call(
        weight_body,
        parts,
        where,
        [
            whole(*xa.shape),
            whole(*xb.shape),
            whole(*second.shape),
            part(rows, width),
            part(right.shape[1], other),
        ],
        outs,
        (xa, xb, second, left, right),
        [pltpu.VMEM((wide, rows), LOW), pltpu.VMEM((wide, second.shape[0]), LOW)],
        flops=2 * parts * wide * (rows * width + right.shape[1] * other),
        moved=2 * parts * wide * total + 4 * parts * rows * total,
    )


def back_body(
    where_ref,
    y_ref,
    dn_keep_ref,
    dn_came_ref,
    gm_ref,
    g2_ref,
    wo_ref,
    p_ref,
    l_ref,
    keep_ref,
    w_ref,
    own_ref,
    far_ref,
    g1_ref,
    dyb_ref,
    dp_ref,
    db_ref,
    sums_ref,
    gi_own_ref,
    gi_far_ref,
    dy_ref,
    dn_ref,
):
    width = wo_ref.shape[2]
    step = pl.program_id(0)
    half = own_ref.shape[0]

    @pl.when(step == 0)
    def _():
        grad_normed = dn_keep_ref[...] + dn_came_ref[...].astype(F32)
        back, gain_sum, shift_sum = layer_norm_back(y_ref[...], g2_ref[...], grad_normed)
        grad_out = gm_ref[...].astype(F32)
        grad_residual = grad_out + back
        dy_ref[...] = grad_residual
        dyb_ref[...] = grad_residual.astype(LOW)
        sums_ref[0:1] = row_sum(dyb_ref[...].astype(F32))
        sums_ref[1:2] = row_sum(grad_out)
        sums_ref[2:3] = gain_sum
        sums_ref[3:4] = shift_sum
        dn_ref[...] = jnp.zeros_like(dn_ref)

    grad_mixed = mm(dyb_ref[...], wo_ref[0]).astype(LOW)
    keep = keep_ref[...] > 0
    for head in range(width // HEAD):
        at = head * HEAD
        query = p_ref[0, :, at : at + HEAD]
        key = p_ref[0, :, width + at : width + at + HEAD]
        value = p_ref[0, :, 2 * width + at : 2 * width + at + HEAD]
        grad = grad_mixed[:, at : at + HEAD]
        scores = jnp.where(keep, mm(key, query, NT) * HEAD**-0.5, -1e30)
        probability = jnp.exp(scores - l_ref[0, head : head + 1, :])
        grad_probability = mm(value, grad, NT)
        grad_value = mm(probability.astype(LOW), grad)
        inner = jnp.sum(grad_probability * probability, axis=0, keepdims=True)
        grad_scores = (probability * (grad_probability - inner)).astype(LOW)
        grad_query = mm(grad_scores, key, TN) * HEAD**-0.5
        grad_key = mm(grad_scores, query) * HEAD**-0.5
        dp_ref[0, :, at : at + HEAD] = grad_query.astype(LOW)
        dp_ref[0, :, width + at : width + at + HEAD] = grad_key.astype(LOW)
        dp_ref[0, :, 2 * width + at : 2 * width + at + HEAD] = grad_value.astype(LOW)
    db_ref[0] = row_sum(dp_ref[0].astype(F32))
    dn_ref[...] += mm(dp_ref[0], w_ref[0], NT)

    @pl.when(step == pl.num_programs(0) - 1)
    def _():
        gain_sum = shift_sum = 0.0
        for at, ref, out_ref in ((0, own_ref, gi_own_ref), (half, far_ref, gi_far_ref)):
            back, gain_add, shift_add = layer_norm_back(
                ref[...].astype(F32), g1_ref[...], dn_ref[at : at + half]
            )
            out_ref[...] = (dy_ref[at : at + half] + back).astype(LOW)
            gain_sum, shift_sum = gain_sum + gain_add, shift_sum + shift_add
        sums_ref[4:5] = gain_sum
        sums_ref[5:6] = shift_sum
        sums_ref[6:8] = jnp.zeros((2, sums_ref.shape[1]), F32)


def attention_back(
    where, residual, dn_keep, dn_came, grad, gain_two, weights, projected, logs, keep, own, far, gain
):
    parts, wide, width4 = weights.shape
    width = width4 // 4
    half = own.shape[0]
    rows = 2 * half
    heads = width // HEAD
    return call(
        back_body,
        parts,
        where,
        [
            whole(rows, wide),
            whole(rows, wide),
            whole(rows, wide),
            whole(rows, wide),
            whole(1, wide),
            columns(wide, width, 3),
            part(rows, 3 * width),
            part(heads, rows),
            whole(rows, 1),
            columns(wide, 3 * width, 0),
            whole(half, wide),
            whole(half, wide),
            whole(1, wide),
        ],
        [
            (whole(rows, wide), (rows, wide), LOW),
            (part(rows, 3 * width), (parts, rows, 3 * width), LOW),
            (part(1, 3 * width), (parts, 1, 3 * width), F32),
            (whole(8, wide), (8, wide), F32),
            (whole(half, wide), (half, wide), LOW),
            (whole(half, wide), (half, wide), LOW),
        ],
        (
            residual,
            dn_keep,
            dn_came,
            grad,
            gain_two,
            weights,
            projected,
            logs,
            keep,
            weights,
            own,
            far,
            gain,
        ),
        [pltpu.VMEM((rows, wide), F32), pltpu.VMEM((rows, wide), F32)],
        flops=2 * parts * rows * wide * width4 + 10 * parts * rows * rows * width,
        moved=2 * weights.size + 16 * parts * rows * width + 16 * rows * wide,
        exps=parts * heads * rows * rows,
    )


def on_device(
    inputs,
    cotangent,
    visible,
    w_qkv,
    b_qv,
    w_out,
    b_out,
    w_up,
    b_up,
    w_down,
    b_down,
    gain_one,
    shift_one,
    gain_two,
    shift_two,
):
    images, half, wide = inputs.shape
    ctx_at, tp_at, fsdp_at = (lax.axis_index(name) for name in ("ctx", "tp", "fsdp"))
    blocks, parts, owners = (lax.axis_size(name) for name in ("ctx", "tp", "fsdp"))
    assert blocks == 2 and images == blocks * parts
    first = blocks * tp_at
    mine, other = first + ctx_at, first + 1 - ctx_at
    where = jnp.stack([ctx_at, fsdp_at % 2, fsdp_at // 2, tp_at]).astype(jnp.int32)
    heads_width = w_qkv.shape[2]
    hidden_half = w_up.shape[1] // 2
    rows = 2 * half

    def swap(values):
        return lax.ppermute(values, "ctx", [(0, 1), (1, 0)])

    def pick(values, index):
        return lax.dynamic_index_in_dim(values, index, 0, keepdims=False)

    def in_order(own, received):
        return jnp.where(ctx_at == 0, own, received), jnp.where(ctx_at == 0, received, own)

    def gather(shard):
        full = lax.all_gather(shard, ("tp", "fsdp"), axis=0, tiled=True)
        return full.reshape(parts, wide, shard.shape[1])

    attention_shard, forward_shard = shards(where, w_qkv, w_out, w_up, w_down)
    attention_w = gather(attention_shard)
    attention_w, forward_shard = lax.optimization_barrier((attention_w, forward_shard))
    forward_w = gather(forward_shard)
    biases = lax.all_gather(jnp.concatenate([b_qv.reshape(-1), b_up]), "tp", axis=0)
    bias_q, bias_v = biases[:, :heads_width], biases[:, heads_width : 2 * heads_width]
    qkv_bias = jnp.concatenate([bias_q, jnp.zeros_like(bias_q), bias_v], axis=1)[:, None]
    up_bias = lax.dynamic_slice_in_dim(
        biases, 2 * heads_width + ctx_at * hidden_half, hidden_half, 1
    )[:, None]

    own = pick(inputs, mine)
    far = swap(pick(inputs, other))
    cot_pair = jnp.stack([pick(cotangent, mine), pick(cotangent, other)])
    cot_swapped = swap(cot_pair)
    mine_seen = pick(visible, mine).reshape(blocks, half)
    other_seen = pick(visible, other).reshape(blocks, half)
    keep = jnp.concatenate([pick(mine_seen, ctx_at), pick(mine_seen, 1 - ctx_at)])
    keep_other = jnp.concatenate([pick(other_seen, 1 - ctx_at), pick(other_seen, ctx_at)])
    keep, keep_other = keep[:, None], keep_other[:, None]
    keep_all = jnp.concatenate([keep, keep_other]).astype(LOW)
    grad_low = (
        jnp.concatenate([cot_pair[0], cot_swapped[1], cot_swapped[0], cot_pair[1]]) * keep_all
    )

    norms = (gain_one[None], shift_one[None], gain_two[None], shift_two[None])
    normed, projected, mixed, logs, residual, normed_two = attention(
        where, own, far, attention_w, qkv_bias, keep, b_out[None], norms
    )
    normed_far = swap(normed_two)
    active, slope = up_product(where, normed_two, normed_far, forward_w, up_bias)
    grad_hidden, up_bias_grad, out_keep, out_send, dn_keep, dn_send = down_product(
        where, active, forward_w, grad_low, slope, residual
    )
    dn_came = swap(dn_send)
    forward_grads = weight_product(
        where, (normed_two, normed_far), grad_low, grad_hidden, active, owners
    )

    out_came = swap(out_send).astype(F32)
    seen = jnp.concatenate([keep[:half], keep_other[half:]]).astype(F32)
    out_rows = out_keep + jnp.concatenate([out_came[half:], out_came[:half]]) + b_down
    out_rows = (out_rows * seen).astype(LOW)
    out_pair = jnp.stack(in_order(out_rows[:half], out_rows[half:]))
    result = lax.all_gather(out_pair, "tp", axis=0, tiled=True).astype(F32)

    grad_attended, grad_projected, qkv_bias_grad, sums, gi_own, gi_far = attention_back(
        where,
        residual,
        dn_keep,
        dn_came,
        grad_low[:rows],
        gain_two[None],
        attention_w,
        projected,
        logs,
        keep,
        own,
        far,
        gain_one[None],
    )
    grad_in_pair = jnp.stack(in_order(gi_own, swap(gi_far)))
    grad_inputs = lax.all_gather(grad_in_pair, "tp", axis=0, tiled=True).astype(F32)
    attention_grads = weight_product(
        where, (normed,), grad_attended, grad_projected, mixed, owners
    )

    def scatter(grads):
        if len(grads) == 1:
            flat = grads[0].reshape(-1, grads[0].shape[2])
            return lax.psum_scatter(flat, ("tp", "fsdp"), scatter_dimension=0, tiled=True)
        keep, send = grads
        came = lax.ppermute(send, "fsdp", [(0, 1), (1, 0), (2, 3), (3, 2)])
        lift = (keep[1].astype(F32) + came[1].astype(F32)).astype(LOW)
        lift = lax.ppermute(lift, "fsdp", [(0, 2), (2, 0), (1, 3), (3, 1)])

        def own_part(at):
            return keep[0, at].astype(F32) + came[0, at].astype(F32) + lift[at].astype(F32)

        total = own_part(parts - 1)
        for at in range(parts - 2, -1, -1):
            moved = lax.ppermute(
                total.astype(LOW), "tp", [(i, (i + 1) % parts) for i in range(parts)]
            )
            total = own_part(at) + moved.astype(F32)
        return total.astype(LOW)

    forward_own = scatter(forward_grads)
    forward_far = swap(forward_own)
    up_total = jnp.concatenate(
        in_order(forward_own[:, :hidden_half], forward_far[:, :hidden_half]), axis=1
    ).astype(F32)
    down_total = jnp.concatenate(
        in_order(forward_own[:, hidden_half:], forward_far[:, hidden_half:]), axis=1
    ).astype(F32)
    attention_own = scatter(attention_grads)
    attention_total = attention_own.astype(F32) + swap(attention_own).astype(F32)

    up_bias_slot = lax.dynamic_update_slice(
        jnp.zeros((parts, 2, hidden_half), F32), up_bias_grad, (0, ctx_at, 0)
    )
    small = jnp.concatenate(
        [
            sums[:6],
            up_bias_slot.reshape(-1, wide),
            qkv_bias_grad.reshape(-1, wide),
        ]
    )
    if owners == 4 and parts == 4:
        for axis, pairs in (
            ("fsdp", [(0, 1), (1, 0), (2, 3), (3, 2)]),
            ("fsdp", [(0, 2), (2, 0), (1, 3), (3, 1)]),
            ("ctx", [(0, 1), (1, 0)]),
            ("tp", [(0, 1), (1, 0), (2, 3), (3, 2)]),
            ("tp", [(0, 2), (2, 0), (1, 3), (3, 1)]),
        ):
            small = small + lax.ppermute(small, axis, pairs)
    else:
        small = lax.psum(small, ("fsdp", "ctx", "tp"))
    up_rows = parts * 2 * hidden_half // wide
    up_small = small[6 : 6 + up_rows].reshape(parts, 2 * hidden_half)
    qkv_small = small[6 + up_rows :].reshape(parts, 3, heads_width)
    return (
        result,
        grad_inputs,
        attention_total[:, : 3 * heads_width].reshape(-1, 3, heads_width),
        pick(qkv_small, tp_at)[0::2],
        attention_total[:, 3 * heads_width :].T,
        small[0],
        up_total,
        pick(up_small, tp_at),
        down_total.T,
        small[1],
        small[4],
        small[5],
        small[2],
        small[3],
    )


def solution(mesh):
    placed = (
        P("fsdp", "ctx", None),
        P("fsdp", "ctx", None),
        P("fsdp", None),
        P("fsdp", None, "tp"),
        P(None, "tp"),
        P("tp", "fsdp"),
        P(),
        P("fsdp", "tp"),
        P("tp"),
        P("tp", "fsdp"),
        P(),
        P(),
        P(),
        P(),
        P(),
    )
    return jax.shard_map(
        on_device,
        mesh=mesh,
        in_specs=placed,
        out_specs=(
            P("fsdp", "ctx", None),
            P("fsdp", "ctx", None),
            P("fsdp", None, "tp"),
            P(None, "tp"),
            P("tp", "fsdp"),
            P(),
            P("fsdp", "tp"),
            P("tp"),
            P("tp", "fsdp"),
            P(),
            P(),
            P(),
            P(),
            P(),
        ),
        check_vma=False,
    )
```

time: 717 us -> 450 us (0.63)
  waiting for transfers between devices: 416 us -> 261 us
  local copies, waits for them, and re-layouts: 106 us -> 24.5 us
  blocking collectives: 54.4 us -> 13.5 us
  Pallas kernels: 68.6 us -> 78.6 us
    reduce_scatter x4 -> x0, waiting for transfers between devices: 157 us -> none  [scatter(): return lax.psum_scatter(flat, spread_axes, scatter_dimension=0, tiled=True)]
    ppermute x0 -> x15, waiting for transfers between devices: none -> 130 us  [the longest x2 74.3 us: scatter(): lift = lax.ppermute(lift, 'fsdp', [(0, 2), (2, 0), (1, 3), (3, 1)])]
    all_gather x1, waiting for transfers between devices: 51 us -> 0.01 us  [on_device(): lax.all_gather(grad_in_pair, 'tp', axis=0, tiled=True).astype(F32)]
    psum x1 -> x0, blocking collectives: 40.6 us -> none  [on_device(): lax.psum((qkv_bias_grad[:, 0::2], up_bias_slot, jnp.sum(grad_attended.ast...]
    all_gather x1, waiting for transfers between devices: 32.3 us -> 0.01 us  [on_device(): result = lax.all_gather(out_pair, 'tp', axis=0, tiled=True).astype(F32)]
    all_gather x4 -> x2, waiting for transfers between devices: 134 us -> 103 us  [gather(): full = lax.all_gather(shard, ('tp', 'fsdp'), axis=0, tiled=True)]
    reshape x4 -> x2, local copies, waits for them, and re-layouts: 24.5 us -> 0.04 us  [the longest x1 0.02 us: on_device(): qkv_small = small[6 + up_rows:].reshape(parts, 3, heads_width)]
    all_gather x3 -> x0, local copies, waits for them, and re-layouts: 18.3 us -> none  [gather(): full = lax.all_gather(shard, spread_axes, axis=0, tiled=True)]
  transfers between devices with their start and end apart: 20 -> 27, of which waited for: 13 -> 14; matrix products, arithmetic and copies ran while one was open for 16% -> 10% of each run, Pallas kernels for 6% -> 12%
where the time goes in v2:
time: 450 us; the launch traced here: 449 us
  waiting for transfers between devices  261 us (58%)
  Pallas kernels  78.6 us (17%)
  other arithmetic  37.6 us (8%)
  local copies, waits for them, and re-layouts  24.5 us (5%)
  starting transfers between devices  18.8 us (4%)
  between operations  14.4 us (3%)
  blocking collectives  13.5 us (3%)
    all_gather x2, waiting for transfers between devices, gather(): full = lax.all_gather(shard, ('tp', 'fsdp'), axis=0, tiled=True)  103 us
    pallas_call x7, Pallas kernels, call(): pl.pallas_call(body, grid_spec=pltpu.PrefetchScalarGridSpec(num_scalar_pr...  78.6 us
    ppermute x2, waiting for transfers between devices, scatter(): lift = lax.ppermute(lift, 'fsdp', [(0, 2), (2, 0), (1, 3), (3, 1)])  74.3 us
    ppermute x5, waiting for transfers between devices, on_device(): small = small + lax.ppermute(small, axis, pairs)  30.3 us
    ppermute x8, waiting for transfers between devices, swap(): return lax.ppermute(values, 'ctx', [(0, 1), (1, 0)])  27.8 us
    ppermute x6, waiting for transfers between devices, scatter(): lax.ppermute(total.astype(LOW), 'tp', [(i, (i + 1) % parts) for i in rang...  25.8 us
    unnamed x62, local copies, waits for them, and re-layouts  16.5 us
    all_gather x1, blocking collectives, on_device(): lax.all_gather(jnp.concatenate([b_qv.reshape(-1), b_up]), 'tp', axis=0)  13.5 us
  transfers between devices with their start and end apart: 27, of which 14 were waited for; matrix products, arithmetic and copies ran while one was open for 10% of the time, Pallas kernels for 12%

profile of v2, /device:TPU:0, one launch (start us, length us, event | category | flops | bytes accessed | tf_op | source)
XLA Modules:
  0.0 448.6 jit_solution(7452863335331487756)
XLA Ops:
  12.4 3.2 shard_map.254
  15.7 77.7 %all-gather.7.cloned.1.call-done = bf16[4096,1024]{1,0:T(8,128)(2,1)} async-done(((bf16[256,1024]{1,0:T(8,128)(2,1)}), bf16[4096,1024]{1,0:T(8,128)(2,1)}) %all-gather.7.cloned.1.call-update) | async-done | bytes 8388624 | tf_op jit(solution)/shard_map/all_gather | solution.py:543
  99.8 13.5 %all-gather.1 = f32[4,1,1536]{2,1,0:T(1,128)S(1)} all-gather(f32[1,1,1536]{2,1,0:T(1,128)S(1)} %reshape.172), channel_id=2, replica_groups=mesh['fsdp'=4,'ctx'=2,'tp'=4] {'tp'}, dimensions={0}, use_global_device_ids=true | all-gather | bytes 30720 | tf_op jit(solution)/shard_map/all_gather | solution.py:550
  113.7 14.0 %shard_map.255 = (bf16[320,1024]{1,0:T(8,128)(2,1)S(1)}, bf16[4,320,768]{2,1,0:T(8,128)(2,1)S(1)}, bf16[4,320,256]{2,1,0:T(8,128)(2,1)S(1)}, f32[4,4,320]{2,1,0:...) custom-call(s32[4]{0:T(128)S(1)} %pad_add_fusion.2.where_ref, ...), custom_call_target="tpu_custom_call" | custom-call | flops 3103784960 | bytes 12320768 | tf_op jit(solution)/shard_map/pallas_call | solution.py:35
  134.8 9.6 %collective-permute-done.1.far_ref.xb_ref = bf16[320,1024]{1,0:T(8,128)(2,1)} collective-permute-done((bf16[320,1024]{1,0:T(8,128)(2,1)S(1)}, bf16[320,1024]{1,0:T(8,128)(2,1)}, u32[]{:S(2)}, u32[]{:S(2)}) %collective-permute-start.1) | collective-permute-done | bytes 655392 | tf_op jit(solution)/shard_map/ppermute | solution.py:534
  144.4 25.1 %all-gather.9.cloned.1.call-done = bf16[4096,1024]{1,0:T(8,128)(2,1)} async-done(((bf16[256,1024]{1,0:T(8,128)(2,1)}), bf16[4096,1024]{1,0:T(8,128)(2,1)}) %all-gather.9.cloned.1.call-update) | async-done | bytes 8388624 | tf_op jit(solution)/shard_map/all_gather | solution.py:543
  169.6 8.3 %shard_map.256 = (bf16[4,640,512]{2,1,0:T(8,128)(2,1)S(1)}, bf16[4,640,512]{2,1,0:T(8,128)(2,1)}) custom-call(s32[4]{0:T(128)S(1)} %pad_add_fusion.2.where_ref, bf16[320,1024]{1,0:T(8,128)(2,1)S(1)} %get-tuple-element.45.own_ref.xa_ref, bf16[320,1024]{1,0:T(8,128)(2,1)} %collective-permute-done.1.far_ref.xb_ref, bf16[4,1024,1024]{2,1,0:T(8,128)(2,1)} %bitcast.149, ...), custom_call_target="tpu_custom_call" | custom-call | flops 2684354560 | bytes 9437184 | tf_op jit(solution)/shard_map/pallas_call | solution.py:35
  179.3 15.5 %shard_map.257 = (bf16[4,640,512]{2,1,0:T(8,128)(2,1)}, f32[4,1,512]{2,1,0:T(1,128)S(1)}, f32[320,1024]{1,0:T(8,128)S(1)}, bf16[320,1024]{1,0:T(8,128)(2,1)}, f3...) custom-call(s32[4]{0:T(128)S(1)} %pad_add_fusion.2.where_ref, bf16[4,640,512]{2,1,0:T(8,128)(2,1)} %copy-done.20, ...), custom_call_target="tpu_custom_call" | custom-call | flops 8053063680 | bytes 21495808 | tf_op jit(solution)/shard_map/pallas_call | solution.py:35
  196.3 1.7 copy-done.21
  198.0 11.7 %shard_map.260 = (bf16[2,4,256,1024]{3,2,1,0:T(8,128)(2,1)}, bf16[2,4,256,1024]{3,2,1,0:T(8,128)(2,1)}) custom-call(s32[4]{0:T(128)S(1)} %pad_add_fusion.2.where_ref, bf16[320,1024]{1,0:T(8,128)(2,1)S(1)} %copy-done.17, bf16[320,1024]{1,0:T(8,128)(2,1)} %collective-permute-done.1.far_ref.xb_ref, bf16[640,1024]{1,0:T(8,128)(2,1)S(1)} %maximum_multiply_fusion.g_ref.z_ref, ...), custom_call_target="tpu_custom_call" | custom-call | flops 5368709120 | bytes 18874368 | tf_op jit(solution)/shard_map/pallas_call | solution.py:35
  211.7 18.4 %shard_map.258 = (bf16[320,1024]{1,0:T(8,128)(2,1)S(1)}, bf16[4,320,768]{2,1,0:T(8,128)(2,1)}, f32[4,1,768]{2,1,0:T(1,128)S(1)}, f32[8,1024]{1,0:T(8,128)S(1)}, ...) custom-call(s32[4]{0:T(128)S(1)} %pad_add_fusion.2.where_ref, f32[320,1024]{1,0:T(8,128)S(1)} %copy-done.2, ...), custom_call_target="tpu_custom_call" | custom-call | flops 3732930560 | bytes 18874368 | tf_op jit(solution)/shard_map/pallas_call | solution.py:35
  231.8 7.6 %shard_map.259 = (bf16[2,4,256,1024]{3,2,1,0:T(8,128)(2,1)}, bf16[2,4,256,1024]{3,2,1,0:T(8,128)(2,1)}) custom-call(s32[4]{0:T(128)S(1)} %pad_add_fusion.2.where_ref, bf16[320,1024]{1,0:T(8,128)(2,1)S(1)} %copy-done.13, bf16[8,1024]{1,0:T(8,128)(2,1)S(1)} %broadcast_in_dim.46.xb_ref, bf16[320,1024]{1,0:T(8,128)(2,1)S(1)} %get-tuple-element.59.z_ref, ...), custom_call_target="tpu_custom_call" | custom-call | flops 2684354560 | bytes 13631488 | tf_op jit(solution)/shard_map/pallas_call | solution.py:35
  242.0 4.8 %fusion.1 = bf16[4,256,1024]{2,1,0:T(8,128)(2,1)} fusion(bf16[2,4,256,1024]{3,2,1,0:T(8,128)(2,1)} %collective-permute-done.17, bf16[2,4,256,1024]{3,2,1,0:T(8,128)(2,1)} %get-tuple-element.68), kind=kLoop, calls=%fused_computation.3 | loop fusion | flops 4194304 | bytes 6291456 | tf_op jit(solution)/shard_map/convert_element_type | solution.py:619
  247.3 2.7 fusion
  253.1 8.1 %collective-permute-done.5 = bf16[160,1024]{1,0:T(8,128)(2,1)S(1)} collective-permute-done((bf16[160,1024]{1,0:T(8,128)(2,1)S(1)}, bf16[160,1024]{1,0:T(8,128)(2,1)S(1)}, u32[]{:S(2)}, u32[]{:S(2)}) %collective-permute-start.5) | collective-permute-done | bytes 327712 | tf_op jit(solution)/shard_map/ppermute | solution.py:534
  262.1 33.4 %collective-permute-done.18 = bf16[4,256,1024]{2,1,0:T(8,128)(2,1)} collective-permute-done((bf16[4,256,1024]{2,1,0:T(8,128)(2,1)}, bf16[4,256,1024]{2,1,0:T(8,128)(2,1)}, u32[]{:S(2)}, u32[]{:S(2)}) %collective-permute-start.18) | collective-permute-done | bytes 2097184 | tf_op jit(solution)/shard_map/ppermute | solution.py:620
  295.5 2.4 fusion.5
  299.0 41.0 %collective-permute-done.7 = bf16[4,256,1024]{2,1,0:T(8,128)(2,1)} collective-permute-done((bf16[4,256,1024]{2,1,0:T(8,128)(2,1)S(1)}, bf16[4,256,1024]{2,1,0:T(8,128)(2,1)}, u32[]{:S(2)}, u32[]{:S(2)}) %collective-permute-start.7) | collective-permute-done | bytes 2097184 | tf_op jit(solution)/shard_map/ppermute | solution.py:620
  342.6 1.7 fusion.7
  346.3 3.7 collective-permute-done.13
  351.5 15.7 %collective-permute-done.8 = bf16[256,1024]{1,0:T(8,128)(2,1)S(1)} collective-permute-done((bf16[256,1024]{1,0:T(8,128)(2,1)S(1)}, bf16[256,1024]{1,0:T(8,128)(2,1)S(1)}, u32[]{:S(2)}, u32[]{:S(2)}) %collective-permute-start.8) | collective-permute-done | bytes 524320 | tf_op jit(solution)/shard_map/ppermute | solution.py:627
  367.2 1.7 fusion.14
  369.3 9.2 %collective-permute-done.20 = bf16[256,1024]{1,0:T(8,128)(2,1)S(1)} collective-permute-done((bf16[256,1024]{1,0:T(8,128)(2,1)S(1)}, bf16[256,1024]{1,0:T(8,128)(2,1)S(1)}, u32[]{:S(2)}, u32[]{:S(2)}) %collective-permute-start.20) | collective-permute-done | bytes 524320 | tf_op jit(solution)/shard_map/ppermute | solution.py:627
  378.5 1.7 fusion.9
  380.4 21.6 %collective-permute-done.15 = f32[13,1024]{1,0:T(8,128)S(1)} collective-permute-done((f32[13,1024]{1,0:T(8,128)S(1)}, f32[13,1024]{1,0:T(8,128)S(1)}, u32[]{:S(2)}, u32[]{:S(2)}) %collective-permute-start.15) | collective-permute-done | bytes 53280 | tf_op jit(solution)/shard_map/ppermute | solution.py:662
  402.6 5.0 %collective-permute-done.16 = f32[13,1024]{1,0:T(8,128)S(1)} collective-permute-done((f32[13,1024]{1,0:T(8,128)S(1)}, f32[13,1024]{1,0:T(8,128)S(1)}, u32[]{:S(2)}, u32[]{:S(2)}) %collective-permute-start.16) | collective-permute-done | bytes 53280 | tf_op jit(solution)/shard_map/ppermute | solution.py:662
  407.7 1.7 fusion.16
  409.5 1.7 fusion.11
  414.6 4.7 %convert_element_type.221 = f32[8,160,1024]{2,1,0:T(8,128)} convert(bf16[8,160,1024]{2,1,0:T(8,128)(2,1)} %all-gather.11.cloned.1.call-done) | non-fusion elementwise | flops 1310720 | bytes 7864320 | tf_op jit(solution)/shard_map/convert_element_type | solution.py:590
  419.3 4.7 %convert_element_type.222 = f32[8,160,1024]{2,1,0:T(8,128)} convert(bf16[8,160,1024]{2,1,0:T(8,128)(2,1)} %all-gather.13.cloned.1.call-done) | non-fusion elementwise | flops 1310720 | bytes 7864320 | tf_op jit(solution)/shard_map/convert_element_type | solution.py:608
  424.9 1.7 fusion.18
  430.8 8.7 %collective-permute-done.11 = bf16[256,1024]{1,0:T(8,128)(2,1)S(1)} collective-permute-done((bf16[256,1024]{1,0:T(8,128)(2,1)S(1)}, bf16[256,1024]{1,0:T(8,128)(2,1)S(1)}, u32[]{:S(2)}, u32[]{:S(2)}) %collective-permute-start.11) | collective-permute-done | bytes 524320 | tf_op jit(solution)/shard_map/ppermute | solution.py:534
  (164 shorter events, 51.8 us)
Async XLA Ops:
  7.2 86.2 %all-gather.7.cloned.1.call-start = ((), (), s32[]{:S(2)}) async-start(), calls=%async_computation | async-start | bytes 8912896 | tf_op jit(solution)/shard_map/all_gather | solution.py:543
  15.6 98.0 %copy-start.6 = (f32[1024]{0:T(1024)S(1)}, f32[1024]{0:T(1024)}, u32[]{:S(2)}) copy-start(f32[1024]{0:T(1024)} %param.26) | copy-start | bytes 12292
  15.6 98.0 %copy-start.7 = (f32[1024]{0:T(1024)S(1)}, f32[1024]{0:T(1024)}, u32[]{:S(2)}) copy-start(f32[1024]{0:T(1024)} %param.28) | copy-start | bytes 12292
  15.6 98.0 %copy-start.8 = (f32[1024]{0:T(1024)S(1)}, f32[1024]{0:T(1024)}, u32[]{:S(2)}) copy-start(f32[1024]{0:T(1024)} %param.21) | copy-start | bytes 12292
  15.6 98.0 %copy-start.9 = (f32[1024]{0:T(1024)S(1)}, f32[1024]{0:T(1024)}, u32[]{:S(2)}) copy-start(f32[1024]{0:T(1024)} %param.27) | copy-start | bytes 12292
  15.6 98.0 %copy-start.10 = (f32[1024]{0:T(1024)S(1)}, f32[1024]{0:T(1024)}, u32[]{:S(2)}) copy-start(f32[1024]{0:T(1024)} %param.29) | copy-start | bytes 12292
  15.7 153.9 %all-gather.9.cloned.1.call-start = ((), (), s32[]{:S(2)}) async-start(), calls=%async_computation.1 | async-start | bytes 8912896 | tf_op jit(solution)/shard_map/all_gather | solution.py:543
  93.4 321.1 %all-gather.11.cloned.1.call-start = ((), (), s32[]{:S(2)}) async-start(), calls=%async_computation.2 | async-start | bytes 3276800 | tf_op jit(solution)/shard_map/all_gather | solution.py:590
  94.6 19.0 %collective-permute-start = (bf16[160,1024]{1,0:T(8,128)(2,1)S(1)}, bf16[160,1024]{1,0:T(8,128)(2,1)S(1)}, u32[]{:S(2)}, u32[]{:S(2)}) collective-permute-start(bf16[160,1024]{1,0:T(8,128)(2,1)S(1)} %get-tuple-element.116), channel_id=1, source_target_pairs={{0,4},{4,0},{1,5},{5,1},{2,6},{6,2},{3,7},{7,3},{8,12},{12,8},{9,1... | collective-permute-start | bytes 983048 | tf_op jit(solution)/shard_map/ppermute | solution.py:534
  98.2 34.2 %collective-permute-start.2 = (bf16[2,160,1024]{2,1,0:T(8,128)(2,1)}, bf16[2,160,1024]{2,1,0:T(8,128)(2,1)}, u32[]{:S(2)}, u32[]{:S(2)}) collective-permute-start(bf16[2,160,1024]{2,1,0:T(8,128)(2,1)} %pad_maximum_fusion), channel_id=1, source_target_pairs={{0,4},{4,0},{1,5},{5,1},{2,6},{6,2},{3,7},{7,3},{8,12},{12,8},{9,1... | collective-permute-start | bytes 1966088 | tf_op jit(solution)/shard_map/ppermute | solution.py:534
  130.9 13.5 %collective-permute-start.1 = (bf16[320,1024]{1,0:T(8,128)(2,1)S(1)}, bf16[320,1024]{1,0:T(8,128)(2,1)}, u32[]{:S(2)}, u32[]{:S(2)}) collective-permute-start(bf16[320,1024]{1,0:T(8,128)(2,1)S(1)} %get-tuple-element.45.own_ref.xa_ref), channel_id=1, source_target_pairs={{0,4},{4,0},{1,5},{5,1},{2,6},{6,2},{3,7},{7,3},{8,12},{12,8},{9,1... | collective-permute-start | bytes 1966088 | tf_op jit(solution)/shard_map/ppermute | solution.py:534
  194.8 16.9 %collective-permute-start.4 = (bf16[320,1024]{1,0:T(8,128)(2,1)S(1)}, bf16[320,1024]{1,0:T(8,128)(2,1)S(1)}, u32[]{:S(2)}, u32[]{:S(2)}) collective-permute-start(bf16[320,1024]{1,0:T(8,128)(2,1)S(1)} %get-tuple-element.53), channel_id=1, source_target_pairs={{0,4},{4,0},{1,5},{5,1},{2,6},{6,2},{3,7},{7,3},{8,12},{12,8},{9,1... | collective-permute-start | bytes 1966088 | tf_op jit(solution)/shard_map/ppermute | solution.py:534
  209.7 32.2 %collective-permute-start.17 = (bf16[2,4,256,1024]{3,2,1,0:T(8,128)(2,1)}, bf16[2,4,256,1024]{3,2,1,0:T(8,128)(2,1)}, u32[]{:S(2)}, u32[]{:S(2)}) collective-permute-start(bf16[2,4,256,1024]{3,2,1,0:T(8,128)(2,1)} %get-tuple-element.69), channel_id=1, source_target_pairs={{0,8},{8,0},{16,24},{24,16},{1,9},{9,1},{17,25},{25,17},{2,10},{10... | collective-permute-start | bytes 12582920 | tf_op jit(solution)/shard_map/ppermute | solution.py:618
  209.7 29.7 %collective-permute-start.3 = (bf16[320,1024]{1,0:T(8,128)(2,1)}, bf16[320,1024]{1,0:T(8,128)(2,1)}, u32[]{:S(2)}, u32[]{:S(2)}) collective-permute-start(bf16[320,1024]{1,0:T(8,128)(2,1)} %get-tuple-element.51), channel_id=1, source_target_pairs={{0,4},{4,0},{1,5},{5,1},{2,6},{6,2},{3,7},{7,3},{8,12},{12,8},{9,1... | collective-permute-start | bytes 1966088 | tf_op jit(solution)/shard_map/ppermute | solution.py:534
  239.4 7.9 %collective-permute-start.6 = (bf16[2,4,256,1024]{3,2,1,0:T(8,128)(2,1)}, bf16[2,4,256,1024]{3,2,1,0:T(8,128)(2,1)}, u32[]{:S(2)}, u32[]{:S(2)}) collective-permute-start(bf16[2,4,256,1024]{3,2,1,0:T(8,128)(2,1)} %get-tuple-element.63), channel_id=1, source_target_pairs={{0,8},{8,0},{16,24},{24,16},{1,9},{9,1},{17,25},{25,17},{2,10},{10... | collective-permute-start | bytes 12582920 | tf_op jit(solution)/shard_map/ppermute | solution.py:618
  241.9 177.4 %all-gather.13.cloned.1.call-start = ((), (), s32[]{:S(2)}) async-start(), calls=%async_computation.3 | async-start | bytes 3276800 | tf_op jit(solution)/shard_map/all_gather | solution.py:608
  246.7 48.7 %collective-permute-start.18 = (bf16[4,256,1024]{2,1,0:T(8,128)(2,1)}, bf16[4,256,1024]{2,1,0:T(8,128)(2,1)}, u32[]{:S(2)}, u32[]{:S(2)}) collective-permute-start(bf16[4,256,1024]{2,1,0:T(8,128)(2,1)} %fusion.1), channel_id=1, source_target_pairs={{0,16},{16,0},{8,24},{24,8},{1,17},{17,1},{9,25},{25,9},{2,18},{18... | collective-permute-start | bytes 6291464 | tf_op jit(solution)/shard_map/ppermute | solution.py:620
  250.0 90.0 %collective-permute-start.7 = (bf16[4,256,1024]{2,1,0:T(8,128)(2,1)S(1)}, bf16[4,256,1024]{2,1,0:T(8,128)(2,1)}, u32[]{:S(2)}, u32[]{:S(2)}) collective-permute-start(bf16[4,256,1024]{2,1,0:T(8,128)(2,1)S(1)} %fusion), channel_id=1, source_target_pairs={{0,16},{16,0},{8,24},{24,8},{1,17},{17,1},{9,25},{25,9},{2,18},{18... | collective-permute-start | bytes 6291464 | tf_op jit(solution)/shard_map/ppermute | solution.py:620
  251.6 9.5 %collective-permute-start.5 = (bf16[160,1024]{1,0:T(8,128)(2,1)S(1)}, bf16[160,1024]{1,0:T(8,128)(2,1)S(1)}, u32[]{:S(2)}, u32[]{:S(2)}) collective-permute-start(bf16[160,1024]{1,0:T(8,128)(2,1)S(1)} %copy-done.19), channel_id=1, source_target_pairs={{0,4},{4,0},{1,5},{5,1},{2,6},{6,2},{3,7},{7,3},{8,12},{12,8},{9,1... | collective-permute-start | bytes 983048 | tf_op jit(solution)/shard_map/ppermute | solution.py:534
  297.9 44.7 %collective-permute-start.19 = (bf16[256,1024]{1,0:T(8,128)(2,1)}, bf16[256,1024]{1,0:T(8,128)(2,1)S(1)}, u32[]{:S(2)}, u32[]{:S(2)}) collective-permute-start(bf16[256,1024]{1,0:T(8,128)(2,1)} %fusion.5), channel_id=1, source_target_pairs={{0,1},{1,2},{2,3},{3,0},{4,5},{5,6},{6,7},{7,4},{8,9},{9,10},{10,1... | collective-permute-start | bytes 1572872 | tf_op jit(solution)/shard_map/ppermute | solution.py:627
  298.9 46.7 %collective-permute-start.12 = (f32[13,1024]{1,0:T(8,128)S(1)}, f32[13,1024]{1,0:T(8,128)S(1)}, u32[]{:S(2)}, u32[]{:S(2)}) collective-permute-start(f32[13,1024]{1,0:T(8,128)S(1)} %pad_maximum_fusion.3), channel_id=1, source_target_pairs={{0,8},{8,0},{16,24},{24,16},{1,9},{9,1},{17,25},{25,17},{2,10},{10... | collective-permute-start | bytes 159752 | tf_op jit(solution)/shard_map/ppermute | solution.py:662
  341.7 25.6 %collective-permute-start.8 = (bf16[256,1024]{1,0:T(8,128)(2,1)S(1)}, bf16[256,1024]{1,0:T(8,128)(2,1)S(1)}, u32[]{:S(2)}, u32[]{:S(2)}) collective-permute-start(bf16[256,1024]{1,0:T(8,128)(2,1)S(1)} %fusion.12), channel_id=1, source_target_pairs={{0,1},{1,2},{2,3},{3,0},{4,5},{5,6},{6,7},{7,4},{8,9},{9,10},{10,1... | collective-permute-start | bytes 1572872 | tf_op jit(solution)/shard_map/ppermute | solution.py:627
  344.3 34.1 %collective-permute-start.20 = (bf16[256,1024]{1,0:T(8,128)(2,1)S(1)}, bf16[256,1024]{1,0:T(8,128)(2,1)S(1)}, u32[]{:S(2)}, u32[]{:S(2)}) collective-permute-start(bf16[256,1024]{1,0:T(8,128)(2,1)S(1)} %fusion.7), channel_id=1, source_target_pairs={{0,1},{1,2},{2,3},{3,0},{4,5},{5,6},{6,7},{7,4},{8,9},{9,10},{10,1... | collective-permute-start | bytes 1572872 | tf_op jit(solution)/shard_map/ppermute | solution.py:627
  345.6 4.3 collective-permute-start.13
  350.0 30.3 %collective-permute-start.14 = (f32[13,1024]{1,0:T(8,128)S(1)}, f32[13,1024]{1,0:T(8,128)S(1)}, u32[]{:S(2)}, u32[]{:S(2)}) collective-permute-start(f32[13,1024]{1,0:T(8,128)S(1)} %add.205), channel_id=1, source_target_pairs={{0,4},{4,0},{1,5},{5,1},{2,6},{6,2},{3,7},{7,3},{8,12},{12,8},{9,1... | collective-permute-start | bytes 159752 | tf_op jit(solution)/shard_map/ppermute | solution.py:662
  369.0 38.7 %collective-permute-start.9 = (bf16[256,1024]{1,0:T(8,128)(2,1)S(1)}, bf16[256,1024]{1,0:T(8,128)(2,1)S(1)}, u32[]{:S(2)}, u32[]{:S(2)}) collective-permute-start(bf16[256,1024]{1,0:T(8,128)(2,1)S(1)} %fusion.14), channel_id=1, source_target_pairs={{0,1},{1,2},{2,3},{3,0},{4,5},{5,6},{6,7},{7,4},{8,9},{9,10},{10,1... | collective-permute-start | bytes 1572872 | tf_op jit(solution)/shard_map/ppermute | solution.py:627
  380.2 29.3 %collective-permute-start.21 = (bf16[256,1024]{1,0:T(8,128)(2,1)S(1)}, bf16[256,1024]{1,0:T(8,128)(2,1)S(1)}, u32[]{:S(2)}, u32[]{:S(2)}) collective-permute-start(bf16[256,1024]{1,0:T(8,128)(2,1)S(1)} %fusion.9), channel_id=1, source_target_pairs={{0,1},{1,2},{2,3},{3,0},{4,5},{5,6},{6,7},{7,4},{8,9},{9,10},{10,1... | collective-permute-start | bytes 1572872 | tf_op jit(solution)/shard_map/ppermute | solution.py:627
  380.3 21.7 %collective-permute-start.15 = (f32[13,1024]{1,0:T(8,128)S(1)}, f32[13,1024]{1,0:T(8,128)S(1)}, u32[]{:S(2)}, u32[]{:S(2)}) collective-permute-start(f32[13,1024]{1,0:T(8,128)S(1)} %add.206), channel_id=1, source_target_pairs={{0,1},{1,0},{2,3},{3,2},{4,5},{5,4},{6,7},{7,6},{8,9},{9,8},{10,11... | collective-permute-start | bytes 159752 | tf_op jit(solution)/shard_map/ppermute | solution.py:662
  402.0 5.6 %collective-permute-start.16 = (f32[13,1024]{1,0:T(8,128)S(1)}, f32[13,1024]{1,0:T(8,128)S(1)}, u32[]{:S(2)}, u32[]{:S(2)}) collective-permute-start(f32[13,1024]{1,0:T(8,128)S(1)} %add.207), channel_id=1, source_target_pairs={{0,2},{2,0},{1,3},{3,1},{4,6},{6,4},{5,7},{7,5},{8,10},{10,8},{9,1... | collective-permute-start | bytes 159752 | tf_op jit(solution)/shard_map/ppermute | solution.py:662
  409.4 15.5 %collective-permute-start.10 = (bf16[256,1024]{1,0:T(8,128)(2,1)S(1)}, bf16[256,1024]{1,0:T(8,128)(2,1)S(1)}, u32[]{:S(2)}, u32[]{:S(2)}) collective-permute-start(bf16[256,1024]{1,0:T(8,128)(2,1)S(1)} %fusion.16), channel_id=1, source_target_pairs={{0,1},{1,2},{2,3},{3,0},{4,5},{5,6},{6,7},{7,4},{8,9},{9,10},{10,1... | collective-permute-start | bytes 1572872 | tf_op jit(solution)/shard_map/ppermute | solution.py:627
  411.2 17.0 %collective-permute-start.22 = (bf16[256,1024]{1,0:T(8,128)(2,1)S(1)}, bf16[256,1024]{1,0:T(8,128)(2,1)S(1)}, u32[]{:S(2)}, u32[]{:S(2)}) collective-permute-start(bf16[256,1024]{1,0:T(8,128)(2,1)S(1)} %fusion.11), channel_id=1, source_target_pairs={{0,4},{4,0},{1,5},{5,1},{2,6},{6,2},{3,7},{7,3},{8,12},{12,8},{9,1... | collective-permute-start | bytes 1572872 | tf_op jit(solution)/shard_map/ppermute | solution.py:534
  426.7 12.9 %collective-permute-start.11 = (bf16[256,1024]{1,0:T(8,128)(2,1)S(1)}, bf16[256,1024]{1,0:T(8,128)(2,1)S(1)}, u32[]{:S(2)}, u32[]{:S(2)}) collective-permute-start(bf16[256,1024]{1,0:T(8,128)(2,1)S(1)} %fusion.18), channel_id=1, source_target_pairs={{0,4},{4,0},{1,5},{5,1},{2,6},{6,2},{3,7},{7,3},{8,12},{12,8},{9,1... | collective-permute-start | bytes 1572872 | tf_op jit(solution)/shard_map/ppermute | solution.py:534
  (22 other events, 347.5 us)
Sparse Core Ops, SparseCore 0:
  15.8 77.5 all-gather.6
  96.1 73.3 all-gather.8
  242.0 53.1 all-gather.10
  297.2 67.9 all-gather.12

commit v3 on v0

v3 whole, which is shorter than its diff:
```python
import types

import jax
import jax.numpy as jnp
from jax import lax
from jax.experimental import pallas as pl
from jax.experimental.pallas import tpu as pltpu
from jax.sharding import PartitionSpec as P

HEAD = 64
EPSILON = 1e-06
EXTRA = 16
F32 = jnp.float32
LOW = jnp.bfloat16

NN = (((1,), (0,)), ((), ()))
NT = (((1,), (1,)), ((), ()))
TN = (((0,), (0,)), ((), ()))


def mm(left, right, dims=NN):
    return lax.dot_general(left, right, dims, preferred_element_type=F32)


def whole(*shape):
    return pl.BlockSpec(shape, lambda t, _: (0,) * len(shape))


def part(*shape):
    return pl.BlockSpec((1,) + shape, lambda t, _: (t,) + (0,) * len(shape))


def call(body, grid, where, ins, outs, scratch=(), pieces=(), flops=0, moved=0, exps=0):
    names = [entry[0] for entry in ins]
    later = [entry[0] for entry in outs] + [entry[0] for entry in scratch]

    def kernel(where_ref, *refs):
        r = types.SimpleNamespace(where=where_ref)
        count = len(names) + len(pieces)
        r.pieces = refs[len(names) : count]
        for name, ref in zip(names + later, refs[: len(names)] + refs[count:]):
            setattr(r, name, ref)
        body(r)

    results = pl.pallas_call(
        kernel,
        grid_spec=pltpu.PrefetchScalarGridSpec(
            num_scalar_prefetch=1,
            grid=(grid,),
            in_specs=[entry[1] for entry in ins]
            + [pl.BlockSpec(memory_space=pltpu.HBM)] * len(pieces),
            out_specs=[entry[1] for entry in outs],
            scratch_shapes=[entry[1] for entry in scratch],
        ),
        out_shape=[jax.ShapeDtypeStruct(entry[2], entry[3]) for entry in outs],
        compiler_params=pltpu.CompilerParams(
            dimension_semantics=("arbitrary",), vmem_limit_bytes=56 << 20
        ),
        cost_estimate=pl.CostEstimate(flops=flops, bytes_accessed=moved, transcendentals=exps),
    )(where, *(entry[2] for entry in ins), *pieces)
    return types.SimpleNamespace(**{entry[0]: value for entry, value in zip(outs, results)})


def at_step(step):
    return pl.when(pl.program_id(0) == step)


def at_end():
    return pl.when(pl.program_id(0) == pl.num_programs(0) - 1)


def layer_norm(values, gain, shift):
    center = values - jnp.mean(values, axis=-1, keepdims=True)
    spread = jnp.mean(center * center, axis=-1, keepdims=True)
    return center * lax.rsqrt(spread + EPSILON) * gain + shift


def layer_norm_back(values, gain, grad):
    center = values - jnp.mean(values, axis=-1, keepdims=True)
    scale = lax.rsqrt(jnp.mean(center * center, axis=-1, keepdims=True) + EPSILON)
    unit = center * scale
    scaled = grad * gain
    back = scale * (
        scaled
        - jnp.mean(scaled, axis=-1, keepdims=True)
        - unit * jnp.mean(scaled * unit, axis=-1, keepdims=True)
    )
    return back, row_sum(grad * unit), row_sum(grad)


def row_sum(values):
    return jnp.sum(values, axis=0, keepdims=True)


def fetch_scratch(pieces, width, parts, wide):
    copies = pieces[0].shape[1] if len(pieces) == 1 else 4
    return [
        ("weights", pltpu.VMEM((parts, wide, width), LOW)),
        ("extras", pltpu.VMEM((parts, EXTRA, width), LOW)),
        ("sems", pltpu.SemaphoreType.DMA((parts, copies + 1))),
    ]


def fetch(r):
    parts = r.weights.shape[0]

    def copies(at):
        if len(r.pieces) == 1:
            sources = [r.pieces[0].at[at, owner] for owner in range(r.pieces[0].shape[1])]
            owners = list(range(len(sources)))
        else:
            core, row = r.where[1], r.where[2]
            sources = [r.pieces[4 * at + which] for which in range(4)]
            owners = [
                2 * (row + up - 2 * row * up) + (core + over - 2 * core * over)
                for over in range(2)
                for up in range(2)
            ]
        rows = sources[0].shape[0] - EXTRA
        extra = sources[0].at[pl.ds(rows, EXTRA), :]
        result = [pltpu.make_async_copy(extra, r.extras.at[at], r.sems.at[at, len(sources)])]
        for which, (source, owner) in enumerate(zip(sources, owners)):
            target = r.weights.at[at, pl.ds(pl.multiple_of(owner * rows, rows), rows), :]
            result.append(
                pltpu.make_async_copy(source.at[pl.ds(0, rows), :], target, r.sems.at[at, which])
            )
        return result

    @at_step(0)
    def _():
        for at in range(parts):
            for copy in copies(at):
                copy.start()

    def wait(at):
        @at_step(at)
        def _():
            for copy in copies(at):
                copy.wait()

    for at in range(parts):
        wait(at)
    return r.weights.at[pl.program_id(0)], r.extras.at[pl.program_id(0)]


def joined(terms):
    wide = terms.astype(F32)
    return wide[0:1] + (wide[1:2] + wide[2:3])


def gradient_outs(parts, wide, total, stepwise):
    if not stepwise:
        return [("gradient", part(wide, total), (parts, wide, total), LOW)]
    shape = (2, parts, wide // 4, total)
    block = pl.BlockSpec((2, 1, wide // 4, total), lambda t, _: (0, t, 0, 0))
    return [("kept", block, shape, LOW), ("sent", block, shape, LOW)]


def store_gradient(r, pairs):
    column = 0
    for turned, right in pairs:
        span = slice(column, column + right.shape[1])
        column += right.shape[1]
        if hasattr(r, "gradient"):
            r.gradient[0, :, span] = mm(turned[...], right).astype(LOW)
            continue
        core, row = r.where[1], r.where[2]
        rows = r.kept.shape[2]
        for which, out in enumerate((r.kept, r.sent)):
            for far in range(2):
                owner = 2 * (row + far - 2 * row * far) + (core + which - 2 * core * which)
                start = pl.multiple_of(owner * rows, rows)
                out[far, 0, :, span] = mm(turned[pl.ds(start, rows), :], right).astype(LOW)


def shards_body(r):
    rows, width = r.qkv.shape[1:]
    hidden = r.up.shape[1]
    for piece in range(3):
        r.a[:rows, piece * width : (piece + 1) * width] = r.qkv[piece].astype(LOW)
    r.a[:rows, 3 * width :] = r.out[...].T.astype(LOW)
    r.f[:rows, :hidden] = r.up[...].astype(LOW)
    r.f[:rows, hidden:] = r.down[...].T.astype(LOW)
    r.a[rows:] = jnp.zeros((EXTRA, 4 * width), LOW)
    r.f[rows:] = jnp.zeros((EXTRA, 2 * hidden), LOW)
    for ref, row, shard in ((r.bqv, 0, r.a), (r.bqv, 1, r.a), (r.bup, 0, r.f)):
        left = ref[row : row + 1, :]
        for piece in range(3):
            low = left.astype(LOW)
            left = left - low.astype(F32)
            at = rows + 3 * row + piece
            shard[at : at + 1, : low.shape[1]] = low


def shards(where, w_qkv, w_out, w_up, w_down, b_qv, b_up):
    _, rows, width = w_qkv.shape
    hidden = w_up.shape[1] // 2
    got = call(
        shards_body,
        1,
        where,
        [
            ("qkv", whole(3, rows, width), w_qkv),
            ("out", whole(width, rows), w_out),
            ("up", pl.BlockSpec((rows, hidden), lambda t, at: (0, at[0])), w_up),
            ("down", pl.BlockSpec((hidden, rows), lambda t, at: (at[0], 0)), w_down),
            ("bqv", whole(2, width), b_qv),
            ("bup", pl.BlockSpec((1, hidden), lambda t, at: (0, at[0])), b_up[None]),
        ],
        [
            ("a", whole(rows + EXTRA, 4 * width), (rows + EXTRA, 4 * width), LOW),
            ("f", whole(rows + EXTRA, 2 * hidden), (rows + EXTRA, 2 * hidden), LOW),
        ],
        moved=6 * rows * (4 * width + 2 * hidden),
    )
    return got.a, got.f


def attention(where, pieces, parts, keep, first, carried, last):
    rows = keep.shape[0]
    half = rows // 2
    width = pieces[0].shape[-1] // 4
    heads = width // HEAD
    wide = first[0].shape[1] if first else carried[0].shape[1]

    def body(r):
        w, extra = fetch(r)
        normed = r.n1_out if first else r.n1

        @at_step(0)
        def _():
            if not first:
                r.y_out[...] = r.y[...]
                return
            for at, ref in ((0, r.own), (half, r.far)):
                tokens = ref[...].astype(F32)
                normed[at : at + half] = layer_norm(tokens, r.g1[...], r.s1[...]).astype(LOW)
                r.y_out[at : at + half] = tokens + r.b_out[...]

        terms = extra[...]
        bias_q, bias_v = joined(terms[0:3, :width]), joined(terms[3:6, :width])
        bias = jnp.concatenate([bias_q, jnp.zeros_like(bias_q), bias_v], axis=1)
        low = (mm(normed[...], w[:, : 3 * width]) + bias).astype(LOW)
        r.p[0] = low
        seen = r.keep[...] > 0
        for head in range(heads):
            at = head * HEAD
            query = low[:, at : at + HEAD]
            key = low[:, width + at : width + at + HEAD]
            value = low[:, 2 * width + at : 2 * width + at + HEAD]
            scores = jnp.where(seen, mm(key, query, NT) * HEAD**-0.5, -1e30)
            top = jnp.max(scores, axis=0, keepdims=True)
            exponent = jnp.exp(scores - top)
            total = jnp.sum(exponent, axis=0, keepdims=True)
            probability = (exponent * (1.0 / total)).astype(LOW)
            r.o[0, :, at : at + HEAD] = mm(probability, value, TN).astype(LOW)
            r.l[0, head : head + 1, :] = top + jnp.log(total)
        r.y_out[...] += mm(r.o[0], w[:, 3 * width :], NT)

        if last:

            @at_end()
            def _():
                r.n2[...] = layer_norm(r.y_out[...], r.g2[...], r.s2[...]).astype(LOW)

    line = whole(1, wide)
    ins = [("keep", whole(rows, 1), keep)]
    outs = [
        ("p", part(rows, 3 * width), (parts, rows, 3 * width), LOW),
        ("o", part(rows, width), (parts, rows, width), LOW),
        ("l", part(heads, rows), (parts, heads, rows), F32),
        ("y_out", whole(rows, wide), (rows, wide), F32),
    ]
    if first:
        specs = [whole(half, wide)] * 2 + [line] * 3
        ins += list(zip(("own", "far", "b_out", "g1", "s1"), specs, first))
        outs.append(("n1_out", whole(rows, wide), (rows, wide), LOW))
    else:
        ins += list(zip(("n1", "y"), [whole(rows, wide)] * 2, carried))
    if last:
        ins += list(zip(("g2", "s2"), [line] * 2, last))
        outs.append(("n2", whole(rows, wide), (rows, wide), LOW))
    return call(
        body,
        parts,
        where,
        ins,
        outs,
        fetch_scratch(pieces, 4 * width, parts, wide),
        pieces,
        flops=8 * parts * rows * wide * width + 4 * parts * rows * rows * width,
        moved=8 * parts * wide * width + 12 * rows * wide,
        exps=parts * heads * rows * rows,
    )


def forward(where, pieces, parts, own, far, grad, carried, residual, stepwise):
    rows, wide = own.shape
    half = rows // 2
    width = pieces[0].shape[-1] // 2

    def body(r):
        w, extra = fetch(r)

        @at_step(0)
        def _():
            r.both[:rows] = r.own[...]
            r.both[rows:] = r.far[...]
            r.turned[...] = r.both[...].T
            r.turned_grad[...] = r.grad[...].T
            r.branch_sum[...] = r.branch_in[...] if carried else jnp.zeros((2 * rows, wide), F32)
            r.grad_sum[...] = r.grad_in[...] if carried else jnp.zeros((2 * rows, wide), F32)

        hidden = mm(r.both[...], w[:, :width]) + joined(extra[0:3, :width])
        bell = 0.5 * (1.0 + lax.erf(hidden * 0.5**0.5))
        active = (hidden * bell).astype(LOW)
        slope = bell + hidden * jnp.exp(hidden * hidden * -0.5) * 0.3989422804014327
        r.branch_sum[...] += mm(active, w[:, width:], NT)
        grad_hidden = (mm(r.grad[...], w[:, width:]) * slope).astype(LOW)
        r.db[0] = row_sum(grad_hidden.astype(F32))
        r.grad_sum[...] += mm(grad_hidden, w[:, :width], NT)
        store_gradient(r, [(r.turned, grad_hidden), (r.turned_grad, active)])

        if residual is None:
            return

        @at_end()
        def _():
            r.out_keep[:half] = r.y[:half] + r.branch_sum[:half]
            r.out_keep[half:] = r.branch_sum[rows + half :]
            r.out_send[:half] = (r.y[half:] + r.branch_sum[half:rows]).astype(LOW)
            r.out_send[half:] = r.branch_sum[rows : rows + half].astype(LOW)
            r.dn_keep[...] = r.grad_sum[:rows]
            r.dn_send[...] = r.grad_sum[rows:].astype(LOW)

    mine, double = whole(rows, wide), whole(2 * rows, wide)
    sums = [("branch_sum", (2 * rows, wide), F32), ("grad_sum", (2 * rows, wide), F32)]
    ins = [("own", mine, own), ("far", mine, far), ("grad", double, grad)]
    outs = [("db", part(1, width), (parts, 1, width), F32)]
    scratch = [
        ("both", pltpu.VMEM((2 * rows, wide), LOW)),
        ("turned", pltpu.VMEM((wide, 2 * rows), LOW)),
        ("turned_grad", pltpu.VMEM((wide, 2 * rows), LOW)),
    ]
    if carried:
        ins += [("branch_in", double, carried[0]), ("grad_in", double, carried[1])]
    if residual is None:
        outs += [(name, double, shape, kind) for name, shape, kind in sums]
    else:
        ins.append(("y", mine, residual))
        outs += [
            ("out_keep", mine, (rows, wide), F32),
            ("out_send", mine, (rows, wide), LOW),
            ("dn_keep", mine, (rows, wide), F32),
            ("dn_send", mine, (rows, wide), LOW),
        ]
        scratch += [(name, pltpu.VMEM(shape, kind)) for name, shape, kind in sums]
    outs += gradient_outs(parts, wide, 2 * width, stepwise)
    return call(
        body,
        parts,
        where,
        ins,
        outs,
        scratch + fetch_scratch(pieces, 2 * width, parts, wide),
        pieces,
        flops=24 * parts * rows * width * wide,
        moved=8 * parts * wide * width + 12 * rows * wide,
        exps=4 * parts * rows * width,
    )


def backward(where, pieces, parts, saved, keep, normed, first, carried, last, stepwise):
    rows, wide = normed.shape
    half = rows // 2
    width = saved.o.shape[2]
    heads = width // HEAD

    def body(r):
        w, _ = fetch(r)
        low_grad = r.dyb_out if first else r.dyb

        @at_step(0)
        def _():
            if first:
                grad_normed = r.dn_keep[...] + r.dn_came[...].astype(F32)
                back, gain_sum, shift_sum = layer_norm_back(r.y[...], r.g2[...], grad_normed)
                grad_out = r.grad[...].astype(F32)
                r.dy_sum[...] = grad_out + back
                low_grad[...] = r.dy_sum[...].astype(LOW)
                r.sums[0:1] = row_sum(low_grad[...].astype(F32))
                r.sums[1:2] = row_sum(grad_out)
                r.sums[2:3] = gain_sum
                r.sums[3:4] = shift_sum
                r.sums[4:8] = jnp.zeros((4, wide), F32)
                r.dn_sum[...] = jnp.zeros_like(r.dn_sum)
            else:
                r.dn_sum[...] = r.dn[...]
            r.turned[...] = r.n1[...].T
            r.turned_grad[...] = low_grad[...].T

        grad_mixed = mm(low_grad[...], w[:, 3 * width :]).astype(LOW)
        seen = r.keep[...] > 0
        for head in range(heads):
            at = head * HEAD
            query = r.p[0, :, at : at + HEAD]
            key = r.p[0, :, width + at : width + at + HEAD]
            value = r.p[0, :, 2 * width + at : 2 * width + at + HEAD]
            grad = grad_mixed[:, at : at + HEAD]
            scores = jnp.where(seen, mm(key, query, NT) * HEAD**-0.5, -1e30)
            probability = jnp.exp(scores - r.l[0, head : head + 1, :])
            grad_probability = mm(value, grad, NT)
            grad_value = mm(probability.astype(LOW), grad)
            inner = jnp.sum(grad_probability * probability, axis=0, keepdims=True)
            grad_scores = (probability * (grad_probability - inner)).astype(LOW)
            grad_query = mm(grad_scores, key, TN) * HEAD**-0.5
            grad_key = mm(grad_scores, query) * HEAD**-0.5
            r.dp[:, at : at + HEAD] = grad_query.astype(LOW)
            r.dp[:, width + at : width + at + HEAD] = grad_key.astype(LOW)
            r.dp[:, 2 * width + at : 2 * width + at + HEAD] = grad_value.astype(LOW)
        r.db[0] = row_sum(r.dp[...].astype(F32))
        r.dn_sum[...] += mm(r.dp[...], w[:, : 3 * width], NT)
        store_gradient(r, [(r.turned, r.dp[...]), (r.turned_grad, r.o[0])])

        if not last:
            return

        @at_end()
        def _():
            dy = r.dy_sum if first else r.dy
            gain_sum = shift_sum = 0.0
            for at, ref, out in ((0, r.own, r.gi_own), (half, r.far, r.gi_far)):
                back, gain_add, shift_add = layer_norm_back(
                    ref[...].astype(F32), r.g1[...], r.dn_sum[at : at + half]
                )
                out[...] = (dy[at : at + half] + back).astype(LOW)
                gain_sum, shift_sum = gain_sum + gain_add, shift_sum + shift_add
            r.end_sums[0:1] = gain_sum
            r.end_sums[1:2] = shift_sum
            r.end_sums[2:8] = jnp.zeros((6, wide), F32)

    mine, line, eight = whole(rows, wide), whole(1, wide), whole(8, wide)
    ins = [
        ("p", part(rows, 3 * width), saved.p),
        ("o", part(rows, width), saved.o),
        ("l", part(heads, rows), saved.l),
        ("keep", whole(rows, 1), keep),
        ("n1", mine, normed),
    ]
    outs = [("db", part(1, 3 * width), (parts, 1, 3 * width), F32)]
    scratch = [
        ("dp", pltpu.VMEM((rows, 3 * width), LOW)),
        ("turned", pltpu.VMEM((wide, rows), LOW)),
        ("turned_grad", pltpu.VMEM((wide, rows), LOW)),
    ]
    sums = [("dn_sum", (rows, wide), F32)]
    if first:
        ins += list(zip(("y", "dn_keep", "dn_came", "grad", "g2"), [mine] * 4 + [line], first))
        outs += [("dyb_out", mine, (rows, wide), LOW), ("sums", eight, (8, wide), F32)]
        sums.append(("dy_sum", (rows, wide), F32))
    else:
        ins += list(zip(("dyb", "dy", "dn"), [mine] * 3, carried))
    if last:
        ins += list(zip(("own", "far", "g1"), [whole(half, wide)] * 2 + [line], last))
        outs += [
            ("gi_own", whole(half, wide), (half, wide), LOW),
            ("gi_far", whole(half, wide), (half, wide), LOW),
            ("end_sums", eight, (8, wide), F32),
        ]
        scratch += [(name, pltpu.VMEM(shape, kind)) for name, shape, kind in sums]
    else:
        outs += [(name, mine, shape, kind) for name, shape, kind in sums]
    outs += gradient_outs(parts, wide, 4 * width, stepwise)
    return call(
        body,
        parts,
        where,
        ins,
        outs,
        scratch + fetch_scratch(pieces, 4 * width, parts, wide),
        pieces,
        flops=16 * parts * rows * wide * width + 10 * parts * rows * rows * width,
        moved=16 * parts * wide * width + 16 * rows * wide,
        exps=parts * heads * rows * rows,
    )


def spread(where, pieces, parts):
    def body(r):
        for at in range(parts):

            @at_step(at)
            def _(ref=getattr(r, f"piece{at}")):
                r.out[...] = ref[...].astype(F32)

    pair = pieces[0].shape
    block = pl.BlockSpec(pair, lambda t, at: (lax.rem(at[3] - t + parts, parts), 0, 0))
    return call(
        body,
        parts,
        where,
        [(f"piece{at}", whole(*pair), piece) for at, piece in enumerate(pieces)],
        [("out", block, (parts * pair[0],) + pair[1:], F32)],
        moved=6 * parts * pieces[0].size,
    ).out


def forward_total(where, own, far):
    rows, width = own.shape[0], own.shape[1] // 2

    def body(r):
        for flip, ref in ((0, r.own), (1, r.far)):
            block = r.where[0] + flip - 2 * r.where[0] * flip
            span = pl.ds(pl.multiple_of(block * width, width), width)
            r.up[:, span] = ref[:, :width].astype(F32)
            r.down[span, :] = ref[:, width:].astype(F32).T

    got = call(
        body,
        1,
        where,
        [("own", whole(rows, 2 * width), own), ("far", whole(rows, 2 * width), far)],
        [
            ("up", whole(rows, 2 * width), (rows, 2 * width), F32),
            ("down", whole(2 * width, rows), (2 * width, rows), F32),
        ],
        moved=24 * rows * width,
    )
    return got.up, got.down


def attention_total(where, grad):
    rows, width = grad.shape[0], grad.shape[1] // 4

    def body(r):
        for piece in range(3):
            r.qkv[piece] = r.grad[:, piece * width : (piece + 1) * width]
        r.out[...] = r.grad[:, 3 * width :].T

    got = call(
        body,
        1,
        where,
        [("grad", whole(rows, 4 * width), grad)],
        [
            ("qkv", whole(3, rows, width), (3, rows, width), F32),
            ("out", whole(width, rows), (width, rows), F32),
        ],
        moved=32 * rows * width,
    )
    return got.qkv, got.out


def on_device(
    inputs,
    cotangent,
    visible,
    w_qkv,
    b_qv,
    w_out,
    b_out,
    w_up,
    b_up,
    w_down,
    b_down,
    gain_one,
    shift_one,
    gain_two,
    shift_two,
):
    images, half, wide = inputs.shape
    ctx_at, tp_at, fsdp_at = (lax.axis_index(name) for name in ("ctx", "tp", "fsdp"))
    blocks, parts, owners = (lax.axis_size(name) for name in ("ctx", "tp", "fsdp"))
    assert blocks == 2 and images == blocks * parts
    first = blocks * tp_at
    mine, other = first + ctx_at, first + 1 - ctx_at
    where = jnp.stack([ctx_at, fsdp_at % 2, fsdp_at // 2, tp_at]).astype(jnp.int32)
    heads_width = w_qkv.shape[2]
    hidden_half = w_up.shape[1] // 2
    rows = 2 * half

    def swap(values):
        return lax.ppermute(values, "ctx", [(0, 1), (1, 0)])

    def pick(values, index):
        return lax.dynamic_index_in_dim(values, index, 0, keepdims=False)

    def in_order(own, received):
        return jnp.where(ctx_at == 0, own, received), jnp.where(ctx_at == 0, received, own)

    stepwise = owners == 4 and parts == 4
    behind = jnp.mod(tp_at - jnp.arange(parts), parts) if stepwise else jnp.arange(parts)

    def to_core(values):
        return lax.ppermute(values, "fsdp", [(0, 1), (1, 0), (2, 3), (3, 2)])

    def to_y(values):
        return lax.ppermute(values, "fsdp", [(0, 2), (2, 0), (1, 3), (3, 1)])

    def to_tp(values):
        return lax.ppermute(values, "tp", [(i, (i + 1) % parts) for i in range(parts)])

    def gather(shard):
        full = lax.all_gather(shard, ("tp", "fsdp"), axis=0, tiled=True)
        return [full.reshape(parts, owners, *shard.shape)]

    def scatter(gradient):
        flat = gradient.reshape(-1, gradient.shape[2])
        return lax.psum_scatter(flat, ("tp", "fsdp"), scatter_dimension=0, tiled=True)

    def raised(upper, came):
        return upper.astype(F32) + came.astype(F32)

    def onward(total):
        return to_tp(total.astype(LOW))

    tie = lax.optimization_barrier

    a0, b0 = shards(where, w_qkv.transpose(1, 0, 2), w_out, w_up, w_down, b_qv, b_up)
    own = pick(inputs, mine)
    cot_pair = jnp.stack([pick(cotangent, mine), pick(cotangent, other)])
    mine_seen = pick(visible, mine).reshape(blocks, half)
    other_seen = pick(visible, other).reshape(blocks, half)
    keep = jnp.concatenate([pick(mine_seen, ctx_at), pick(mine_seen, 1 - ctx_at)])
    keep_other = jnp.concatenate([pick(other_seen, 1 - ctx_at), pick(other_seen, ctx_at)])
    keep, keep_other = keep[:, None], keep_other[:, None]
    keep_all = jnp.concatenate([keep, keep_other]).astype(LOW)
    norm_one, norm_two = (gain_one[None], shift_one[None]), (gain_two[None], shift_two[None])
    far = swap(pick(inputs, other))

    def hidden_gradient(swapped):
        rows_of = [cot_pair[0], swapped[1], swapped[0], cot_pair[1]]
        return jnp.concatenate(rows_of) * keep_all

    def output_pair(kept, came):
        seen = jnp.concatenate([keep[:half], keep_other[half:]]).astype(F32)
        came = came.astype(F32)
        rows_of = kept + jnp.concatenate([came[half:], came[:half]]) + b_down
        rows_of = (rows_of * seen).astype(LOW)
        return jnp.stack(in_order(rows_of[:half], rows_of[half:]))

    if stepwise:
        a0, b0, a1, ya0, far = tie((a0, b0, to_tp(a0), to_y(a0), far))

        a1, a2, ya1, ca0, cya0, cot_swapped = tie(
            (a1, to_tp(a1), to_y(a1), to_core(a0), to_core(ya0), swap(cot_pair))
        )

        a2, a3, ya2, ca1, cya1 = tie((a2, to_tp(a2), to_y(a2), to_core(a1), to_core(ya1)))

        start = (own, far, b_out[None]) + norm_one
        early = attention(
            where, [a0, ya0, ca0, cya0, a1, ya1, ca1, cya1], 2, keep, start, None, None
        )
        grad_low = hidden_gradient(cot_swapped)
        normed, total_y, grad_low, a3, b0, ya3, b1, ca2, cya2 = tie(
            (
                early.n1_out,
                early.y_out,
                grad_low,
                a3,
                b0,
                to_y(a3),
                to_tp(b0),
                to_core(a2),
                to_core(ya2),
            )
        )

        b2, yb0 = to_tp(b1), to_y(b0)
        ca3, cya3 = to_core(a3), to_core(ya3)
        late = attention(
            where,
            [a2, ya2, ca2, cya2, a3, ya3, ca3, cya3],
            2,
            keep,
            None,
            (normed, total_y),
            norm_two,
        )
        normed_two, residual = late.n2, late.y_out
        normed_two, b2, yb0 = tie((normed_two, b2, yb0))

        normed_far, b3, yb1, cb0, cyb0 = tie(
            (swap(normed_two), to_tp(b2), to_y(b1), to_core(b0), to_core(yb0))
        )

        def block(pieces, carried, last):
            return forward(
                where, pieces, 1, normed_two, normed_far, grad_low, carried, last, True
            )

        def sums(got):
            return got.branch_sum, got.grad_sum

        f0 = block([b0, yb0, cb0, cyb0], None, None)
        sums0, sent0, yb2, cb1, cyb1 = tie(
            (sums(f0), f0.sent, to_y(b2), to_core(b1), to_core(yb1))
        )

        f1 = block([b1, yb1, cb1, cyb1], sums0, None)
        sums1, sent1, came0, yb3, cb2, cyb2 = tie(
            (sums(f1), f1.sent, to_core(sent0), to_y(b3), to_core(b2), to_core(yb2))
        )

        f2 = block([b2, yb2, cb2, cyb2], sums1, None)
        sums2, sent2, came1, cb3, cyb3 = tie(
            (sums(f2), f2.sent, to_core(sent1), to_core(b3), to_core(yb3))
        )

        def upper(got, came):
            return to_y(raised(got.kept[1, 0], came[1, 0]).astype(LOW))

        def lower(got, came, lift):
            return raised(got.kept[0, 0], came[0, 0]) + lift.astype(F32)

        lift1 = upper(f1, came1)
        f3 = block([b3, yb3, cb3, cyb3], sums2, residual)
        dn_send, out_send, sent3, came2 = tie(
            (f3.dn_send, f3.out_send, f3.sent, to_core(sent2))
        )

        lift2 = upper(f2, came2)
        dn_came, came3, lift1 = tie((swap(dn_send), to_core(sent3), lift1))

        ring_sum = onward(lower(f1, came1, lift1))
        out_came = swap(out_send)
        begin = (residual, f3.dn_keep, dn_came, grad_low[:rows], gain_two[None])
        g_early = backward(
            where,
            [a0, ya0, ca0, cya0, a1, ya1, ca1, cya1],
            2,
            early,
            keep,
            normed,
            begin,
            None,
            None,
            True,
        )
        carried, sent_early, ring_sum, out_came, lift2 = tie(
            (
                (g_early.dyb_out, g_early.dy_sum, g_early.dn_sum),
                g_early.sent,
                ring_sum,
                out_came,
                lift2,
            )
        )

        lift3 = upper(f3, came3)
        ring_sum = onward(ring_sum.astype(F32) + lower(f2, came2, lift2))
        h0 = output_pair(f3.out_keep, out_came)
        h1 = to_tp(h0)
        came_early = to_core(sent_early)
        g_late = backward(
            where,
            [a2, ya2, ca2, cya2, a3, ya3, ca3, cya3],
            2,
            late,
            keep,
            normed,
            None,
            carried,
            (own, far, gain_one[None]),
            True,
        )
        gi_far, sent_late, came_early, ring_sum, lift3 = tie(
            (g_late.gi_far, g_late.sent, came_early, ring_sum, lift3)
        )

        quarter = wide // owners // 4

        def rows_of(values, axis, block):
            return lax.dynamic_slice_in_dim(values, block * quarter, quarter, axis)

        def both(kept, came, block):
            return raised(rows_of(kept, 2, block), rows_of(came, 2, block))

        def first_sends(got, came):
            across = swap(both(got.kept, came, 1 - ctx_at).astype(LOW))
            second = raised(got.kept[1, :, 2 * quarter :], came[1, :, 2 * quarter :])
            return across, to_y(second.astype(LOW))

        def second_sends(got, came, across, up):
            near = both(got.kept, came, ctx_at) + across.astype(F32)
            second = raised(got.kept[0, :, 2 * quarter :], came[0, :, 2 * quarter :])
            second = second + up.astype(F32)
            return (
                near[0],
                to_y(near[1].astype(LOW)),
                rows_of(second, 1, ctx_at),
                swap(rows_of(second, 1, 1 - ctx_at).astype(LOW)),
            )

        def third(near, lifted, second, across):
            return jnp.concatenate(
                [near + lifted.astype(F32), second + across.astype(F32)], axis=1
            )

        up_bias = jnp.concatenate([f0.db, f1.db, f2.db, f3.db])
        qkv_bias = jnp.concatenate([g_early.db, g_late.db])
        up_bias = lax.dynamic_update_slice(
            jnp.zeros((parts, 2, hidden_half), F32), up_bias, (0, ctx_at, 0)
        )
        small = jnp.concatenate(
            [
                g_early.sums[:4],
                g_late.end_sums[:2],
                up_bias[behind].reshape(-1, wide),
                qkv_bias[behind].reshape(-1, wide),
            ]
        )
        ring_sum = onward(ring_sum.astype(F32) + lower(f3, came3, lift3))
        side0, up0 = first_sends(g_early, came_early)
        gi_far, came_late, small, small_came, h1 = tie(
            (swap(gi_far), to_core(sent_late), small, to_core(small), h1)
        )

        g0 = jnp.stack(in_order(g_late.gi_own, gi_far))
        h2, g1 = to_tp(h1), to_tp(g0)
        side1, up1 = first_sends(g_late, came_late)
        lift0 = upper(f0, came0)
        small = small + small_came
        side0, up0, ring_sum, h2, small, small_came = tie(
            (side0, up0, ring_sum, h2, small, to_y(small))
        )

        h3 = to_tp(h2)
        sends0 = second_sends(g_early, came_early, side0, up0)
        small = small + small_came
        sends0, g1, side1, up1, lift0, small, small_came = tie(
            (sends0, g1, side1, up1, lift0, small, swap(small))
        )

        g2 = to_tp(g1)
        forward_own = (ring_sum.astype(F32) + lower(f0, came0, lift0)).astype(LOW)
        sends1 = second_sends(g_late, came_late, side1, up1)
        halves0 = third(*sends0)
        small = small + small_came
        sends1, h3, forward_own, small, small_came = tie(
            (
                sends1,
                h3,
                forward_own,
                small,
                lax.ppermute(small, "tp", [(0, 1), (1, 0), (2, 3), (3, 2)]),
            )
        )

        total = onward(halves0[1])
        forward_far = swap(forward_own)
        result = spread(where, [h0, h1, h2, h3], parts)
        halves1 = third(*sends1)
        small = small + small_came
        total, g2, result, small, small_came = tie(
            (
                total,
                g2,
                result,
                small,
                lax.ppermute(small, "tp", [(0, 2), (2, 0), (1, 3), (3, 1)]),
            )
        )

        g3 = to_tp(g2)
        small = small + small_came
        total, forward_far = tie((onward(total.astype(F32) + halves1[0]), forward_far))

        up_total, down_total = forward_total(where, forward_own, forward_far)
        total, g3, up_total = tie((onward(total.astype(F32) + halves1[1]), g3, up_total))

        mine_half = (total.astype(F32) + halves0[0]).astype(LOW)
        far_half = swap(mine_half)
        grad_inputs = spread(where, [g0, g1, g2, g3], parts)
        lows, highs = in_order(mine_half, far_half)
        attention_sum = jnp.concatenate(
            [lows[:quarter], highs[:quarter], lows[quarter:], highs[quarter:]]
        ).astype(F32)
    else:
        attention_w, forward_w = gather(a0), gather(b0)
        grad_low = hidden_gradient(swap(cot_pair))
        start = (own, far, b_out[None]) + norm_one
        got = attention(where, attention_w, parts, keep, start, None, norm_two)
        end = forward(
            where,
            forward_w,
            parts,
            got.n2,
            swap(got.n2),
            grad_low,
            None,
            got.y_out,
            False,
        )
        h0 = output_pair(end.out_keep, swap(end.out_send))
        result = lax.all_gather(h0, "tp", axis=0, tiled=True).astype(F32)
        begin = (got.y_out, end.dn_keep, swap(end.dn_send), grad_low[:rows], gain_two[None])
        back = backward(
            where,
            attention_w,
            parts,
            got,
            keep,
            got.n1_out,
            begin,
            None,
            (own, far, gain_one[None]),
            False,
        )
        g0 = jnp.stack(in_order(back.gi_own, swap(back.gi_far)))
        grad_inputs = lax.all_gather(g0, "tp", axis=0, tiled=True).astype(F32)
        forward_own = scatter(end.gradient)
        attention_own = scatter(back.gradient)
        attention_sum = attention_own.astype(F32) + swap(attention_own).astype(F32)
        up_total, down_total = forward_total(where, forward_own, swap(forward_own))
        up_bias = lax.dynamic_update_slice(
            jnp.zeros((parts, 2, hidden_half), F32), end.db, (0, ctx_at, 0)
        )
        small = jnp.concatenate(
            [
                back.sums[:4],
                back.end_sums[:2],
                up_bias.reshape(-1, wide),
                back.db.reshape(-1, wide),
            ]
        )
        small = lax.psum(small, ("fsdp", "ctx", "tp"))
    qkv_total, out_total = attention_total(where, attention_sum)

    up_rows = parts * 2 * hidden_half // wide
    up_small = small[6 : 6 + up_rows].reshape(parts, 2 * hidden_half)
    qkv_small = small[6 + up_rows :].reshape(parts, 3, heads_width)
    return (
        result,
        grad_inputs,
        qkv_total.transpose(1, 0, 2),
        pick(qkv_small, tp_at)[0::2],
        out_total,
        small[0],
        up_total,
        pick(up_small, tp_at),
        down_total,
        small[1],
        small[4],
        small[5],
        small[2],
        small[3],
    )


def solution(mesh):
    placed = (
        P("fsdp", "ctx", None),
        P("fsdp", "ctx", None),
        P("fsdp", None),
        P("fsdp", None, "tp"),
        P(None, "tp"),
        P("tp", "fsdp"),
        P(),
        P("fsdp", "tp"),
        P("tp"),
        P("tp", "fsdp"),
        P(),
        P(),
        P(),
        P(),
        P(),
    )
    return jax.shard_map(
        on_device,
        mesh=mesh,
        in_specs=placed,
        out_specs=(
            P("fsdp", "ctx", None),
            P("fsdp", "ctx", None),
            P("fsdp", None, "tp"),
            P(None, "tp"),
            P("tp", "fsdp"),
            P(),
            P("fsdp", "tp"),
            P("tp"),
            P("tp", "fsdp"),
            P(),
            P(),
            P(),
            P(),
            P(),
        ),
        check_vma=False,
    )
```

time: 1300 us -> 389 us (0.30)
  waiting for transfers between devices: 1010 us -> 157 us
  Pallas kernels: 0 us -> 137 us
  matrix products: 110 us -> 0 us
  other arithmetic: 71.5 us -> 18.1 us
  starting transfers between devices: 2.05 us -> 49.6 us
  local copies, waits for them, and re-layouts: 56.8 us -> 16.6 us
  blocking collectives: 33.2 us -> 0 us
    psum x4 -> x0, waiting for transfers between devices: 773 us -> none  [the longest x3 731 us: head_total(): return lax.psum(partial_sum, 'tp')]
    ppermute x0 -> x73, waiting for transfers between devices: none -> 157 us  [the longest x18 84.1 us: to_tp(): lax.ppermute(values, 'tp', [(i, (i + 1) % parts) for i in range(parts)])]
    reduce_scatter x6 -> x0, waiting for transfers between devices: 156 us -> none  [the longest x1 47.2 us: on_device(): lax.psum_scatter(down_grad, 'fsdp', scatter_dimension=1, tiled=True)]
    pallas_call x0 -> x13, Pallas kernels: none -> 137 us  [call(): pl.pallas_call(kernel, grid_spec=pltpu.PrefetchScalarGridSpec(num_scalar_...]
    dot_general x18 -> x0, matrix products: 110 us -> none  [the longest x1 18.4 us: on_device(): jnp.dot(grad_branch, down_w.T, preferred_element_type=jnp.float32)]
    all_gather x5 -> x0, waiting for transfers between devices: 76.5 us -> none  [the longest x1 17.3 us: on_device(): lax.all_gather(w_up.astype(jnp.bfloat16), 'fsdp', axis=0, tiled=True)]
    ppermute x0 -> x73, starting transfers between devices: none -> 49.6 us  [the longest x17 17.2 us: to_y(): return lax.ppermute(values, 'fsdp', [(0, 2), (2, 0), (1, 3), (3, 1)])]
    reduce_sum x12 -> x0, other arithmetic: 29.1 us -> none  [the longest x3 12 us: layer_norm(): return center * lax.rsqrt(spread + EPSILON) * gain + shift]
  transfers between devices with their start and end apart: 15 -> 73, of which waited for: 14 -> 24; matrix products, arithmetic and copies ran while one was open for 11% -> 7% of each run, Pallas kernels for 0% -> 34%
where the time goes in v3:
time: 389 us; the launch traced here: 381 us
  waiting for transfers between devices  157 us (40%)
  Pallas kernels  137 us (35%)
  starting transfers between devices  49.6 us (13%)
  other arithmetic  18.1 us (5%)
  local copies, waits for them, and re-layouts  16.6 us (4%)
    pallas_call x13, Pallas kernels, call(): pl.pallas_call(kernel, grid_spec=pltpu.PrefetchScalarGridSpec(num_scalar_...  137 us
    ppermute x18, waiting for transfers between devices, to_tp(): lax.ppermute(values, 'tp', [(i, (i + 1) % parts) for i in range(parts)])  84.1 us
    ppermute x17, waiting for transfers between devices, to_y(): return lax.ppermute(values, 'fsdp', [(0, 2), (2, 0), (1, 3), (3, 1)])  26.5 us
    ppermute x1, waiting for transfers between devices, on_device(): lax.ppermute(small, 'tp', [(0, 1), (1, 0), (2, 3), (3, 2)])  22.2 us
    ppermute x13, waiting for transfers between devices, swap(): return lax.ppermute(values, 'ctx', [(0, 1), (1, 0)])  21.4 us
    ppermute x17, starting transfers between devices, to_y(): return lax.ppermute(values, 'fsdp', [(0, 2), (2, 0), (1, 3), (3, 1)])  17.2 us
    ppermute x18, starting transfers between devices, to_tp(): lax.ppermute(values, 'tp', [(i, (i + 1) % parts) for i in range(parts)])  12.8 us
    ppermute x13, starting transfers between devices, swap(): return lax.ppermute(values, 'ctx', [(0, 1), (1, 0)])  12.5 us
  transfers between devices with their start and end apart: 73, of which 24 were waited for; matrix products, arithmetic and copies ran while one was open for 7% of the time, Pallas kernels for 34%

profile of v3, /device:TPU:0, one launch (start us, length us, event | category | flops | bytes accessed | tf_op | source)
XLA Modules:
  0.0 381.4 jit_solution(2748372507619935232)
XLA Ops:
  1.2 3.4 shard_map.254
  4.6 3.0 collective-permute-start
  14.3 7.4 %collective-permute-done.2.refs_2_.refs_9_ = bf16[160,1024]{1,0:T(8,128)(2,1)S(1)} collective-permute-done((bf16[160,1024]{1,0:T(8,128)(2,1)S(1)}, bf16[160,1024]{1,0:T(8,128)(2,1)S(1)}, u32[]{:S(2)}, u32[]{:S(2)}) %collective-permute-start.2) | collective-permute-done | bytes 327712 | tf_op jit(solution)/shard_map/ppermute | solution.py:583
  25.6 8.4 %collective-permute-done.7 = bf16[2,160,1024]{2,1,0:T(8,128)(2,1)S(1)} collective-permute-done((bf16[2,160,1024]{2,1,0:T(8,128)(2,1)S(1)}, bf16[2,160,1024]{2,1,0:T(8,128)(2,1)S(1)}, u32[]{:S(2)}, u32[]{:S(2)}) %collective-permute-start.7) | collective-permute-done | bytes 655392 | tf_op jit(solution)/shard_map/ppermute | solution.py:583
  33.9 4.6 %collective-permute-done.3.refs_5_.refs_11_ = bf16[272,1024]{1,0:T(8,128)(2,1)S(1)} collective-permute-done((bf16[272,1024]{1,0:T(8,128)(2,1)}, bf16[272,1024]{1,0:T(8,128)(2,1)S(1)}, u32[]{:S(2)}, u32[]{:S(2)}) %collective-permute-start.3) | collective-permute-done | bytes 557088 | tf_op jit(solution)/shard_map/ppermute | solution.py:601
  43.2 12.7 %collective-permute-done.8.refs_9_.refs_15_ = bf16[272,1024]{1,0:T(8,128)(2,1)S(1)} collective-permute-done((bf16[272,1024]{1,0:T(8,128)(2,1)S(1)}, bf16[272,1024]{1,0:T(8,128)(2,1)S(1)}, u32[]{:S(2)}, u32[]{:S(2)}) %collective-permute-start.8) | collective-permute-done | bytes 557088 | tf_op jit(solution)/shard_map/ppermute | solution.py:601
  59.3 11.0 %shard_map.255 = (bf16[2,320,768]{2,1,0:T(8,128)(2,1)}, bf16[2,320,256]{2,1,0:T(8,128)(2,1)}, f32[2,4,320]{2,1,0:T(4,128)}, f32[320,1024]{1,0:T(8,128)}, bf16[320,1024]{1,0:T(8,128)(2,1)}) custom-call(s32[4]{0:T(128)} %pad_add_fusion.2.where_ref, s32[320,1]{1,0:T(8,128)} %broadcast_in_dim.38.refs_0_.refs_3_, ...), custom_call_target="tpu_custom_call" | custom-call | flops 1551892480 | bytes 8126464 | tf_op jit(solution)/shard_map/pallas_call | solution.py:45
  74.0 11.6 %shard_map.256 = (bf16[2,320,768]{2,1,0:T(8,128)(2,1)}, bf16[2,320,256]{2,1,0:T(8,128)(2,1)}, f32[2,4,320]{2,1,0:T(4,128)}, f32[320,1024]{1,0:T(8,128)}, bf16[320,1024]{1,0:T(8,128)(2,1)}) custom-call(s32[4]{0:T(128)} %pad_add_fusion.2.where_ref, s32[320,1]{1,0:T(8,128)} %broadcast_in_dim.38.refs_0_.refs_3_, ...), custom_call_target="tpu_custom_call" | custom-call | flops 1551892480 | bytes 8126464 | tf_op jit(solution)/shard_map/pallas_call | solution.py:45
  90.3 12.2 %collective-permute-done.22.refs_6_ = bf16[272,1024]{1,0:T(8,128)(2,1)S(1)} collective-permute-done((bf16[272,1024]{1,0:T(8,128)(2,1)S(1)}, bf16[272,1024]{1,0:T(8,128)(2,1)S(1)}, u32[]{:S(2)}, u32[]{:S(2)}) %collective-permute-start.22) | collective-permute-done | bytes 557088 | tf_op jit(solution)/shard_map/ppermute | solution.py:598
  103.0 3.5 collective-permute-done.21.refs_6_
  107.6 10.9 %shard_map.257 = (f32[1,1,512]{2,1,0:T(1,128)}, f32[640,1024]{1,0:T(8,128)}, f32[640,1024]{1,0:T(8,128)}, bf16[2,1,256,1024]{3,2,1,0:T(8,128)(2,1)}, bf16[2,1,256,1024]{3,2,1,0:T(8,128)(2,1)}) custom-call(s32[4]{0:T(128)} %pad_add_fusion.2.where_ref, bf16[320,1024]{1,0:T(8,128)(2,1)} %get-tuple-element.208.refs_0_, bf16[320,1024]{1,0:T(8,128)(2,1)} %copy-done.47, ...), custom_call_target="tpu_custom_call" | custom-call | flops 4026531840 | bytes 8126464 | tf_op jit(solution)/shard_map/pallas_call | solution.py:45
  121.5 12.5 %shard_map.258 = (f32[1,1,512]{2,1,0:T(1,128)}, f32[640,1024]{1,0:T(8,128)}, f32[640,1024]{1,0:T(8,128)}, bf16[2,1,256,1024]{3,2,1,0:T(8,128)(2,1)}, bf16[2,1,256,1024]{3,2,1,0:T(8,128)(2,1)}) custom-call(s32[4]{0:T(128)} %pad_add_fusion.2.where_ref, bf16[320,1024]{1,0:T(8,128)(2,1)} %get-tuple-element.208.refs_0_, bf16[320,1024]{1,0:T(8,128)(2,1)} %copy-done.47, ...), custom_call_target="tpu_custom_call" | custom-call | flops 4026531840 | bytes 8126464 | tf_op jit(solution)/shard_map/pallas_call | solution.py:45
  135.3 25.4 %shard_map.259 = (f32[1,1,512]{2,1,0:T(1,128)}, f32[640,1024]{1,0:T(8,128)}, f32[640,1024]{1,0:T(8,128)}, bf16[2,1,256,1024]{3,2,1,0:T(8,128)(2,1)}, bf16[2,1,256,1024]{3,2,1,0:T(8,128)(2,1)}) custom-call(s32[4]{0:T(128)} %pad_add_fusion.2.where_ref, bf16[320,1024]{1,0:T(8,128)(2,1)} %get-tuple-element.208.refs_0_, bf16[320,1024]{1,0:T(8,128)(2,1)} %copy-done.47, ...), custom_call_target="tpu_custom_call" | custom-call | flops 4026531840 | bytes 8126464 | tf_op jit(solution)/shard_map/pallas_call | solution.py:45
  161.8 12.1 %shard_map.260 = (f32[1,1,512]{2,1,0:T(1,128)}, f32[320,1024]{1,0:T(8,128)}, bf16[320,1024]{1,0:T(8,128)(2,1)}, f32[320,1024]{1,0:T(8,128)}, bf16[320,1024]{1,0:...) custom-call(s32[4]{0:T(128)} %pad_add_fusion.2.where_ref, ...), custom_call_target="tpu_custom_call" | custom-call | flops 4026531840 | bytes 8126464 | tf_op jit(solution)/shard_map/pallas_call | solution.py:45
  178.8 11.2 %collective-permute-done.38 = bf16[256,1024]{1,0:T(8,128)(2,1)S(1)} collective-permute-done((bf16[256,1024]{1,0:T(8,128)(2,1)S(1)}, bf16[256,1024]{1,0:T(8,128)(2,1)S(1)}, u32[]{:S(2)}, u32[]{:S(2)}) %collective-permute-start.38) | collective-permute-done | bytes 524320 | tf_op jit(solution)/shard_map/ppermute | solution.py:598
  193.2 17.3 %shard_map.261 = (f32[2,1,768]{2,1,0:T(1,128)}, bf16[320,1024]{1,0:T(8,128)(2,1)}, f32[8,1024]{1,0:T(8,128)}, f32[320,1024]{1,0:T(8,128)}, f32[320,1024]{1,0:T(8...) custom-call(s32[4]{0:T(128)} %pad_add_fusion.2.where_ref, ...), custom_call_target="tpu_custom_call" | custom-call | flops 3208642560 | bytes 13631488 | tf_op jit(solution)/shard_map/pallas_call | solution.py:45
  216.3 16.8 %shard_map.262 = (f32[2,1,768]{2,1,0:T(1,128)}, bf16[160,1024]{1,0:T(8,128)(2,1)}, bf16[160,1024]{1,0:T(8,128)(2,1)}, f32[8,1024]{1,0:T(8,128)}, bf16[2,2,256,10...) custom-call(s32[4]{0:T(128)} %pad_add_fusion.2.where_ref, bf16[2,320,768]{2,1,0:T(8,128)(2,1)} %get-tuple-element.253.refs_0_, ...), custom_call_target="tpu_custom_call" | custom-call | flops 3208642560 | bytes 13631488 | tf_op jit(solution)/shard_map/pallas_call | solution.py:45
  244.3 12.8 %collective-permute-done.51.refs_1_ = bf16[2,160,1024]{2,1,0:T(8,128)(2,1)S(1)} collective-permute-done((bf16[2,160,1024]{2,1,0:T(8,128)(2,1)S(1)}, bf16[2,160,1024]{2,1,0:T(8,128)(2,1)S(1)}, u32[]{:S(2)}, u32[]{:S(2)}) %collective-permute-start.51) | collective-permute-done | bytes 655392 | tf_op jit(solution)/shard_map/ppermute | solution.py:601
  257.5 3.7 collective-permute-done.48
  261.2 3.0 collective-permute-start.52
  271.2 2.6 collective-permute-done.47
  275.0 12.8 %collective-permute-done.52.refs_2_ = bf16[2,160,1024]{2,1,0:T(8,128)(2,1)S(1)} collective-permute-done((bf16[2,160,1024]{2,1,0:T(8,128)(2,1)S(1)}, bf16[2,160,1024]{2,1,0:T(8,128)(2,1)S(1)}, u32[]{:S(2)}, u32[]{:S(2)}) %collective-permute-start.52) | collective-permute-done | bytes 655392 | tf_op jit(solution)/shard_map/ppermute | solution.py:601
  291.4 2.6 collective-permute-done.58
  295.8 6.1 %collective-permute-done.56.refs_1_ = bf16[2,160,1024]{2,1,0:T(8,128)(2,1)S(1)} collective-permute-done((bf16[2,160,1024]{2,1,0:T(8,128)(2,1)S(1)}, bf16[2,160,1024]{2,1,0:T(8,128)(2,1)S(1)}, u32[]{:S(2)}, u32[]{:S(2)}) %collective-permute-start.56) | collective-permute-done | bytes 655392 | tf_op jit(solution)/shard_map/ppermute | solution.py:601
  308.0 22.2 %collective-permute-done.66 = f32[13,1024]{1,0:T(8,128)S(1)} collective-permute-done((f32[13,1024]{1,0:T(8,128)S(1)}, f32[13,1024]{1,0:T(8,128)S(1)}, u32[]{:S(2)}, u32[]{:S(2)}) %collective-permute-start.66) | collective-permute-done | bytes 53280 | tf_op jit(solution)/shard_map/ppermute | solution.py:847
  331.7 5.1 %shard_map.263 = f32[8,160,1024]{2,1,0:T(8,128)} custom-call(s32[4]{0:T(128)} %pad_add_fusion.2.where_ref, bf16[2,160,1024]{2,1,0:T(8,128)(2,1)} %copy-done.2, bf16[2,160,1024]{2,1,0:T(8,128)(2,1)} %copy-done.19, bf16[2,160,1024]{2,1,0:T(8,128)(2,1)} %copy-done.20, bf16[2,160,1024]{2,1,0:T(8,128)(2,1)} %copy-done.22), custom_call_target="tpu_custom_call" | custom-call | bytes 7864320 | tf_op jit(solution)/shard_map/pallas_call | solution.py:45
  336.9 4.1 %collective-permute-done.61 = bf16[128,1024]{1,0:T(8,128)(2,1)S(1)} collective-permute-done((bf16[128,1024]{1,0:T(8,128)(2,1)S(1)}, bf16[128,1024]{1,0:T(8,128)(2,1)S(1)}, u32[]{:S(2)}, u32[]{:S(2)}) %collective-permute-start.61) | collective-permute-done | bytes 262176 | tf_op jit(solution)/shard_map/ppermute | solution.py:601
  342.6 10.9 %collective-permute-done.68 = bf16[128,1024]{1,0:T(8,128)(2,1)S(1)} collective-permute-done((bf16[128,1024]{1,0:T(8,128)(2,1)S(1)}, bf16[128,1024]{1,0:T(8,128)(2,1)S(1)}, u32[]{:S(2)}, u32[]{:S(2)}) %collective-permute-start.68) | collective-permute-done | bytes 262176 | tf_op jit(solution)/shard_map/ppermute | solution.py:601
  354.6 3.4 shard_map.264
  358.0 11.2 %collective-permute-done.70 = bf16[128,1024]{1,0:T(8,128)(2,1)S(1)} collective-permute-done((bf16[128,1024]{1,0:T(8,128)(2,1)S(1)}, bf16[128,1024]{1,0:T(8,128)(2,1)S(1)}, u32[]{:S(2)}, u32[]{:S(2)}) %collective-permute-start.70) | collective-permute-done | bytes 262176 | tf_op jit(solution)/shard_map/ppermute | solution.py:601
  371.7 5.1 %shard_map.265 = f32[8,160,1024]{2,1,0:T(8,128)} custom-call(s32[4]{0:T(128)} %pad_add_fusion.2.where_ref, bf16[2,160,1024]{2,1,0:T(8,128)(2,1)} %copy-done.1, bf16[2,160,1024]{2,1,0:T(8,128)(2,1)} %copy-done.18, bf16[2,160,1024]{2,1,0:T(8,128)(2,1)} %copy-done.21, bf16[2,160,1024]{2,1,0:T(8,128)(2,1)} %copy-done.23), custom_call_target="tpu_custom_call" | custom-call | bytes 7864320 | tf_op jit(solution)/shard_map/pallas_call | solution.py:45
  378.1 2.9 shard_map.266
  (355 shorter events, 86.5 us)
Async XLA Ops:
  4.6 18.1 %collective-permute-start = (bf16[272,1024]{1,0:T(8,128)(2,1)}, bf16[272,1024]{1,0:T(8,128)(2,1)}, u32[]{:S(2)}, u32[]{:S(2)}) collective-permute-start(bf16[272,1024]{1,0:T(8,128)(2,1)} %get-tuple-element.178.refs_6_.refs_10_), channel_id=1, source_target_pairs={{0,1},{1,2},{2,3},{3,0},{4,5},{5,6},{6,7},{7,4},{8,9},{9,10},{10,1... | collective-permute-start | bytes 1671176 | tf_op jit(solution)/shard_map/ppermute | solution.py:601
  13.7 20.3 %collective-permute-start.7 = (bf16[2,160,1024]{2,1,0:T(8,128)(2,1)S(1)}, bf16[2,160,1024]{2,1,0:T(8,128)(2,1)S(1)}, u32[]{:S(2)}, u32[]{:S(2)}) collective-permute-start(bf16[2,160,1024]{2,1,0:T(8,128)(2,1)S(1)} %pad_maximum_fusion), channel_id=1, source_target_pairs={{0,4},{4,0},{1,5},{5,1},{2,6},{6,2},{3,7},{7,3},{8,12},{12,8},{9,1... | collective-permute-start | bytes 1966088 | tf_op jit(solution)/shard_map/ppermute | solution.py:583
  38.6 17.4 %collective-permute-start.8 = (bf16[272,1024]{1,0:T(8,128)(2,1)S(1)}, bf16[272,1024]{1,0:T(8,128)(2,1)S(1)}, u32[]{:S(2)}, u32[]{:S(2)}) collective-permute-start(bf16[272,1024]{1,0:T(8,128)(2,1)S(1)} %collective-permute-done.3.refs_5_.refs_11_), channel_id=1, source_target_pairs={{0,1},{1,2},{2,3},{3,0},{4,5},{5,6},{6,7},{7,4},{8,9},{9,10},{10,1... | collective-permute-start | bytes 1671176 | tf_op jit(solution)/shard_map/ppermute | solution.py:601
  43.2 27.1 %collective-permute-start.13 = (bf16[272,1024]{1,0:T(8,128)(2,1)}, bf16[272,1024]{1,0:T(8,128)(2,1)S(1)}, u32[]{:S(2)}, u32[]{:S(2)}) collective-permute-start(bf16[272,1024]{1,0:T(8,128)(2,1)} %get-tuple-element.207.refs_3_), channel_id=1, source_target_pairs={{0,1},{1,2},{2,3},{3,0},{4,5},{5,6},{6,7},{7,4},{8,9},{9,10},{10,1... | collective-permute-start | bytes 1671176 | tf_op jit(solution)/shard_map/ppermute | solution.py:601
  87.4 19.1 %collective-permute-start.20 = (bf16[320,1024]{1,0:T(8,128)(2,1)}, bf16[320,1024]{1,0:T(8,128)(2,1)S(1)}, u32[]{:S(2)}, u32[]{:S(2)}) collective-permute-start(bf16[320,1024]{1,0:T(8,128)(2,1)} %get-tuple-element.208.refs_0_), channel_id=1, source_target_pairs={{0,4},{4,0},{1,5},{5,1},{2,6},{6,2},{3,7},{7,3},{8,12},{12,8},{9,1... | collective-permute-start | bytes 1966088 | tf_op jit(solution)/shard_map/ppermute | solution.py:583
  89.5 17.1 %collective-permute-start.21 = (bf16[272,1024]{1,0:T(8,128)(2,1)S(1)}, bf16[272,1024]{1,0:T(8,128)(2,1)S(1)}, u32[]{:S(2)}, u32[]{:S(2)}) collective-permute-start(bf16[272,1024]{1,0:T(8,128)(2,1)S(1)} %collective-permute-done.18.refs_5_), channel_id=1, source_target_pairs={{0,1},{1,2},{2,3},{3,0},{4,5},{5,6},{6,7},{7,4},{8,9},{9,10},{10,1... | collective-permute-start | bytes 1671176 | tf_op jit(solution)/shard_map/ppermute | solution.py:601
  134.5 26.3 %collective-permute-start.32 = (bf16[2,1,256,1024]{3,2,1,0:T(8,128)(2,1)}, bf16[2,1,256,1024]{3,2,1,0:T(8,128)(2,1)S(1)}, u32[]{:S(2)}, u32[]{:S(2)}) collective-permute-start(bf16[2,1,256,1024]{3,2,1,0:T(8,128)(2,1)} %get-tuple-element.236), channel_id=1, source_target_pairs={{0,8},{8,0},{16,24},{24,16},{1,9},{9,1},{17,25},{25,17},{2,10},{10... | collective-permute-start | bytes 3145736 | tf_op jit(solution)/shard_map/ppermute | solution.py:595
  134.6 26.2 %collective-permute-start.33 = (bf16[272,1024]{1,0:T(8,128)(2,1)S(1)}, bf16[272,1024]{1,0:T(8,128)(2,1)S(1)}, u32[]{:S(2)}, u32[]{:S(2)}) collective-permute-start(bf16[272,1024]{1,0:T(8,128)(2,1)S(1)} %collective-permute-done.21.refs_6_), channel_id=1, source_target_pairs={{0,8},{8,0},{16,24},{24,16},{1,9},{9,1},{17,25},{25,17},{2,10},{10... | collective-permute-start | bytes 1671176 | tf_op jit(solution)/shard_map/ppermute | solution.py:595
  135.1 25.7 %collective-permute-start.34 = (bf16[272,1024]{1,0:T(8,128)(2,1)S(1)}, bf16[272,1024]{1,0:T(8,128)(2,1)S(1)}, u32[]{:S(2)}, u32[]{:S(2)}) collective-permute-start(bf16[272,1024]{1,0:T(8,128)(2,1)S(1)} %collective-permute-done.29.refs_7_), channel_id=1, source_target_pairs={{0,8},{8,0},{16,24},{24,16},{1,9},{9,1},{17,25},{25,17},{2,10},{10... | collective-permute-start | bytes 1671176 | tf_op jit(solution)/shard_map/ppermute | solution.py:595
  173.9 18.1 %collective-permute-start.37 = (bf16[2,1,256,1024]{3,2,1,0:T(8,128)(2,1)}, bf16[2,1,256,1024]{3,2,1,0:T(8,128)(2,1)}, u32[]{:S(2)}, u32[]{:S(2)}) collective-permute-start(bf16[2,1,256,1024]{3,2,1,0:T(8,128)(2,1)} %get-tuple-element.248), channel_id=1, source_target_pairs={{0,8},{8,0},{16,24},{24,16},{1,9},{9,1},{17,25},{25,17},{2,10},{10... | collective-permute-start | bytes 3145736 | tf_op jit(solution)/shard_map/ppermute | solution.py:595
  174.2 17.8 %collective-permute-start.36 = (bf16[320,1024]{1,0:T(8,128)(2,1)}, bf16[320,1024]{1,0:T(8,128)(2,1)S(1)}, u32[]{:S(2)}, u32[]{:S(2)}) collective-permute-start(bf16[320,1024]{1,0:T(8,128)(2,1)} %get-tuple-element.247), channel_id=1, source_target_pairs={{0,4},{4,0},{1,5},{5,1},{2,6},{6,2},{3,7},{7,3},{8,12},{12,8},{9,1... | collective-permute-start | bytes 1966088 | tf_op jit(solution)/shard_map/ppermute | solution.py:583
  176.5 34.1 %collective-permute-start.40 = (bf16[320,1024]{1,0:T(8,128)(2,1)}, bf16[320,1024]{1,0:T(8,128)(2,1)S(1)}, u32[]{:S(2)}, u32[]{:S(2)}) collective-permute-start(bf16[320,1024]{1,0:T(8,128)(2,1)} %get-tuple-element.261), channel_id=1, source_target_pairs={{0,4},{4,0},{1,5},{5,1},{2,6},{6,2},{3,7},{7,3},{8,12},{12,8},{9,1... | collective-permute-start | bytes 1966088 | tf_op jit(solution)/shard_map/ppermute | solution.py:583
  178.2 32.4 %collective-permute-start.41 = (bf16[256,1024]{1,0:T(8,128)(2,1)S(1)}, bf16[256,1024]{1,0:T(8,128)(2,1)S(1)}, u32[]{:S(2)}, u32[]{:S(2)}) collective-permute-start(bf16[256,1024]{1,0:T(8,128)(2,1)S(1)} %fusion.11), channel_id=1, source_target_pairs={{0,16},{16,0},{8,24},{24,8},{1,17},{17,1},{9,25},{25,9},{2,18},{18... | collective-permute-start | bytes 1572872 | tf_op jit(solution)/shard_map/ppermute | solution.py:598
  192.3 18.3 %collective-permute-start.39 = (bf16[256,1024]{1,0:T(8,128)(2,1)S(1)}, bf16[256,1024]{1,0:T(8,128)(2,1)S(1)}, u32[]{:S(2)}, u32[]{:S(2)}) collective-permute-start(bf16[256,1024]{1,0:T(8,128)(2,1)S(1)} %fusion.9), channel_id=1, source_target_pairs={{0,1},{1,2},{2,3},{3,0},{4,5},{5,6},{6,7},{7,4},{8,9},{9,10},{10,1... | collective-permute-start | bytes 1572872 | tf_op jit(solution)/shard_map/ppermute | solution.py:601
  211.4 21.8 %collective-permute-start.42 = (bf16[2,2,256,1024]{3,2,1,0:T(8,128)(2,1)}, bf16[2,2,256,1024]{3,2,1,0:T(8,128)(2,1)S(1)}, u32[]{:S(2)}, u32[]{:S(2)}) collective-permute-start(bf16[2,2,256,1024]{3,2,1,0:T(8,128)(2,1)} %get-tuple-element.269), channel_id=1, source_target_pairs={{0,8},{8,0},{16,24},{24,16},{1,9},{9,1},{17,25},{25,17},{2,10},{10... | collective-permute-start | bytes 6291464 | tf_op jit(solution)/shard_map/ppermute | solution.py:595
  212.8 20.3 %collective-permute-start.44 = (bf16[256,1024]{1,0:T(8,128)(2,1)S(1)}, bf16[256,1024]{1,0:T(8,128)(2,1)S(1)}, u32[]{:S(2)}, u32[]{:S(2)}) collective-permute-start(bf16[256,1024]{1,0:T(8,128)(2,1)S(1)} %fusion.12), channel_id=1, source_target_pairs={{0,16},{16,0},{8,24},{24,8},{1,17},{17,1},{9,25},{25,9},{2,18},{18... | collective-permute-start | bytes 1572872 | tf_op jit(solution)/shard_map/ppermute | solution.py:598
  233.2 28.0 %collective-permute-start.49 = (bf16[2,2,256,1024]{3,2,1,0:T(8,128)(2,1)}, bf16[2,2,256,1024]{3,2,1,0:T(8,128)(2,1)}, u32[]{:S(2)}, u32[]{:S(2)}) collective-permute-start(bf16[2,2,256,1024]{3,2,1,0:T(8,128)(2,1)} %get-tuple-element.278), channel_id=1, source_target_pairs={{0,8},{8,0},{16,24},{24,16},{1,9},{9,1},{17,25},{25,17},{2,10},{10... | collective-permute-start | bytes 6291464 | tf_op jit(solution)/shard_map/ppermute | solution.py:595
  238.1 19.0 %collective-permute-start.51 = (bf16[2,160,1024]{2,1,0:T(8,128)(2,1)S(1)}, bf16[2,160,1024]{2,1,0:T(8,128)(2,1)S(1)}, u32[]{:S(2)}, u32[]{:S(2)}) collective-permute-start(bf16[2,160,1024]{2,1,0:T(8,128)(2,1)S(1)} %pad_maximum_fusion.1.refs_0_), channel_id=1, source_target_pairs={{0,1},{1,2},{2,3},{3,0},{4,5},{5,6},{6,7},{7,4},{8,9},{9,10},{10,1... | collective-permute-start | bytes 1966088 | tf_op jit(solution)/shard_map/ppermute | solution.py:601
  240.0 27.8 %collective-permute-start.45 = (bf16[2,2,64,1024]{3,2,1,0:T(8,128)(2,1)S(1)}, bf16[2,2,64,1024]{3,2,1,0:T(8,128)(2,1)S(1)}, u32[]{:S(2)}, u32[]{:S(2)}) collective-permute-start(bf16[2,2,64,1024]{3,2,1,0:T(8,128)(2,1)S(1)} %add_convert_fusion.4), channel_id=1, source_target_pairs={{0,4},{4,0},{1,5},{5,1},{2,6},{6,2},{3,7},{7,3},{8,12},{12,8},{9,1... | collective-permute-start | bytes 1572872 | tf_op jit(solution)/shard_map/ppermute | solution.py:583
  240.6 20.6 %collective-permute-start.48 = (bf16[160,1024]{1,0:T(8,128)(2,1)S(1)}, bf16[160,1024]{1,0:T(8,128)(2,1)S(1)}, u32[]{:S(2)}, u32[]{:S(2)}) collective-permute-start(bf16[160,1024]{1,0:T(8,128)(2,1)S(1)} %copy-done.70), channel_id=1, source_target_pairs={{0,4},{4,0},{1,5},{5,1},{2,6},{6,2},{3,7},{7,3},{8,12},{12,8},{9,1... | collective-permute-start | bytes 983048 | tf_op jit(solution)/shard_map/ppermute | solution.py:583
  243.7 25.6 %collective-permute-start.46 = (bf16[2,128,1024]{2,1,0:T(8,128)(2,1)S(1)}, bf16[2,128,1024]{2,1,0:T(8,128)(2,1)S(1)}, u32[]{:S(2)}, u32[]{:S(2)}) collective-permute-start(bf16[2,128,1024]{2,1,0:T(8,128)(2,1)S(1)} %fusion.13), channel_id=1, source_target_pairs={{0,16},{16,0},{8,24},{24,8},{1,17},{17,1},{9,25},{25,9},{2,18},{18... | collective-permute-start | bytes 1572872 | tf_op jit(solution)/shard_map/ppermute | solution.py:598
  261.2 26.6 %collective-permute-start.52 = (bf16[2,160,1024]{2,1,0:T(8,128)(2,1)S(1)}, bf16[2,160,1024]{2,1,0:T(8,128)(2,1)S(1)}, u32[]{:S(2)}, u32[]{:S(2)}) collective-permute-start(bf16[2,160,1024]{2,1,0:T(8,128)(2,1)S(1)} %collective-permute-done.51.refs_1_), channel_id=1, source_target_pairs={{0,1},{1,2},{2,3},{3,0},{4,5},{5,6},{6,7},{7,4},{8,9},{9,10},{10,1... | collective-permute-start | bytes 1966088 | tf_op jit(solution)/shard_map/ppermute | solution.py:601
  267.8 21.3 %collective-permute-start.59 = (bf16[256,1024]{1,0:T(8,128)(2,1)S(1)}, bf16[256,1024]{1,0:T(8,128)(2,1)S(1)}, u32[]{:S(2)}, u32[]{:S(2)}) collective-permute-start(bf16[256,1024]{1,0:T(8,128)(2,1)S(1)} %fusion.15), channel_id=1, source_target_pairs={{0,16},{16,0},{8,24},{24,8},{1,17},{17,1},{9,25},{25,9},{2,18},{18... | collective-permute-start | bytes 1572872 | tf_op jit(solution)/shard_map/ppermute | solution.py:598
  269.4 32.5 %collective-permute-start.56 = (bf16[2,160,1024]{2,1,0:T(8,128)(2,1)S(1)}, bf16[2,160,1024]{2,1,0:T(8,128)(2,1)S(1)}, u32[]{:S(2)}, u32[]{:S(2)}) collective-permute-start(bf16[2,160,1024]{2,1,0:T(8,128)(2,1)S(1)} %pad_maximum_fusion.2.refs_0_), channel_id=1, source_target_pairs={{0,1},{1,2},{2,3},{3,0},{4,5},{5,6},{6,7},{7,4},{8,9},{9,10},{10,1... | collective-permute-start | bytes 1966088 | tf_op jit(solution)/shard_map/ppermute | solution.py:601
  274.4 19.6 %collective-permute-start.58 = (bf16[2,128,1024]{2,1,0:T(8,128)(2,1)S(1)}, bf16[2,128,1024]{2,1,0:T(8,128)(2,1)S(1)}, u32[]{:S(2)}, u32[]{:S(2)}) collective-permute-start(bf16[2,128,1024]{2,1,0:T(8,128)(2,1)S(1)} %fusion.14), channel_id=1, source_target_pairs={{0,16},{16,0},{8,24},{24,8},{1,17},{17,1},{9,25},{25,9},{2,18},{18... | collective-permute-start | bytes 1572872 | tf_op jit(solution)/shard_map/ppermute | solution.py:598
  294.0 36.2 %collective-permute-start.65 = (bf16[2,160,1024]{2,1,0:T(8,128)(2,1)S(1)}, bf16[2,160,1024]{2,1,0:T(8,128)(2,1)S(1)}, u32[]{:S(2)}, u32[]{:S(2)}) collective-permute-start(bf16[2,160,1024]{2,1,0:T(8,128)(2,1)S(1)} %collective-permute-done.52.refs_2_), channel_id=1, source_target_pairs={{0,1},{1,2},{2,3},{3,0},{4,5},{5,6},{6,7},{7,4},{8,9},{9,10},{10,1... | collective-permute-start | bytes 1966088 | tf_op jit(solution)/shard_map/ppermute | solution.py:601
  305.0 37.3 %collective-permute-start.62 = (bf16[2,160,1024]{2,1,0:T(8,128)(2,1)S(1)}, bf16[2,160,1024]{2,1,0:T(8,128)(2,1)S(1)}, u32[]{:S(2)}, u32[]{:S(2)}) collective-permute-start(bf16[2,160,1024]{2,1,0:T(8,128)(2,1)S(1)} %collective-permute-done.56.refs_1_), channel_id=1, source_target_pairs={{0,1},{1,2},{2,3},{3,0},{4,5},{5,6},{6,7},{7,4},{8,9},{9,10},{10,1... | collective-permute-start | bytes 1966088 | tf_op jit(solution)/shard_map/ppermute | solution.py:601
  305.0 25.1 %collective-permute-start.63 = (bf16[2,64,1024]{2,1,0:T(8,128)(2,1)S(1)}, bf16[2,64,1024]{2,1,0:T(8,128)(2,1)S(1)}, u32[]{:S(2)}, u32[]{:S(2)}) collective-permute-start(bf16[2,64,1024]{2,1,0:T(8,128)(2,1)S(1)} %fusion.29), channel_id=1, source_target_pairs={{0,16},{16,0},{8,24},{24,8},{1,17},{17,1},{9,25},{25,9},{2,18},{18... | collective-permute-start | bytes 786440 | tf_op jit(solution)/shard_map/ppermute | solution.py:598
  305.6 24.5 %collective-permute-start.64 = (bf16[2,64,1024]{2,1,0:T(8,128)(2,1)S(1)}, bf16[2,64,1024]{2,1,0:T(8,128)(2,1)S(1)}, u32[]{:S(2)}, u32[]{:S(2)}) collective-permute-start(bf16[2,64,1024]{2,1,0:T(8,128)(2,1)S(1)} %dynamic-slice_convert_fusion), channel_id=1, source_target_pairs={{0,4},{4,0},{1,5},{5,1},{2,6},{6,2},{3,7},{7,3},{8,12},{12,8},{9,1... | collective-permute-start | bytes 786440 | tf_op jit(solution)/shard_map/ppermute | solution.py:583
  306.4 23.8 %collective-permute-start.66 = (f32[13,1024]{1,0:T(8,128)S(1)}, f32[13,1024]{1,0:T(8,128)S(1)}, u32[]{:S(2)}, u32[]{:S(2)}) collective-permute-start(f32[13,1024]{1,0:T(8,128)S(1)} %add.289), channel_id=1, source_target_pairs={{0,1},{1,0},{2,3},{3,2},{4,5},{5,4},{6,7},{7,6},{8,9},{9,8},{10,11... | collective-permute-start | bytes 159752 | tf_op jit(solution)/shard_map/ppermute | solution.py:847
  331.0 22.4 %collective-permute-start.69 = (bf16[256,1024]{1,0:T(8,128)(2,1)S(1)}, bf16[256,1024]{1,0:T(8,128)(2,1)S(1)}, u32[]{:S(2)}, u32[]{:S(2)}) collective-permute-start(bf16[256,1024]{1,0:T(8,128)(2,1)S(1)} %fusion.4.refs_0_), channel_id=1, source_target_pairs={{0,4},{4,0},{1,5},{5,1},{2,6},{6,2},{3,7},{7,3},{8,12},{12,8},{9,1... | collective-permute-start | bytes 1572872 | tf_op jit(solution)/shard_map/ppermute | solution.py:583
  342.4 26.8 %collective-permute-start.71 = (bf16[2,160,1024]{2,1,0:T(8,128)(2,1)S(1)}, bf16[2,160,1024]{2,1,0:T(8,128)(2,1)S(1)}, u32[]{:S(2)}, u32[]{:S(2)}) collective-permute-start(bf16[2,160,1024]{2,1,0:T(8,128)(2,1)S(1)} %collective-permute-done.62.refs_2_), channel_id=1, source_target_pairs={{0,1},{1,2},{2,3},{3,0},{4,5},{5,6},{6,7},{7,4},{8,9},{9,10},{10,1... | collective-permute-start | bytes 1966088 | tf_op jit(solution)/shard_map/ppermute | solution.py:601
  (112 other events, 1350.6 us)
